TPU v7x, 256 devices: a whole 4x4x8 slice. The times are simulated.
256 devices in a mesh: win: 32 (over z_hi, y, core), chan: 8 (over z_lo, x).
Axes of the slice: x: 4, y: 4, z: 8 (z_hi: 4, z_lo: 2; z = z_hi * 2 + z_lo), core: 2. Of those that a mesh axis runs over, the one named last changes fastest.
Arguments:
- traces: bfloat16 [64, 2048, 4096], P('win', 'chan'), may hold values from -120 to 120
- block_pairs: int32 [32, 2], replicated, may hold values from 0 to 15
- valid_count: int32 [1], replicated, may hold values from 8 to 31
Outputs:
- cross_spectra: float32 [32, 8, 2, 128, 128], P('win', 'chan')
Inputs may be any that keep to these rules, and one draw needn't show every extreme that they name: `block_pairs`: entries are channel block numbers; a pair may repeat.
All inputs are finite; a program needn't handle non-finite values.
Results may differ from a plain program's by a relative error of at most 0.0037.
Values may be sent and summed in bfloat16 or wider, within the bound.
No kernel may reach another device: no remote copies, remote signals or barrier semaphores. Data moves between devices by JAX's collectives and lax.ppermute only.
A program may use at most 64 MiB of HBM per device.

v0:
```python
import math

import jax
import jax.numpy as jnp
from jax import lax
from jax.sharding import PartitionSpec as P

BLOCK = 128
NBINS = 256
FREQ_LO = 64
GROUP = 32


EPS = 1e-06


def dft_table(length, first_bin, bins):
    times = jnp.arange(length, dtype=jnp.int32)
    freqs = first_bin + jnp.arange(bins, dtype=jnp.int32)
    phases = times[:, None] * freqs[None, :] % length
    angles = phases.astype(jnp.float32) * (2.0 * math.pi / length)
    factor = 1.0 / math.sqrt(length)
    return (jnp.concatenate([jnp.cos(angles), -jnp.sin(angles)], axis=1) * factor).astype(
        jnp.bfloat16
    )


def block_layout(band_part, block, group):
    windows, channels, _, width = band_part.shape
    shaped = band_part.reshape(windows, channels // block, block, 2, width // group, group)
    rotated = jnp.stack([shaped[:, :, :, 1], -shaped[:, :, :, 0]], axis=3)

    def arrange(values):
        moved = jnp.transpose(values, (1, 4, 2, 0, 3, 5))
        return moved.reshape(channels // block, width // group, block, windows * 2 * group)

    return (arrange(shaped), arrange(rotated))


def pair_products(upper_direct, upper_rotated, lower):
    upper = jnp.concatenate([upper_direct, upper_rotated], axis=2)
    products = jnp.einsum("pgik,pgjk->pgij", upper, lower, preferred_element_type=jnp.float32)
    return products.reshape(products.shape[0], products.shape[1], 2, lower.shape[2], lower.shape[2])


def pair_terms(direct, rotated, chosen):
    return pair_products(direct[chosen[:, 0]], rotated[chosen[:, 0]], direct[chosen[:, 1]])


def on_device(traces, block_pairs, valid_count):
    windows, channels, length = traces.shape
    spectra = jnp.dot(
        traces.reshape(windows * channels, length),
        dft_table(length, FREQ_LO, NBINS),
        preferred_element_type=jnp.float32,
    )
    energy = jnp.sum(spectra * spectra, axis=1, keepdims=True) / NBINS
    whitened = (
        (spectra * lax.rsqrt(energy + EPS))
        .astype(jnp.bfloat16)
        .reshape(windows, channels, 2, NBINS)
    )
    banded = lax.all_to_all(whitened, "chan", split_axis=3, concat_axis=1, tiled=True)
    stack_scale = 1.0 / math.sqrt(windows * lax.axis_size("win") * GROUP)
    slots = block_pairs.shape[0] // lax.axis_size("win")
    first_slot = lax.axis_index("win") * slots
    mine = lax.dynamic_slice_in_dim(block_pairs, first_slot, slots, 0)
    direct, rotated = block_layout(lax.all_gather(banded, "win", axis=0, tiled=True), BLOCK, GROUP)
    stacked = pair_terms(direct, rotated, mine)
    slot_ids = first_slot + jnp.arange(slots, dtype=jnp.int32)
    live = (slot_ids < valid_count[0]).astype(jnp.float32)
    return stacked * stack_scale * live[:, None, None, None, None]


def solution(mesh):
    in_specs = (P("win", "chan", None), P(), P())
    out_specs = P("win", "chan", None, None, None)
    return jax.shard_map(
        on_device, mesh=mesh, in_specs=in_specs, out_specs=out_specs, check_vma=False
    )
```

profile of v0, /device:TPU:43, one launch (start us, length us, event | category | flops | bytes accessed | tf_op | source)
XLA Modules:
  0.0 213.0 jit_solution(3849331905427035691)
XLA Ops:
  6.5 0.0 copy-start
  6.5 0.0 all-gather.2.cloned.1.call-start
  6.5 0.0 copy-start.2
  6.5 16.7 %fusion.10 = (f32[4096,256]{1,0:T(8,128)S(1)}, f32[4096,256]{1,0:T(8,128)S(1)}) fusion(s32[256]{0:T(256)S(1)} %iota_add_fusion), kind=kLoop, calls=%fused_computation.17 | loop fusion | flops 15728640 | bytes 8389632 | tf_op jit(solution)/shard_map/cos | solution.py:23
  23.3 0.0 copy-done.2
  23.3 2.5 %multiply_reduce_fusion = (f32[512]{0:T(512)S(1)}, f32[512,512]{1,0:T(8,128)S(1)}) fusion(bf16[512,4096]{1,0:T(8,128)(2,1)S(1)} %bitcast.49, f32[4096,256]{1,0:T(8,128)S(1)} %get-tuple-element.43, f32[4096,256]{1,0:T(8,128)S(1)} %get-tuple-element.42), kind=kOutput, calls=%fused_computation.23 | convolution fusion | flops 2154298880 | bytes 13633536 | tf_op jit(solution)/shard_map/dot_general | solution.py:52
  25.8 0.1 fusion.14
  25.9 0.1 reshape.48
  26.0 0.8 copy.21
  26.8 12.4 %all_to_all.18 = bf16[2,256,2,256]{1,2,0,3:T(2,128)(2,1)S(1)} all-to-all(bf16[2,256,2,256]{1,2,0,3:T(2,128)(2,1)S(1)} %copy.21), channel_id=1, replica_groups=mesh['win'=32,'chan'=8] {'chan'}, dimensions={3} | all-to-all | bytes 1048576 | tf_op jit(solution)/shard_map/all_to_all | solution.py:63
  39.3 0.1 copy.22
  39.3 0.9 copy.28
  40.2 0.0 all-gather.2.cloned.1.call-update
  40.2 0.0 copy-done
  40.2 0.1 constant_dynamic-slice_fusion.2
  40.3 0.5 fusion.19
  45.1 116.9 %all-gather.2.cloned.1.call-done = bf16[64,2048,2,32]{1,3,2,0:T(8,128)(2,1)} async-done(((bf16[2,2048,2,32]{1,3,2,0:T(8,128)(2,1)}), bf16[64,2048,2,32]{1,3,2,0:T(8,128)(2,1)}) %all-gather.2.cloned.1.call-update) | async-done | bytes 16777232 | tf_op jit(solution)/shard_map/all_gather | solution.py:68
  162.0 9.6 %copy.29 = bf16[512,8,16,128]{3,2,1,0:T(8,128)(2,1)S(1)} copy(bf16[512,8,16,128]{3,1,2,0:T(8,128)(2,1)} %bitcast.45) | data formatting | bytes 33554432
  171.7 12.0 %copy.24 = bf16[16,1,128,64,2,32]{2,5,4,3,0,1:T(8,128)(2,1)} copy(bf16[16,1,128,64,2,32]{2,0,5,4,3,1:T(8,128)(2,1)S(1)} %bitcast.40) | data formatting | bytes 33554432 | tf_op jit(solution)/shard_map/transpose | solution.py:34
  183.6 1.7 fusion.18
  185.3 1.7 maximum_bitcast_fusion
  187.0 10.7 %copy.25 = bf16[16,1,128,64,2,32]{2,5,4,3,0,1:T(8,128)(2,1)S(1)} copy(bf16[16,1,128,64,2,32]{2,0,5,4,3,1:T(8,128)(2,1)S(1)} %maximum_bitcast_fusion) | data formatting | bytes 33554432 | tf_op jit(solution)/shard_map/transpose | solution.py:34
  197.7 1.4 constant_dynamic-slice_fusion
  199.0 0.0 copy-start.1
  199.0 1.6 pad_maximum_fusion
  200.6 2.9 %copy.26 = bf16[1,1,256,4096]{3,2,1,0:T(8,128)(2,1)S(1)} copy(bf16[1,1,256,4096]{2,3,0,1:T(8,128)(2,1)} %pad_maximum_fusion) | data formatting | bytes 4194304 | tf_op jit(solution)/shard_map/concatenate | solution.py:41
  203.5 2.6 %fusion.11 = f32[1,1,2,128,128]{4,3,2,1,0:T(8,128)} fusion(bf16[2,128,4096]{2,1,0:T(8,128)(2,1)S(1)} %bitcast.46, bf16[16,1,128,4096]{2,3,0,1:T(8,128)(2,1)} %bitcast.43, s32[]{:T(128)} %bitcast.12, f32[]{:T(128)} %bitcast.16), kind=kOutput, calls=%fused_computation.19 | convolution fusion | flops 268468224 | bytes 3277824 | tf_op jit(solution)/shard_map/pgik,pgjk->pgij/dot_general | solution.py:42
  206.2 0.0 copy-done.1
  (2 shorter events, 0.0 us)
Async XLA Ops:
  6.5 33.7 %copy-start = (s32[32,2]{0,1:T(2,128)S(1)}, s32[32,2]{0,1:T(2,128)}, u32[]{:S(2)}) copy-start(s32[32,2]{0,1:T(2,128)} %param.4) | copy-start | bytes 772
  6.5 155.5 %all-gather.2.cloned.1.call-start = ((), (), s32[]{:S(2)}) async-start(), calls=%async_computation.1 | async-start | bytes 17301504 | tf_op jit(solution)/shard_map/all_gather | solution.py:68
  6.5 16.7 %copy-start.2 = (bf16[2,256,4096]{2,1,0:T(8,128)(2,1)S(1)}, bf16[2,256,4096]{2,1,0:T(8,128)(2,1)}, u32[]{:S(2)}) copy-start(bf16[2,256,4096]{2,1,0:T(8,128)(2,1)} %param.3) | copy-start | bytes 12582916
  199.0 7.1 %copy-start.1 = (s32[32,2]{0,1:T(2,128)S(1)}, s32[32,2]{0,1:T(2,128)}, u32[]{:S(2)}) copy-start(s32[32,2]{0,1:T(2,128)} %param.4) | copy-start | bytes 772
Sparse Core Ops, SparseCore 0:
  40.4 121.6 all-gather.1
where the time goes:
time: 213 us
  waiting for transfers between devices  117 us (55%)
  local copies, waits for them, and re-layouts  39 us (18%)
  other arithmetic  21.8 us (10%)
  between operations  17.8 us (8%)
  blocking collectives  12.4 us (6%)
  matrix products  5.11 us (2%)
    all_gather x1, waiting for transfers between devices, on_device(): lax.all_gather(banded, 'win', axis=0, tiled=True)  117 us
    transpose x2, local copies, waits for them, and re-layouts, arrange(): moved = jnp.transpose(values, (1, 4, 2, 0, 3, 5))  22.6 us
    cos x1, other arithmetic, dft_table(): jnp.cos(angles)  16.7 us
    all_to_all x1, blocking collectives, on_device(): lax.all_to_all(whitened, 'chan', split_axis=3, concat_axis=1, tiled=True)  12.4 us
    unnamed x7, local copies, waits for them, and re-layouts  9.66 us
  transfers between devices with their start and end apart: 1, of which 1 were waited for; matrix products, arithmetic and copies ran while one was open for 0% of the time, Pallas kernels for 0%

commit v1 on v0

v1 whole, which is shorter than its diff:
```python
import math

import jax
import jax.numpy as jnp
import numpy as np
from jax import lax
from jax.experimental import pallas as pl
from jax.experimental.pallas import tpu as pltpu
from jax.sharding import Mesh, PartitionSpec as P

BLOCK = 128
NBINS = 256
FREQ_LO = 64
GROUP = 32
EPS = 1e-06
QUARTERS = 4


def packed_table(length):
    times = np.arange(length // QUARTERS, dtype=np.int64)
    freqs = FREQ_LO + np.arange(NBINS, dtype=np.int64)
    angles = (times[:, None] * freqs[None, :] % length) * (2.0 * math.pi / length)
    factor = 1.0 / math.sqrt(length)
    re = (np.cos(angles) * factor).reshape(-1, NBINS // 64, 64)
    im = (-np.sin(angles) * factor).reshape(-1, NBINS // 64, 64)
    return np.concatenate([re, im], axis=2).reshape(-1, 2 * NBINS).astype(jnp.bfloat16)


def spectra_kernel(traces, table, out, table_buf, buf, sems):
    steps, windows, span, length = buf.shape
    quarter = length // QUARTERS
    load_table = pltpu.make_async_copy(table, table_buf, sems.at[steps])
    load_table.start()
    loads = []
    for step in range(steps):
        load = pltpu.make_async_copy(
            traces.at[:, pl.ds(step * span, span), :], buf.at[step], sems.at[step]
        )
        load.start()
        loads.append(load)
    lanes = lax.broadcasted_iota(jnp.int32, (span, 128), 1)
    bin4 = (FREQ_LO + lanes) % 4
    sign2 = jnp.where(bin4 % 2 == 0, 1.0, -1.0)
    direct = jnp.where(bin4 == 0, 1.0, jnp.where(bin4 == 2, -1.0, 0.0))
    up = jnp.where(bin4 == 1, 1.0, jnp.where(bin4 == 3, -1.0, 0.0))
    cross = jnp.where(lanes < 64, up, -up)
    lane32 = lanes // 32 % 2
    tiles = 2 * NBINS // 128
    load_table.wait()
    for step in range(steps):
        loads[step].wait()
        whole = buf[step].reshape(windows * span, length)
        stacked = jnp.concatenate(
            [whole[:, q * quarter : (q + 1) * quarter] for q in range(QUARTERS)], axis=0
        )
        dots = jnp.dot(stacked, table_buf[...], preferred_element_type=jnp.float32)
        spans = []
        for w in range(windows):
            parts = []
            energy = jnp.zeros((span, 1), jnp.float32)
            for t in range(tiles):
                cols = slice(t * 128, (t + 1) * 128)
                d0, d1, d2, d3 = (
                    dots[(q * windows + w) * span : (q * windows + w + 1) * span, cols]
                    for q in range(QUARTERS)
                )
                main = d0 + sign2 * d2
                turn = d1 + sign2 * d3
                full = main + direct * turn + cross * pltpu.roll(turn, 64, 1)
                energy = energy + jnp.sum(full * full, axis=1, keepdims=True)
                parts.append(full)
            scale = lax.rsqrt(energy / NBINS + EPS)
            spans.append([part * scale for part in parts])
        rows = pl.ds(step * span, span)
        for t in range(tiles):
            first, second = spans[0][t], spans[1][t]
            out[2 * t, rows] = jnp.where(lane32 == 0, first, pltpu.roll(second, 32, 1)).astype(out.dtype)
            out[2 * t + 1, rows] = jnp.where(lane32 == 1, first, pltpu.roll(second, 96, 1)).astype(
                out.dtype
            )


def whitened_groups(traces, steps=4):
    windows, channels, length = traces.shape
    table = jnp.asarray(packed_table(length))
    groups = NBINS // GROUP
    return pl.pallas_call(
        spectra_kernel,
        out_shape=jax.ShapeDtypeStruct((groups, channels, windows * 2 * GROUP), jnp.bfloat16),
        in_specs=[pl.BlockSpec(memory_space=pltpu.HBM), pl.BlockSpec(memory_space=pltpu.HBM)],
        out_specs=pl.BlockSpec(memory_space=pltpu.VMEM),
        scratch_shapes=[
            pltpu.VMEM(table.shape, table.dtype),
            pltpu.VMEM((steps, windows, channels // steps, length), traces.dtype),
            pltpu.SemaphoreType.DMA((steps + 1,)),
        ],
        compiler_params=pltpu.CompilerParams(vmem_limit_bytes=48 << 20),
        name="spectra",
    )(pltpu.with_memory_space_constraint(traces, pltpu.HBM), pltpu.with_memory_space_constraint(table, pltpu.HBM))


def products_kernel(pairs, own, sib, out):
    lanes = lax.broadcasted_iota(jnp.int32, (BLOCK, 128), 1)
    is_re = lanes < 64
    dims = (((1,), (1,)), ((), ()))
    for q in range(out.shape[0]):
        r = pairs[q, 0]
        s = pairs[q, 1]
        total_re = jnp.zeros((BLOCK, BLOCK), jnp.float32)
        total_im = jnp.zeros((BLOCK, BLOCK), jnp.float32)
        upper = []
        rotated = []
        lower = []
        for ref in (own, sib):
            a = ref[r]
            turned = pltpu.roll(a.astype(jnp.float32), 64, 1)
            upper.append(a)
            rotated.append(jnp.where(is_re, turned, -turned).astype(a.dtype))
            lower.append(ref[s])
        a = jnp.concatenate([jnp.concatenate(upper, 1), jnp.concatenate(rotated, 1)], 0)
        b = jnp.concatenate(lower, 1)
        both = lax.dot_general(a, b, dims, preferred_element_type=jnp.float32)
        out[q, 0] = both[:BLOCK].astype(out.dtype)
        out[q, 1] = both[BLOCK:].astype(out.dtype)


def partial_sums(pairs, own, sib):
    slots = pairs.shape[0]
    return pl.pallas_call(
        products_kernel,
        out_shape=jax.ShapeDtypeStruct((slots, 2, BLOCK, BLOCK), jnp.bfloat16),
        in_specs=[
            pl.BlockSpec(memory_space=pltpu.SMEM),
            pl.BlockSpec(memory_space=pltpu.VMEM),
            pl.BlockSpec(memory_space=pltpu.VMEM),
        ],
        out_specs=pl.BlockSpec(memory_space=pltpu.VMEM),
        compiler_params=pltpu.CompilerParams(vmem_limit_bytes=32 << 20),
        name="products",
    )(pairs, own, sib)


def on_device(traces, block_pairs, valid_count):
    windows, channels, _ = traces.shape
    chips = lax.axis_size(("zh", "y"))
    cores = lax.axis_size("core")
    grouped = whitened_groups(traces)
    banded = lax.all_to_all(grouped, ("zl", "x"), split_axis=0, concat_axis=0, tiled=True)
    own = banded.reshape(-1, BLOCK, banded.shape[2])
    sib = lax.ppermute(own, "core", [(0, 1), (1, 0)])
    core = lax.axis_index("core")
    pairs = lax.dynamic_index_in_dim(block_pairs.reshape(chips, cores, 2), core, 1, keepdims=False)
    partial = partial_sums(pairs, own, sib)
    received = lax.all_to_all(partial, ("zh", "y"), split_axis=0, concat_axis=0, tiled=True)
    total = jnp.sum(received.astype(jnp.float32), axis=0)
    stack_scale = 1.0 / math.sqrt(windows * chips * cores * GROUP)
    slot = lax.axis_index(("zh", "y")) * cores + core
    live = (slot < valid_count[0]).astype(jnp.float32)
    return (total * (stack_scale * live))[None, None]


def solution(mesh):
    fine = Mesh(mesh.devices.reshape(4, 4, 2, 2, 4), ("zh", "y", "core", "zl", "x"))
    win = ("zh", "y", "core")
    chan = ("zl", "x")
    return jax.shard_map(
        on_device,
        mesh=fine,
        in_specs=(P(win, chan, None), P(), P()),
        out_specs=P(win, chan, None, None, None),
        check_vma=False,
    )
```

time: 213 us -> 65.7 us (0.31)
  the two profiles are of different devices: /device:TPU:43 before, /device:TPU:8 now
where the time goes in v1:
time: 65.7 us; the launch traced here: 65.5 us
  waiting for transfers between devices  29.5 us (45%)
  blocking collectives  15.5 us (24%)
  starting transfers between devices  10.7 us (16%)
  Pallas kernels  7.98 us (12%)
  other arithmetic  0.82 us (1%)
  between operations  0.67 us (1%)
    all_to_all x1, waiting for transfers between devices, on_device(): lax.all_to_all(partial, ('zh', 'y'), split_axis=0, concat_axis=0, tiled=T...  27.9 us
    all_to_all x1, blocking collectives, on_device(): lax.all_to_all(grouped, ('zl', 'x'), split_axis=0, concat_axis=0, tiled=T...  15.5 us
    all_to_all x1, starting transfers between devices, on_device(): lax.all_to_all(partial, ('zh', 'y'), split_axis=0, concat_axis=0, tiled=T...  10.7 us
    pallas_call x1, Pallas kernels, whitened_groups(): pl.pallas_call(spectra_kernel, out_shape=jax.ShapeDtypeStruct((groups, ch...  5.6 us
    pallas_call x1, Pallas kernels, partial_sums(): pl.pallas_call(products_kernel, out_shape=jax.ShapeDtypeStruct((slots, 2,...  2.38 us
    ppermute x1, waiting for transfers between devices, on_device(): sib = lax.ppermute(own, 'core', [(0, 1), (1, 0)])  1.55 us
  transfers between devices with their start and end apart: 2, of which 2 were waited for; matrix products, arithmetic and copies ran while one was open for 1% of the time, Pallas kernels for 0%

profile of v1, /device:TPU:8, one launch (start us, length us, event | category | flops | bytes accessed | tf_op | source)
XLA Modules:
  0.0 65.5 jit_solution(6639324493380081904)
XLA Ops:
  0.0 0.0 copy-start
  0.0 5.6 %spectra.1 = bf16[8,256,128]{2,1,0:T(8,128)(2,1)S(1)} custom-call(bf16[2,256,4096]{2,1,0:T(8,128)(2,1)} %traces.1, bf16[1024,512]{1,0:T(8,128)(2,1)} %constant.31.clone.table), custom_call_target="tpu_custom_call" | custom-call | tf_op jit(solution)/shard_map/spectra/pallas_call | solution.py:87
  5.6 15.5 %all_to_all.10 = bf16[8,256,128]{2,1,0:T(8,128)(2,1)S(1)} all-to-all(bf16[8,256,128]{2,1,0:T(8,128)(2,1)S(1)} %spectra.1), channel_id=1, replica_groups=mesh['zh'=4,'y'=4,'core'=2,'zl'=2,'x'=4] {'zl','x'}, dimensions={0} | all-to-all | bytes 1048576 | tf_op jit(solution)/shard_map/all_to_all | solution.py:148
  21.1 0.0 collective-permute-start
  21.1 0.0 copy-done
  21.1 0.1 reshape.15
  21.2 0.1 constant_dynamic-slice_fusion
  21.3 0.2 copy.7
  21.5 1.5 %collective-permute-done.sib = bf16[16,128,128]{2,1,0:T(8,128)(2,1)S(1)} collective-permute-done((bf16[16,128,128]{2,1,0:T(8,128)(2,1)S(1)}, bf16[16,128,128]{2,1,0:T(8,128)(2,1)S(1)}, u32[]{:S(2)}, u32[]{:S(2)}) %collective-permute-start) | collective-permute-done | bytes 524320 | tf_op jit(solution)/shard_map/ppermute | solution.py:150
  23.0 2.4 %products.1 = bf16[16,2,128,128]{3,2,1,0:T(8,128)(2,1)} custom-call(s32[16,2]{1,0:T(8,128)S(1)} %bitcast.10, bf16[16,128,128]{2,1,0:T(8,128)(2,1)S(1)} %bitcast.9, bf16[16,128,128]{2,1,0:T(8,128)(2,1)S(1)} %collective-permute-done.sib), custom_call_target="tpu_custom_call" | custom-call | tf_op jit(solution)/shard_map/products/pallas_call | solution.py:129
  25.4 10.7 %all-to-all-start.1 = ((bf16[16,2,128,128]{3,2,1,0:T(8,128)(2,1)}), bf16[16,2,128,128]{3,2,1,0:T(8,128)(2,1)S(1)}, u32[]{:S(2)}, u32[]{:S(2)}) async-start(bf16[16,2,128,128]{3,2,1,0:T(8,128)(2,1)} %products.1), calls=%async_computation.1 | async-start | bytes 2097152 | tf_op jit(solution)/shard_map/all_to_all | solution.py:154
  36.7 27.9 %all-to-all-done.1 = bf16[16,2,128,128]{3,2,1,0:T(8,128)(2,1)S(1)} async-done(((bf16[16,2,128,128]{3,2,1,0:T(8,128)(2,1)}), bf16[16,2,128,128]{3,2,1,0:T(8,128)(2,1)S(1)}, u32[]{:S(2)}, u32[]{:S(2)}) %all-to-all-start.1) | async-done | bytes 1048608 | tf_op jit(solution)/shard_map/all_to_all | solution.py:154
  64.7 0.1 convert_reduce_fusion
  64.8 0.7 %multiply_bitcast_fusion = f32[1,1,2,128,128]{4,3,2,1,0:T(8,128)} fusion(f32[2,128,128]{2,1,0:T(8,128)S(1)} %convert_reduce_fusion, f32[]{:T(128)S(6)} %mul_shard_map.3), kind=kLoop, calls=%fused_computation.1 | loop fusion | flops 32768 | bytes 262148 | tf_op jit(solution)/shard_map/mul | solution.py:159
Async XLA Ops:
  0.0 21.1 %copy-start = (s32[32,2]{0,1:T(2,128)S(1)}, s32[32,2]{0,1:T(2,128)}, u32[]{:S(2)}) copy-start(s32[32,2]{0,1:T(2,128)} %param.5) | copy-start | bytes 772
  21.1 1.9 %collective-permute-start = (bf16[16,128,128]{2,1,0:T(8,128)(2,1)S(1)}, bf16[16,128,128]{2,1,0:T(8,128)(2,1)S(1)}, u32[]{:S(2)}, u32[]{:S(2)}) collective-permute-start(bf16[16,128,128]{2,1,0:T(8,128)(2,1)S(1)} %bitcast.8), channel_id=1, source_target_pairs={{0,8},{8,0},{1,9},{9,1},{2,10},{10,2},{3,11},{11,3},{4,12},{12,4},... | collective-permute-start | bytes 1572872 | tf_op jit(solution)/shard_map/ppermute | solution.py:150
  25.4 39.2 %all-to-all-start.1 = ((bf16[16,2,128,128]{3,2,1,0:T(8,128)(2,1)}), bf16[16,2,128,128]{3,2,1,0:T(8,128)(2,1)S(1)}, u32[]{:S(2)}, u32[]{:S(2)}) async-start(bf16[16,2,128,128]{3,2,1,0:T(8,128)(2,1)} %products.1), calls=%async_computation.1 | async-start | bytes 2097152 | tf_op jit(solution)/shard_map/all_to_all | solution.py:154

commit v2 on v1

--- a/solution.py
+++ b/solution.py
@@ -80,6 +80,10 @@
             )
 
 
+def in_hbm(values):
+    return pltpu.with_memory_space_constraint(values, pltpu.HBM)
+
+
 def whitened_groups(traces, steps=4):
     windows, channels, length = traces.shape
     table = jnp.asarray(packed_table(length))
@@ -94,67 +98,108 @@
             pltpu.VMEM((steps, windows, channels // steps, length), traces.dtype),
             pltpu.SemaphoreType.DMA((steps + 1,)),
         ],
-        compiler_params=pltpu.CompilerParams(vmem_limit_bytes=48 << 20),
+        compiler_params=pltpu.CompilerParams(vmem_limit_bytes=16 << 20),
         name="spectra",
-    )(pltpu.with_memory_space_constraint(traces, pltpu.HBM), pltpu.with_memory_space_constraint(table, pltpu.HBM))
-
-
-def products_kernel(pairs, own, sib, out):
+    )(in_hbm(traces), in_hbm(table))
+
+
+def products_kernel(pairs, own, sib, *outs):
     lanes = lax.broadcasted_iota(jnp.int32, (BLOCK, 128), 1)
     is_re = lanes < 64
     dims = (((1,), (1,)), ((), ()))
-    for q in range(out.shape[0]):
-        r = pairs[q, 0]
-        s = pairs[q, 1]
-        total_re = jnp.zeros((BLOCK, BLOCK), jnp.float32)
-        total_im = jnp.zeros((BLOCK, BLOCK), jnp.float32)
-        upper = []
-        rotated = []
-        lower = []
-        for ref in (own, sib):
-            a = ref[r]
-            turned = pltpu.roll(a.astype(jnp.float32), 64, 1)
-            upper.append(a)
-            rotated.append(jnp.where(is_re, turned, -turned).astype(a.dtype))
-            lower.append(ref[s])
-        a = jnp.concatenate([jnp.concatenate(upper, 1), jnp.concatenate(rotated, 1)], 0)
-        b = jnp.concatenate(lower, 1)
-        both = lax.dot_general(a, b, dims, preferred_element_type=jnp.float32)
-        out[q, 0] = both[:BLOCK].astype(out.dtype)
-        out[q, 1] = both[BLOCK:].astype(out.dtype)
+    here_z = lax.axis_index("zh")
+    here_y = lax.axis_index("y")
+    core = lax.axis_index("core")
+    cores = lax.axis_size("core")
+    for d, out in enumerate(outs):
+        size_z = out.shape[0]
+        for e in range(size_z):
+            chip = (here_z + e) % size_z * len(outs) + (here_y + d) % len(outs)
+            slot = chip * cores + core
+            r = pairs[slot, 0]
+            s = pairs[slot, 1]
+            upper = []
+            rotated = []
+            lower = []
+            for ref in (own, sib):
+                block = ref[r]
+                turned = pltpu.roll(block.astype(jnp.float32), 64, 1)
+                upper.append(block)
+                rotated.append(jnp.where(is_re, turned, -turned).astype(block.dtype))
+                lower.append(ref[s])
+            a = jnp.concatenate([jnp.concatenate(upper, 1), jnp.concatenate(rotated, 1)], 0)
+            b = jnp.concatenate(lower, 1)
+            both = lax.dot_general(a, b, dims, preferred_element_type=jnp.float32)
+            out[e, 0] = both[:BLOCK].astype(out.dtype)
+            out[e, 1] = both[BLOCK:].astype(out.dtype)
+
+
+def vmem():
+    return pl.BlockSpec(memory_space=pltpu.VMEM)
 
 
 def partial_sums(pairs, own, sib):
-    slots = pairs.shape[0]
+    size_z = lax.axis_size("zh")
+    size_y = lax.axis_size("y")
+    shape = (size_z, 2, BLOCK, BLOCK)
     return pl.pallas_call(
         products_kernel,
-        out_shape=jax.ShapeDtypeStruct((slots, 2, BLOCK, BLOCK), jnp.bfloat16),
-        in_specs=[
-            pl.BlockSpec(memory_space=pltpu.SMEM),
-            pl.BlockSpec(memory_space=pltpu.VMEM),
-            pl.BlockSpec(memory_space=pltpu.VMEM),
+        out_shape=[
+            jax.ShapeDtypeStruct(shape, jnp.bfloat16 if d else jnp.float32) for d in range(size_y)
         ],
-        out_specs=pl.BlockSpec(memory_space=pltpu.VMEM),
-        compiler_params=pltpu.CompilerParams(vmem_limit_bytes=32 << 20),
+        in_specs=[pl.BlockSpec(memory_space=pltpu.SMEM), vmem(), vmem()],
+        out_specs=[vmem()] * size_y,
+        compiler_params=pltpu.CompilerParams(vmem_limit_bytes=8 << 20),
         name="products",
     )(pairs, own, sib)
 
 
+def stage_kernel(*refs):
+    parts = len(refs) // 2
+    for e in range(parts):
+        total = refs[0][e]
+        for ref in refs[1:parts]:
+            total = total + ref[e].astype(jnp.float32)
+        refs[parts + e][...] = total.astype(refs[parts + e].dtype)
+
+
+def stage_sums(arrays):
+    size_z = arrays[0].shape[0]
+    shape = arrays[0].shape[1:]
+    return pl.pallas_call(
+        stage_kernel,
+        out_shape=[
+            jax.ShapeDtypeStruct(shape, jnp.bfloat16 if e else jnp.float32) for e in range(size_z)
+        ],
+        in_specs=[vmem()] * len(arrays),
+        out_specs=[vmem()] * size_z,
+        compiler_params=pltpu.CompilerParams(vmem_limit_bytes=8 << 20),
+        name="stage",
+    )(*arrays)
+
+
+def shifted(values, axis, offset):
+    size = lax.axis_size(axis)
+    return lax.ppermute(values, axis, [(i, (i + offset) % size) for i in range(size)])
+
+
+def spread(arrays, axis):
+    return [arrays[0]] + [shifted(values, axis, d) for d, values in enumerate(arrays) if d]
+
+
 def on_device(traces, block_pairs, valid_count):
-    windows, channels, _ = traces.shape
-    chips = lax.axis_size(("zh", "y"))
-    cores = lax.axis_size("core")
+    windows = traces.shape[0] * lax.axis_size(("zh", "y", "core"))
     grouped = whitened_groups(traces)
     banded = lax.all_to_all(grouped, ("zl", "x"), split_axis=0, concat_axis=0, tiled=True)
     own = banded.reshape(-1, BLOCK, banded.shape[2])
-    sib = lax.ppermute(own, "core", [(0, 1), (1, 0)])
-    core = lax.axis_index("core")
-    pairs = lax.dynamic_index_in_dim(block_pairs.reshape(chips, cores, 2), core, 1, keepdims=False)
-    partial = partial_sums(pairs, own, sib)
-    received = lax.all_to_all(partial, ("zh", "y"), split_axis=0, concat_axis=0, tiled=True)
-    total = jnp.sum(received.astype(jnp.float32), axis=0)
-    stack_scale = 1.0 / math.sqrt(windows * chips * cores * GROUP)
-    slot = lax.axis_index(("zh", "y")) * cores + core
+    sib = shifted(own, "core", 1)
+    along_y = spread(partial_sums(block_pairs, own, sib), "y")
+    along_z = spread(stage_sums(along_y), "zh")
+    total = along_z[0]
+    for values in along_z[1:]:
+        total = total + values.astype(jnp.float32)
+    stack_scale = 1.0 / math.sqrt(windows * GROUP)
+    slot = lax.axis_index(("zh", "y", "core"))
     live = (slot < valid_count[0]).astype(jnp.float32)
     return (total * (stack_scale * live))[None, None]
 

time: 65.7 us -> 56.3 us (0.86)
  waiting for transfers between devices: 29.5 us -> 15.7 us
  starting transfers between devices: 10.7 us -> 15.5 us
  Pallas kernels: 7.98 us -> 7.27 us
    all_to_all x1 -> x0, waiting for transfers between devices: 27.9 us -> none  [on_device(): lax.all_to_all(partial, ('zh', 'y'), split_axis=0, concat_axis=0, tiled=T...]
    ppermute x1 -> x7, starting transfers between devices: 0.01 us -> 15.5 us  [shifted(): lax.ppermute(values, axis, [(i, (i + offset) % size) for i in range(size)])]
    ppermute x1 -> x7, waiting for transfers between devices: 1.55 us -> 15.7 us  [shifted(): lax.ppermute(values, axis, [(i, (i + offset) % size) for i in range(size)])]
    all_to_all x1 -> x0, starting transfers between devices: 10.7 us -> none  [on_device(): lax.all_to_all(partial, ('zh', 'y'), split_axis=0, concat_axis=0, tiled=T...]
    pallas_call x1 -> x2, Pallas kernels: 2.38 us -> 1.68 us  [the longest x1 1.56 us: partial_sums(): pl.pallas_call(products_kernel, out_shape=[jax.ShapeDtypeStruct(shape, jn...]
    broadcast_in_dim x0 -> x1, other arithmetic: none -> 0.69 us  [on_device(): return (total * (stack_scale * live))[None, None]]
    mul x1 -> x0, other arithmetic: 0.67 us -> none  [on_device(): return (total * (stack_scale * live))[None, None]]
  transfers between devices with their start and end apart: 2 -> 7, of which waited for: 2 -> 6; matrix products, arithmetic and copies ran while one was open for 1% -> 0% of each run, Pallas kernels for 0% -> 0%
where the time goes in v2:
time: 56.3 us; the launch traced here: 55.5 us
  waiting for transfers between devices  15.7 us (28%)
  blocking collectives  15.5 us (28%)
  starting transfers between devices  15.5 us (28%)
  Pallas kernels  7.27 us (13%)
  other arithmetic  0.69 us (1%)
  between operations  0.69 us (1%)
    ppermute x7, waiting for transfers between devices, shifted(): lax.ppermute(values, axis, [(i, (i + offset) % size) for i in range(size)])  15.7 us
    all_to_all x1, blocking collectives, on_device(): lax.all_to_all(grouped, ('zl', 'x'), split_axis=0, concat_axis=0, tiled=T...  15.5 us
    ppermute x7, starting transfers between devices, shifted(): lax.ppermute(values, axis, [(i, (i + offset) % size) for i in range(size)])  15.5 us
    pallas_call x1, Pallas kernels, whitened_groups(): pl.pallas_call(spectra_kernel, out_shape=jax.ShapeDtypeStruct((groups, ch...  5.6 us
    pallas_call x1, Pallas kernels, partial_sums(): pl.pallas_call(products_kernel, out_shape=[jax.ShapeDtypeStruct(shape, jn...  1.56 us
  transfers between devices with their start and end apart: 7, of which 6 were waited for; matrix products, arithmetic and copies ran while one was open for 0% of the time, Pallas kernels for 0%

profile of v2, /device:TPU:8, one launch (start us, length us, event | category | flops | bytes accessed | tf_op | source)
XLA Modules:
  0.0 55.5 jit_solution(14607502185486434755)
XLA Ops:
  0.0 0.0 copy-start
  0.0 5.6 %spectra.1 = bf16[8,256,128]{2,1,0:T(8,128)(2,1)S(1)} custom-call(bf16[2,256,4096]{2,1,0:T(8,128)(2,1)} %traces.1, bf16[1024,512]{1,0:T(8,128)(2,1)} %constant.25.clone.table), custom_call_target="tpu_custom_call" | custom-call | tf_op jit(solution)/shard_map/spectra/pallas_call | solution.py:91
  5.6 15.5 %all_to_all.5 = bf16[8,256,128]{2,1,0:T(8,128)(2,1)S(1)} all-to-all(bf16[8,256,128]{2,1,0:T(8,128)(2,1)S(1)} %spectra.1), channel_id=1, replica_groups=mesh['zh'=4,'y'=4,'core'=2,'zl'=2,'x'=4] {'zl','x'}, dimensions={0} | all-to-all | bytes 1048576 | tf_op jit(solution)/shard_map/all_to_all | solution.py:193
  21.1 0.0 collective-permute-start
  21.1 0.0 copy-done
  21.1 0.1 copy.5.pairs
  21.2 1.8 %collective-permute-done.sib = bf16[16,128,128]{2,1,0:T(8,128)(2,1)S(1)} collective-permute-done((bf16[16,128,128]{2,1,0:T(8,128)(2,1)S(1)}, bf16[16,128,128]{2,1,0:T(8,128)(2,1)S(1)}, u32[]{:S(2)}, u32[]{:S(2)}) %collective-permute-start) | collective-permute-done | bytes 524320 | tf_op jit(solution)/shard_map/ppermute | solution.py:183
  23.0 1.6 %products.1 = (f32[4,2,128,128]{3,2,1,0:T(8,128)S(1)}, bf16[4,2,128,128]{3,2,1,0:T(8,128)(2,1)S(1)}, bf16[4,2,128,128]{3,2,1,0:T(8,128)(2,1)S(1)}, bf16[4,2,128,128]{3,2,1,0:T(8,128)(2,1)S(1)}) custom-call(s32[32,2]{1,0:T(8,128)S(1)} %copy.5.pairs, bf16[16,128,128]{2,1,0:T(8,128)(2,1)S(1)} %bitcast.6, bf16[16,128,128]{2,1,0:T(8,128)(2,1)S(1)} %collective-permute-done.sib), custom_call_target="tpu_custom_call" | custom-call | tf_op jit(solution)/shard_map/products/pallas_call | solution.py:145
  24.6 1.7 %collective-permute-start.1 = (bf16[4,2,128,128]{3,2,1,0:T(8,128)(2,1)S(1)}, bf16[4,2,128,128]{3,2,1,0:T(8,128)(2,1)S(1)}, u32[]{:S(2)}, u32[]{:S(2)}) collective-permute-start(bf16[4,2,128,128]{3,2,1,0:T(8,128)(2,1)S(1)} %get-tuple-element.14), channel_id=1, source_target_pairs={{0,16},{16,32},{32,48},{48,0},{1,17},{17,33},{33,49},{49,1},{2,18}... | collective-permute-start | bytes 786440 | tf_op jit(solution)/shard_map/ppermute | solution.py:183
  26.3 0.9 %collective-permute-start.2 = (bf16[4,2,128,128]{3,2,1,0:T(8,128)(2,1)S(1)}, bf16[4,2,128,128]{3,2,1,0:T(8,128)(2,1)S(1)}, u32[]{:S(2)}, u32[]{:S(2)}) collective-permute-start(bf16[4,2,128,128]{3,2,1,0:T(8,128)(2,1)S(1)} %get-tuple-element.15), channel_id=1, source_target_pairs={{0,32},{16,48},{32,0},{48,16},{1,33},{17,49},{33,1},{49,17},{2,34}... | collective-permute-start | bytes 786440 | tf_op jit(solution)/shard_map/ppermute | solution.py:183
  27.2 2.4 %collective-permute-start.3 = (bf16[4,2,128,128]{3,2,1,0:T(8,128)(2,1)S(1)}, bf16[4,2,128,128]{3,2,1,0:T(8,128)(2,1)S(1)}, u32[]{:S(2)}, u32[]{:S(2)}) collective-permute-start(bf16[4,2,128,128]{3,2,1,0:T(8,128)(2,1)S(1)} %get-tuple-element.16), channel_id=1, source_target_pairs={{0,48},{16,0},{32,16},{48,32},{1,49},{17,1},{33,17},{49,33},{2,50}... | collective-permute-start | bytes 786440 | tf_op jit(solution)/shard_map/ppermute | solution.py:183
  29.6 4.2 %collective-permute-done.1.refs_1_ = bf16[4,2,128,128]{3,2,1,0:T(8,128)(2,1)S(1)} collective-permute-done((bf16[4,2,128,128]{3,2,1,0:T(8,128)(2,1)S(1)}, bf16[4,2,128,128]{3,2,1,0:T(8,128)(2,1)S(1)}, u32[]{:S(2)}, u32[]{:S(2)}) %collective-permute-start.1) | collective-permute-done | bytes 262176 | tf_op jit(solution)/shard_map/ppermute | solution.py:183
  33.8 3.1 %collective-permute-done.2.refs_2_ = bf16[4,2,128,128]{3,2,1,0:T(8,128)(2,1)S(1)} collective-permute-done((bf16[4,2,128,128]{3,2,1,0:T(8,128)(2,1)S(1)}, bf16[4,2,128,128]{3,2,1,0:T(8,128)(2,1)S(1)}, u32[]{:S(2)}, u32[]{:S(2)}) %collective-permute-start.2) | collective-permute-done | bytes 262176 | tf_op jit(solution)/shard_map/ppermute | solution.py:183
  37.0 3.8 %collective-permute-done.3.refs_3_ = bf16[4,2,128,128]{3,2,1,0:T(8,128)(2,1)S(1)} collective-permute-done((bf16[4,2,128,128]{3,2,1,0:T(8,128)(2,1)S(1)}, bf16[4,2,128,128]{3,2,1,0:T(8,128)(2,1)S(1)}, u32[]{:S(2)}, u32[]{:S(2)}) %collective-permute-start.3) | collective-permute-done | bytes 262176 | tf_op jit(solution)/shard_map/ppermute | solution.py:183
  40.8 0.1 stage.1
  40.9 3.4 %collective-permute-start.4 = (bf16[2,128,128]{2,1,0:T(8,128)(2,1)S(1)}, bf16[2,128,128]{2,1,0:T(8,128)(2,1)S(1)}, u32[]{:S(2)}, u32[]{:S(2)}) collective-permute-start(bf16[2,128,128]{2,1,0:T(8,128)(2,1)S(1)} %get-tuple-element.18), channel_id=1, source_target_pairs={{0,64},{64,128},{128,192},{192,0},{1,65},{65,129},{129,193},{193,1... | collective-permute-start | bytes 196616 | tf_op jit(solution)/shard_map/ppermute | solution.py:183
  44.2 4.5 %collective-permute-start.5 = (bf16[2,128,128]{2,1,0:T(8,128)(2,1)S(1)}, bf16[2,128,128]{2,1,0:T(8,128)(2,1)S(1)}, u32[]{:S(2)}, u32[]{:S(2)}) collective-permute-start(bf16[2,128,128]{2,1,0:T(8,128)(2,1)S(1)} %get-tuple-element.19), channel_id=1, source_target_pairs={{0,128},{64,192},{128,0},{192,64},{1,129},{65,193},{129,1},{193,65... | collective-permute-start | bytes 196616 | tf_op jit(solution)/shard_map/ppermute | solution.py:183
  48.7 2.7 %collective-permute-start.6 = (bf16[2,128,128]{2,1,0:T(8,128)(2,1)S(1)}, bf16[2,128,128]{2,1,0:T(8,128)(2,1)S(1)}, u32[]{:S(2)}, u32[]{:S(2)}) collective-permute-start(bf16[2,128,128]{2,1,0:T(8,128)(2,1)S(1)} %get-tuple-element.20), channel_id=1, source_target_pairs={{0,192},{64,0},{128,64},{192,128},{1,193},{65,1},{129,65},{193,129... | collective-permute-start | bytes 196616 | tf_op jit(solution)/shard_map/ppermute | solution.py:183
  52.1 0.0 collective-permute-done.4
  52.1 2.0 %collective-permute-done.5 = bf16[2,128,128]{2,1,0:T(8,128)(2,1)S(1)} collective-permute-done((bf16[2,128,128]{2,1,0:T(8,128)(2,1)S(1)}, bf16[2,128,128]{2,1,0:T(8,128)(2,1)S(1)}, u32[]{:S(2)}, u32[]{:S(2)}) %collective-permute-start.5) | collective-permute-done | bytes 65568 | tf_op jit(solution)/shard_map/ppermute | solution.py:183
  54.1 0.7 %collective-permute-done.6 = bf16[2,128,128]{2,1,0:T(8,128)(2,1)S(1)} collective-permute-done((bf16[2,128,128]{2,1,0:T(8,128)(2,1)S(1)}, bf16[2,128,128]{2,1,0:T(8,128)(2,1)S(1)}, u32[]{:S(2)}, u32[]{:S(2)}) %collective-permute-start.6) | collective-permute-done | bytes 65568 | tf_op jit(solution)/shard_map/ppermute | solution.py:183
  54.8 0.7 %multiply_bitcast_fusion = f32[1,1,2,128,128]{4,3,2,1,0:T(8,128)} fusion(bf16[2,128,128]{2,1,0:T(8,128)(2,1)S(1)} %collective-permute-done.6, bf16[2,128,128]{2,1,0:T(8,128)(2,1)S(1)} %collective-permute-done.5, f32[2,128,128]{2,1,0:T(8,128)S(1)} %get-tuple-element.17, bf16[2,128,128]{2,1,0:T(8,128)(2,1)S(1)} %collective-permute-done.4, f32[]{:T(128)S(6)} %mul_shard_map.3), kind=kLoop, calls=%fused_computation | loop fusion | flops 229376 | bytes 458756 | tf_op jit(solution)/shard_map/broadcast_in_dim | solution.py:204
Async XLA Ops:
  0.0 21.1 %copy-start = (s32[32,2]{0,1:T(2,128)S(1)}, s32[32,2]{0,1:T(2,128)}, u32[]{:S(2)}) copy-start(s32[32,2]{0,1:T(2,128)} %param.5) | copy-start | bytes 772
  21.1 1.9 %collective-permute-start = (bf16[16,128,128]{2,1,0:T(8,128)(2,1)S(1)}, bf16[16,128,128]{2,1,0:T(8,128)(2,1)S(1)}, u32[]{:S(2)}, u32[]{:S(2)}) collective-permute-start(bf16[16,128,128]{2,1,0:T(8,128)(2,1)S(1)} %bitcast.5), channel_id=1, source_target_pairs={{0,8},{8,0},{1,9},{9,1},{2,10},{10,2},{3,11},{11,3},{4,12},{12,4},... | collective-permute-start | bytes 1572872 | tf_op jit(solution)/shard_map/ppermute | solution.py:183
  24.6 9.2 %collective-permute-start.1 = (bf16[4,2,128,128]{3,2,1,0:T(8,128)(2,1)S(1)}, bf16[4,2,128,128]{3,2,1,0:T(8,128)(2,1)S(1)}, u32[]{:S(2)}, u32[]{:S(2)}) collective-permute-start(bf16[4,2,128,128]{3,2,1,0:T(8,128)(2,1)S(1)} %get-tuple-element.14), channel_id=1, source_target_pairs={{0,16},{16,32},{32,48},{48,0},{1,17},{17,33},{33,49},{49,1},{2,18}... | collective-permute-start | bytes 786440 | tf_op jit(solution)/shard_map/ppermute | solution.py:183
  26.3 10.7 %collective-permute-start.2 = (bf16[4,2,128,128]{3,2,1,0:T(8,128)(2,1)S(1)}, bf16[4,2,128,128]{3,2,1,0:T(8,128)(2,1)S(1)}, u32[]{:S(2)}, u32[]{:S(2)}) collective-permute-start(bf16[4,2,128,128]{3,2,1,0:T(8,128)(2,1)S(1)} %get-tuple-element.15), channel_id=1, source_target_pairs={{0,32},{16,48},{32,0},{48,16},{1,33},{17,49},{33,1},{49,17},{2,34}... | collective-permute-start | bytes 786440 | tf_op jit(solution)/shard_map/ppermute | solution.py:183
  27.2 13.6 %collective-permute-start.3 = (bf16[4,2,128,128]{3,2,1,0:T(8,128)(2,1)S(1)}, bf16[4,2,128,128]{3,2,1,0:T(8,128)(2,1)S(1)}, u32[]{:S(2)}, u32[]{:S(2)}) collective-permute-start(bf16[4,2,128,128]{3,2,1,0:T(8,128)(2,1)S(1)} %get-tuple-element.16), channel_id=1, source_target_pairs={{0,48},{16,0},{32,16},{48,32},{1,49},{17,1},{33,17},{49,33},{2,50}... | collective-permute-start | bytes 786440 | tf_op jit(solution)/shard_map/ppermute | solution.py:183
  40.9 11.2 %collective-permute-start.4 = (bf16[2,128,128]{2,1,0:T(8,128)(2,1)S(1)}, bf16[2,128,128]{2,1,0:T(8,128)(2,1)S(1)}, u32[]{:S(2)}, u32[]{:S(2)}) collective-permute-start(bf16[2,128,128]{2,1,0:T(8,128)(2,1)S(1)} %get-tuple-element.18), channel_id=1, source_target_pairs={{0,64},{64,128},{128,192},{192,0},{1,65},{65,129},{129,193},{193,1... | collective-permute-start | bytes 196616 | tf_op jit(solution)/shard_map/ppermute | solution.py:183
  44.2 9.8 %collective-permute-start.5 = (bf16[2,128,128]{2,1,0:T(8,128)(2,1)S(1)}, bf16[2,128,128]{2,1,0:T(8,128)(2,1)S(1)}, u32[]{:S(2)}, u32[]{:S(2)}) collective-permute-start(bf16[2,128,128]{2,1,0:T(8,128)(2,1)S(1)} %get-tuple-element.19), channel_id=1, source_target_pairs={{0,128},{64,192},{128,0},{192,64},{1,129},{65,193},{129,1},{193,65... | collective-permute-start | bytes 196616 | tf_op jit(solution)/shard_map/ppermute | solution.py:183
  48.7 6.1 %collective-permute-start.6 = (bf16[2,128,128]{2,1,0:T(8,128)(2,1)S(1)}, bf16[2,128,128]{2,1,0:T(8,128)(2,1)S(1)}, u32[]{:S(2)}, u32[]{:S(2)}) collective-permute-start(bf16[2,128,128]{2,1,0:T(8,128)(2,1)S(1)} %get-tuple-element.20), channel_id=1, source_target_pairs={{0,192},{64,0},{128,64},{192,128},{1,193},{65,1},{129,65},{193,129... | collective-permute-start | bytes 196616 | tf_op jit(solution)/shard_map/ppermute | solution.py:183

commit v3 on v2

--- a/solution.py
+++ b/solution.py
@@ -1,3 +1,4 @@
+import functools
 import math
 
 import jax
@@ -103,52 +104,46 @@
     )(in_hbm(traces), in_hbm(table))
 
 
-def products_kernel(pairs, own, sib, *outs):
+def products_kernel(offset, pairs, own, sib, out):
     lanes = lax.broadcasted_iota(jnp.int32, (BLOCK, 128), 1)
     is_re = lanes < 64
     dims = (((1,), (1,)), ((), ()))
-    here_z = lax.axis_index("zh")
-    here_y = lax.axis_index("y")
-    core = lax.axis_index("core")
+    size_z = lax.axis_size("zh")
+    size_y = lax.axis_size("y")
     cores = lax.axis_size("core")
-    for d, out in enumerate(outs):
-        size_z = out.shape[0]
-        for e in range(size_z):
-            chip = (here_z + e) % size_z * len(outs) + (here_y + d) % len(outs)
-            slot = chip * cores + core
-            r = pairs[slot, 0]
-            s = pairs[slot, 1]
-            upper = []
-            rotated = []
-            lower = []
-            for ref in (own, sib):
-                block = ref[r]
-                turned = pltpu.roll(block.astype(jnp.float32), 64, 1)
-                upper.append(block)
-                rotated.append(jnp.where(is_re, turned, -turned).astype(block.dtype))
-                lower.append(ref[s])
-            a = jnp.concatenate([jnp.concatenate(upper, 1), jnp.concatenate(rotated, 1)], 0)
-            b = jnp.concatenate(lower, 1)
-            both = lax.dot_general(a, b, dims, preferred_element_type=jnp.float32)
-            out[e, 0] = both[:BLOCK].astype(out.dtype)
-            out[e, 1] = both[BLOCK:].astype(out.dtype)
+    to_y = (lax.axis_index("y") + offset) % size_y
+    for e in range(size_z):
+        to_z = (lax.axis_index("zh") + e) % size_z
+        slot = (to_z * size_y + to_y) * cores + lax.axis_index("core")
+        r = pairs[slot, 0]
+        s = pairs[slot, 1]
+        upper = []
+        rotated = []
+        lower = []
+        for ref in (own, sib):
+            block = ref[r]
+            turned = pltpu.roll(block.astype(jnp.float32), 64, 1)
+            upper.append(block)
+            rotated.append(jnp.where(is_re, turned, -turned).astype(block.dtype))
+            lower.append(ref[s])
+        a = jnp.concatenate([jnp.concatenate(upper, 1), jnp.concatenate(rotated, 1)], 0)
+        b = jnp.concatenate(lower, 1)
+        both = lax.dot_general(a, b, dims, preferred_element_type=jnp.float32)
+        out[e, 0] = both[:BLOCK].astype(out.dtype)
+        out[e, 1] = both[BLOCK:].astype(out.dtype)
 
 
 def vmem():
     return pl.BlockSpec(memory_space=pltpu.VMEM)
 
 
-def partial_sums(pairs, own, sib):
-    size_z = lax.axis_size("zh")
-    size_y = lax.axis_size("y")
-    shape = (size_z, 2, BLOCK, BLOCK)
+def partial_sums(offset, pairs, own, sib):
+    shape = (lax.axis_size("zh"), 2, BLOCK, BLOCK)
     return pl.pallas_call(
-        products_kernel,
-        out_shape=[
-            jax.ShapeDtypeStruct(shape, jnp.bfloat16 if d else jnp.float32) for d in range(size_y)
-        ],
+        functools.partial(products_kernel, offset),
+        out_shape=jax.ShapeDtypeStruct(shape, jnp.bfloat16 if offset else jnp.float32),
         in_specs=[pl.BlockSpec(memory_space=pltpu.SMEM), vmem(), vmem()],
-        out_specs=[vmem()] * size_y,
+        out_specs=vmem(),
         compiler_params=pltpu.CompilerParams(vmem_limit_bytes=8 << 20),
         name="products",
     )(pairs, own, sib)
@@ -183,8 +178,8 @@
     return lax.ppermute(values, axis, [(i, (i + offset) % size) for i in range(size)])
 
 
-def spread(arrays, axis):
-    return [arrays[0]] + [shifted(values, axis, d) for d, values in enumerate(arrays) if d]
+def far_first(size):
+    return sorted(range(1, size), key=lambda d: -min(d, size - d))
 
 
 def on_device(traces, block_pairs, valid_count):
@@ -193,10 +188,12 @@
     banded = lax.all_to_all(grouped, ("zl", "x"), split_axis=0, concat_axis=0, tiled=True)
     own = banded.reshape(-1, BLOCK, banded.shape[2])
     sib = shifted(own, "core", 1)
-    along_y = spread(partial_sums(block_pairs, own, sib), "y")
-    along_z = spread(stage_sums(along_y), "zh")
-    total = along_z[0]
-    for values in along_z[1:]:
+    arrived = []
+    for d in far_first(lax.axis_size("y")):
+        arrived.append(shifted(partial_sums(d, block_pairs, own, sib), "y", d))
+    staged = stage_sums([partial_sums(0, block_pairs, own, sib)] + arrived)
+    total = staged[0]
+    for values in [shifted(staged[e], "zh", e) for e in far_first(len(staged))]:
         total = total + values.astype(jnp.float32)
     stack_scale = 1.0 / math.sqrt(windows * GROUP)
     slot = lax.axis_index(("zh", "y", "core"))

time: 56.3 us -> 56.2 us (level); the launches traced: 55.5 us -> 56.1 us
  Pallas kernels: 7.27 us -> 10.3 us
  waiting for transfers between devices: 15.7 us -> 13.7 us
    pallas_call x1 -> x4, Pallas kernels: 1.56 us -> 4.58 us  [partial_sums(): pl.pallas_call(functools.partial(products_kernel, offset), out_shape=jax....]
    ppermute x7, waiting for transfers between devices: 15.7 us -> 13.7 us  [shifted(): lax.ppermute(values, axis, [(i, (i + offset) % size) for i in range(size)])]
  transfers between devices with their start and end apart: 7 -> 7, of which waited for: 6 -> 6; matrix products, arithmetic and copies ran while one was open for 0% -> 0% of each run, Pallas kernels for 0% -> 6%
where the time goes in v3:
time: 56.2 us; the launch traced here: 56.1 us
  blocking collectives  15.5 us (28%)
  starting transfers between devices  15.1 us (27%)
  waiting for transfers between devices  13.7 us (24%)
  Pallas kernels  10.3 us (18%)
  between operations  0.72 us (1%)
  other arithmetic  0.69 us (1%)
    all_to_all x1, blocking collectives, on_device(): lax.all_to_all(grouped, ('zl', 'x'), split_axis=0, concat_axis=0, tiled=T...  15.5 us
    ppermute x7, starting transfers between devices, shifted(): lax.ppermute(values, axis, [(i, (i + offset) % size) for i in range(size)])  15.1 us
    ppermute x7, waiting for transfers between devices, shifted(): lax.ppermute(values, axis, [(i, (i + offset) % size) for i in range(size)])  13.7 us
    pallas_call x1, Pallas kernels, whitened_groups(): pl.pallas_call(spectra_kernel, out_shape=jax.ShapeDtypeStruct((groups, ch...  5.6 us
    pallas_call x4, Pallas kernels, partial_sums(): pl.pallas_call(functools.partial(products_kernel, offset), out_shape=jax....  4.58 us
  transfers between devices with their start and end apart: 7, of which 6 were waited for; matrix products, arithmetic and copies ran while one was open for 0% of the time, Pallas kernels for 6%

profile of v3, /device:TPU:8, one launch (start us, length us, event | category | flops | bytes accessed | tf_op | source)
XLA Modules:
  0.0 56.1 jit_solution(11068414876980921409)
XLA Ops:
  0.0 0.0 copy-start
  0.0 5.6 %spectra.1 = bf16[8,256,128]{2,1,0:T(8,128)(2,1)S(1)} custom-call(bf16[2,256,4096]{2,1,0:T(8,128)(2,1)} %traces.1, bf16[1024,512]{1,0:T(8,128)(2,1)} %constant.25.clone.table), custom_call_target="tpu_custom_call" | custom-call | tf_op jit(solution)/shard_map/spectra/pallas_call | solution.py:92
  5.6 15.5 %all_to_all.5 = bf16[8,256,128]{2,1,0:T(8,128)(2,1)S(1)} all-to-all(bf16[8,256,128]{2,1,0:T(8,128)(2,1)S(1)} %spectra.1), channel_id=1, replica_groups=mesh['zh'=4,'y'=4,'core'=2,'zl'=2,'x'=4] {'zl','x'}, dimensions={0} | all-to-all | bytes 1048576 | tf_op jit(solution)/shard_map/all_to_all | solution.py:188
  21.1 0.0 collective-permute-start
  21.1 0.0 copy-done
  21.1 0.1 copy.5.pairs
  21.2 1.8 %collective-permute-done.sib = bf16[16,128,128]{2,1,0:T(8,128)(2,1)S(1)} collective-permute-done((bf16[16,128,128]{2,1,0:T(8,128)(2,1)S(1)}, bf16[16,128,128]{2,1,0:T(8,128)(2,1)S(1)}, u32[]{:S(2)}, u32[]{:S(2)}) %collective-permute-start) | collective-permute-done | bytes 524320 | tf_op jit(solution)/shard_map/ppermute | solution.py:178
  23.0 1.1 %products.6 = bf16[4,2,128,128]{3,2,1,0:T(8,128)(2,1)S(1)} custom-call(s32[32,2]{1,0:T(8,128)S(1)} %copy.5.pairs, bf16[16,128,128]{2,1,0:T(8,128)(2,1)S(1)} %bitcast.6, bf16[16,128,128]{2,1,0:T(8,128)(2,1)S(1)} %collective-permute-done.sib), custom_call_target="tpu_custom_call" | custom-call | tf_op jit(solution)/shard_map/products/pallas_call | solution.py:142
  24.2 1.7 %collective-permute-start.2 = (bf16[4,2,128,128]{3,2,1,0:T(8,128)(2,1)S(1)}, bf16[4,2,128,128]{3,2,1,0:T(8,128)(2,1)S(1)}, u32[]{:S(2)}, u32[]{:S(2)}) collective-permute-start(bf16[4,2,128,128]{3,2,1,0:T(8,128)(2,1)S(1)} %products.6), channel_id=1, source_target_pairs={{0,16},{16,32},{32,48},{48,0},{1,17},{17,33},{33,49},{49,1},{2,18}... | collective-permute-start | bytes 786440 | tf_op jit(solution)/shard_map/ppermute | solution.py:178
  25.9 1.1 %products.7 = bf16[4,2,128,128]{3,2,1,0:T(8,128)(2,1)S(1)} custom-call(s32[32,2]{1,0:T(8,128)S(1)} %copy.5.pairs, bf16[16,128,128]{2,1,0:T(8,128)(2,1)S(1)} %bitcast.7, bf16[16,128,128]{2,1,0:T(8,128)(2,1)S(1)} %collective-permute-done.sib), custom_call_target="tpu_custom_call" | custom-call | tf_op jit(solution)/shard_map/products/pallas_call | solution.py:142
  27.0 0.5 collective-permute-start.3
  27.5 1.1 %products.5 = bf16[4,2,128,128]{3,2,1,0:T(8,128)(2,1)S(1)} custom-call(s32[32,2]{1,0:T(8,128)S(1)} %copy.5.pairs, bf16[16,128,128]{2,1,0:T(8,128)(2,1)S(1)} %bitcast.8, bf16[16,128,128]{2,1,0:T(8,128)(2,1)S(1)} %collective-permute-done.sib), custom_call_target="tpu_custom_call" | custom-call | tf_op jit(solution)/shard_map/products/pallas_call | solution.py:142
  28.7 2.4 %collective-permute-start.1 = (bf16[4,2,128,128]{3,2,1,0:T(8,128)(2,1)S(1)}, bf16[4,2,128,128]{3,2,1,0:T(8,128)(2,1)S(1)}, u32[]{:S(2)}, u32[]{:S(2)}) collective-permute-start(bf16[4,2,128,128]{3,2,1,0:T(8,128)(2,1)S(1)} %products.5), channel_id=1, source_target_pairs={{0,32},{16,48},{32,0},{48,16},{1,33},{17,49},{33,1},{49,17},{2,34}... | collective-permute-start | bytes 786440 | tf_op jit(solution)/shard_map/ppermute | solution.py:178
  31.1 1.1 %products.4.refs_0_ = f32[4,2,128,128]{3,2,1,0:T(8,128)S(1)} custom-call(s32[32,2]{1,0:T(8,128)S(1)} %copy.5.pairs, bf16[16,128,128]{2,1,0:T(8,128)(2,1)S(1)} %bitcast.9, bf16[16,128,128]{2,1,0:T(8,128)(2,1)S(1)} %collective-permute-done.sib), custom_call_target="tpu_custom_call" | custom-call | tf_op jit(solution)/shard_map/products/pallas_call | solution.py:142
  32.2 0.4 collective-permute-done.2.refs_2_
  32.6 2.9 %collective-permute-done.3.refs_3_ = bf16[4,2,128,128]{3,2,1,0:T(8,128)(2,1)S(1)} collective-permute-done((bf16[4,2,128,128]{3,2,1,0:T(8,128)(2,1)S(1)}, bf16[4,2,128,128]{3,2,1,0:T(8,128)(2,1)S(1)}, u32[]{:S(2)}, u32[]{:S(2)}) %collective-permute-start.3) | collective-permute-done | bytes 262176 | tf_op jit(solution)/shard_map/ppermute | solution.py:178
  35.5 5.9 %collective-permute-done.1.refs_1_ = bf16[4,2,128,128]{3,2,1,0:T(8,128)(2,1)S(1)} collective-permute-done((bf16[4,2,128,128]{3,2,1,0:T(8,128)(2,1)S(1)}, bf16[4,2,128,128]{3,2,1,0:T(8,128)(2,1)S(1)}, u32[]{:S(2)}, u32[]{:S(2)}) %collective-permute-start.1) | collective-permute-done | bytes 262176 | tf_op jit(solution)/shard_map/ppermute | solution.py:178
  41.5 0.1 stage.1
  41.6 6.4 %collective-permute-start.4 = (bf16[2,128,128]{2,1,0:T(8,128)(2,1)S(1)}, bf16[2,128,128]{2,1,0:T(8,128)(2,1)S(1)}, u32[]{:S(2)}, u32[]{:S(2)}) collective-permute-start(bf16[2,128,128]{2,1,0:T(8,128)(2,1)S(1)} %get-tuple-element.10), channel_id=1, source_target_pairs={{0,128},{64,192},{128,0},{192,64},{1,129},{65,193},{129,1},{193,65... | collective-permute-start | bytes 196616 | tf_op jit(solution)/shard_map/ppermute | solution.py:178
  48.0 1.5 %collective-permute-start.5 = (bf16[2,128,128]{2,1,0:T(8,128)(2,1)S(1)}, bf16[2,128,128]{2,1,0:T(8,128)(2,1)S(1)}, u32[]{:S(2)}, u32[]{:S(2)}) collective-permute-start(bf16[2,128,128]{2,1,0:T(8,128)(2,1)S(1)} %get-tuple-element.11), channel_id=1, source_target_pairs={{0,64},{64,128},{128,192},{192,0},{1,65},{65,129},{129,193},{193,1... | collective-permute-start | bytes 196616 | tf_op jit(solution)/shard_map/ppermute | solution.py:178
  49.5 2.7 %collective-permute-start.6 = (bf16[2,128,128]{2,1,0:T(8,128)(2,1)S(1)}, bf16[2,128,128]{2,1,0:T(8,128)(2,1)S(1)}, u32[]{:S(2)}, u32[]{:S(2)}) collective-permute-start(bf16[2,128,128]{2,1,0:T(8,128)(2,1)S(1)} %get-tuple-element.12), channel_id=1, source_target_pairs={{0,192},{64,0},{128,64},{192,128},{1,193},{65,1},{129,65},{193,129... | collective-permute-start | bytes 196616 | tf_op jit(solution)/shard_map/ppermute | solution.py:178
  52.8 0.0 collective-permute-done.4
  52.8 1.6 %collective-permute-done.5 = bf16[2,128,128]{2,1,0:T(8,128)(2,1)S(1)} collective-permute-done((bf16[2,128,128]{2,1,0:T(8,128)(2,1)S(1)}, bf16[2,128,128]{2,1,0:T(8,128)(2,1)S(1)}, u32[]{:S(2)}, u32[]{:S(2)}) %collective-permute-start.5) | collective-permute-done | bytes 65568 | tf_op jit(solution)/shard_map/ppermute | solution.py:178
  54.4 1.0 %collective-permute-done.6 = bf16[2,128,128]{2,1,0:T(8,128)(2,1)S(1)} collective-permute-done((bf16[2,128,128]{2,1,0:T(8,128)(2,1)S(1)}, bf16[2,128,128]{2,1,0:T(8,128)(2,1)S(1)}, u32[]{:S(2)}, u32[]{:S(2)}) %collective-permute-start.6) | collective-permute-done | bytes 65568 | tf_op jit(solution)/shard_map/ppermute | solution.py:178
  55.4 0.7 %multiply_bitcast_fusion = f32[1,1,2,128,128]{4,3,2,1,0:T(8,128)} fusion(bf16[2,128,128]{2,1,0:T(8,128)(2,1)S(1)} %collective-permute-done.6, bf16[2,128,128]{2,1,0:T(8,128)(2,1)S(1)} %collective-permute-done.5, f32[2,128,128]{2,1,0:T(8,128)S(1)} %get-tuple-element.9, bf16[2,128,128]{2,1,0:T(8,128)(2,1)S(1)} %collective-permute-done.4, f32[]{:T(128)S(6)} %mul_shard_map.3), kind=kLoop, calls=%fused_computation | loop fusion | flops 229376 | bytes 458756 | tf_op jit(solution)/shard_map/broadcast_in_dim | solution.py:201
Async XLA Ops:
  0.0 21.1 %copy-start = (s32[32,2]{0,1:T(2,128)S(1)}, s32[32,2]{0,1:T(2,128)}, u32[]{:S(2)}) copy-start(s32[32,2]{0,1:T(2,128)} %param.5) | copy-start | bytes 772
  21.1 1.9 %collective-permute-start = (bf16[16,128,128]{2,1,0:T(8,128)(2,1)S(1)}, bf16[16,128,128]{2,1,0:T(8,128)(2,1)S(1)}, u32[]{:S(2)}, u32[]{:S(2)}) collective-permute-start(bf16[16,128,128]{2,1,0:T(8,128)(2,1)S(1)} %bitcast.5), channel_id=1, source_target_pairs={{0,8},{8,0},{1,9},{9,1},{2,10},{10,2},{3,11},{11,3},{4,12},{12,4},... | collective-permute-start | bytes 1572872 | tf_op jit(solution)/shard_map/ppermute | solution.py:178
  24.2 8.4 %collective-permute-start.2 = (bf16[4,2,128,128]{3,2,1,0:T(8,128)(2,1)S(1)}, bf16[4,2,128,128]{3,2,1,0:T(8,128)(2,1)S(1)}, u32[]{:S(2)}, u32[]{:S(2)}) collective-permute-start(bf16[4,2,128,128]{3,2,1,0:T(8,128)(2,1)S(1)} %products.6), channel_id=1, source_target_pairs={{0,16},{16,32},{32,48},{48,0},{1,17},{17,33},{33,49},{49,1},{2,18}... | collective-permute-start | bytes 786440 | tf_op jit(solution)/shard_map/ppermute | solution.py:178
  27.0 8.5 %collective-permute-start.3 = (bf16[4,2,128,128]{3,2,1,0:T(8,128)(2,1)S(1)}, bf16[4,2,128,128]{3,2,1,0:T(8,128)(2,1)S(1)}, u32[]{:S(2)}, u32[]{:S(2)}) collective-permute-start(bf16[4,2,128,128]{3,2,1,0:T(8,128)(2,1)S(1)} %products.7), channel_id=1, source_target_pairs={{0,48},{16,0},{32,16},{48,32},{1,49},{17,1},{33,17},{49,33},{2,50}... | collective-permute-start | bytes 786440 | tf_op jit(solution)/shard_map/ppermute | solution.py:178
  28.7 12.8 %collective-permute-start.1 = (bf16[4,2,128,128]{3,2,1,0:T(8,128)(2,1)S(1)}, bf16[4,2,128,128]{3,2,1,0:T(8,128)(2,1)S(1)}, u32[]{:S(2)}, u32[]{:S(2)}) collective-permute-start(bf16[4,2,128,128]{3,2,1,0:T(8,128)(2,1)S(1)} %products.5), channel_id=1, source_target_pairs={{0,32},{16,48},{32,0},{48,16},{1,33},{17,49},{33,1},{49,17},{2,34}... | collective-permute-start | bytes 786440 | tf_op jit(solution)/shard_map/ppermute | solution.py:178
  41.6 11.2 %collective-permute-start.4 = (bf16[2,128,128]{2,1,0:T(8,128)(2,1)S(1)}, bf16[2,128,128]{2,1,0:T(8,128)(2,1)S(1)}, u32[]{:S(2)}, u32[]{:S(2)}) collective-permute-start(bf16[2,128,128]{2,1,0:T(8,128)(2,1)S(1)} %get-tuple-element.10), channel_id=1, source_target_pairs={{0,128},{64,192},{128,0},{192,64},{1,129},{65,193},{129,1},{193,65... | collective-permute-start | bytes 196616 | tf_op jit(solution)/shard_map/ppermute | solution.py:178
  48.0 6.4 %collective-permute-start.5 = (bf16[2,128,128]{2,1,0:T(8,128)(2,1)S(1)}, bf16[2,128,128]{2,1,0:T(8,128)(2,1)S(1)}, u32[]{:S(2)}, u32[]{:S(2)}) collective-permute-start(bf16[2,128,128]{2,1,0:T(8,128)(2,1)S(1)} %get-tuple-element.11), channel_id=1, source_target_pairs={{0,64},{64,128},{128,192},{192,0},{1,65},{65,129},{129,193},{193,1... | collective-permute-start | bytes 196616 | tf_op jit(solution)/shard_map/ppermute | solution.py:178
  49.5 5.9 %collective-permute-start.6 = (bf16[2,128,128]{2,1,0:T(8,128)(2,1)S(1)}, bf16[2,128,128]{2,1,0:T(8,128)(2,1)S(1)}, u32[]{:S(2)}, u32[]{:S(2)}) collective-permute-start(bf16[2,128,128]{2,1,0:T(8,128)(2,1)S(1)} %get-tuple-element.12), channel_id=1, source_target_pairs={{0,192},{64,0},{128,64},{192,128},{1,193},{65,1},{129,65},{193,129... | collective-permute-start | bytes 196616 | tf_op jit(solution)/shard_map/ppermute | solution.py:178

commit v4 on v2

--- a/solution.py
+++ b/solution.py
@@ -14,6 +14,7 @@
 GROUP = 32
 EPS = 1e-06
 QUARTERS = 4
+ROWS = 32
 
 
 def packed_table(length):
@@ -38,7 +39,7 @@
         )
         load.start()
         loads.append(load)
-    lanes = lax.broadcasted_iota(jnp.int32, (span, 128), 1)
+    lanes = lax.broadcasted_iota(jnp.int32, (1, 128), 1)
     bin4 = (FREQ_LO + lanes) % 4
     sign2 = jnp.where(bin4 % 2 == 0, 1.0, -1.0)
     direct = jnp.where(bin4 == 0, 1.0, jnp.where(bin4 == 2, -1.0, 0.0))
@@ -46,7 +47,36 @@
     cross = jnp.where(lanes < 64, up, -up)
     lane32 = lanes // 32 % 2
     tiles = 2 * NBINS // 128
+
+    def finish(step, dots):
+        for start in range(0, span, ROWS):
+            spans = []
+            for w in range(windows):
+                parts = []
+                squares = jnp.zeros((ROWS, 128), jnp.float32)
+                for t in range(tiles):
+                    first_rows = [(q * windows + w) * span + start for q in range(QUARTERS)]
+                    d0, d1, d2, d3 = (
+                        dots[row : row + ROWS, t * 128 : (t + 1) * 128] for row in first_rows
+                    )
+                    main = d0 + sign2 * d2
+                    turn = d1 + sign2 * d3
+                    full = main + direct * turn + cross * pltpu.roll(turn, 64, 1)
+                    squares = squares + full * full
+                    parts.append(full)
+                energy = jnp.sum(squares, axis=1, keepdims=True)
+                scale = lax.rsqrt(energy / NBINS + EPS)
+                spans.append([part * scale for part in parts])
+            rows = pl.ds(step * span + start, ROWS)
+            for t in range(tiles):
+                first, second = spans[0][t], spans[1][t]
+                even = jnp.where(lane32 == 0, first, pltpu.roll(second, 32, 1))
+                odd = jnp.where(lane32 == 1, first, pltpu.roll(second, 96, 1))
+                out[2 * t, rows] = even.astype(out.dtype)
+                out[2 * t + 1, rows] = odd.astype(out.dtype)
+
     load_table.wait()
+    before = None
     for step in range(steps):
         loads[step].wait()
         whole = buf[step].reshape(windows * span, length)
@@ -54,30 +84,10 @@
             [whole[:, q * quarter : (q + 1) * quarter] for q in range(QUARTERS)], axis=0
         )
         dots = jnp.dot(stacked, table_buf[...], preferred_element_type=jnp.float32)
-        spans = []
-        for w in range(windows):
-            parts = []
-            energy = jnp.zeros((span, 1), jnp.float32)
-            for t in range(tiles):
-                cols = slice(t * 128, (t + 1) * 128)
-                d0, d1, d2, d3 = (
-                    dots[(q * windows + w) * span : (q * windows + w + 1) * span, cols]
-                    for q in range(QUARTERS)
-                )
-                main = d0 + sign2 * d2
-                turn = d1 + sign2 * d3
-                full = main + direct * turn + cross * pltpu.roll(turn, 64, 1)
-                energy = energy + jnp.sum(full * full, axis=1, keepdims=True)
-                parts.append(full)
-            scale = lax.rsqrt(energy / NBINS + EPS)
-            spans.append([part * scale for part in parts])
-        rows = pl.ds(step * span, span)
-        for t in range(tiles):
-            first, second = spans[0][t], spans[1][t]
-            out[2 * t, rows] = jnp.where(lane32 == 0, first, pltpu.roll(second, 32, 1)).astype(out.dtype)
-            out[2 * t + 1, rows] = jnp.where(lane32 == 1, first, pltpu.roll(second, 96, 1)).astype(
-                out.dtype
-            )
+        if step:
+            finish(step - 1, before)
+        before = dots
+    finish(steps - 1, before)
 
 
 def in_hbm(values):
@@ -184,7 +194,9 @@
 
 
 def spread(arrays, axis):
-    return [arrays[0]] + [shifted(values, axis, d) for d, values in enumerate(arrays) if d]
+    size = len(arrays)
+    order = sorted(range(1, size), key=lambda d: -min(d, size - d))
+    return [arrays[0]] + [shifted(arrays[d], axis, d) for d in order]
 
 
 def on_device(traces, block_pairs, valid_count):

time: 56.3 us -> 54 us (0.959)
  Pallas kernels: 7.27 us -> 6.42 us
  starting transfers between devices: 15.5 us -> 14.9 us
  waiting for transfers between devices: 15.7 us -> 15.1 us
    pallas_call x1, Pallas kernels: 5.6 us -> 4.74 us  [whitened_groups(): pl.pallas_call(spectra_kernel, out_shape=jax.ShapeDtypeStruct((groups, ch...]
    ppermute x7, starting transfers between devices: 15.5 us -> 14.9 us  [shifted(): lax.ppermute(values, axis, [(i, (i + offset) % size) for i in range(size)])]
  transfers between devices with their start and end apart: 7 -> 7, of which waited for: 6 -> 5; matrix products, arithmetic and copies ran while one was open for 0% -> 0% of each run, Pallas kernels for 0% -> 0%
where the time goes in v4:
time: 54 us; the launch traced here: 53.5 us
  blocking collectives  15.5 us (29%)
  waiting for transfers between devices  15.1 us (28%)
  starting transfers between devices  14.9 us (28%)
  Pallas kernels  6.42 us (12%)
  other arithmetic  0.69 us (1%)
  between operations  0.69 us (1%)
    all_to_all x1, blocking collectives, on_device(): lax.all_to_all(grouped, ('zl', 'x'), split_axis=0, concat_axis=0, tiled=T...  15.5 us
    ppermute x7, waiting for transfers between devices, shifted(): lax.ppermute(values, axis, [(i, (i + offset) % size) for i in range(size)])  15.1 us
    ppermute x7, starting transfers between devices, shifted(): lax.ppermute(values, axis, [(i, (i + offset) % size) for i in range(size)])  14.9 us
    pallas_call x1, Pallas kernels, whitened_groups(): pl.pallas_call(spectra_kernel, out_shape=jax.ShapeDtypeStruct((groups, ch...  4.74 us
    pallas_call x1, Pallas kernels, partial_sums(): pl.pallas_call(products_kernel, out_shape=[jax.ShapeDtypeStruct(shape, jn...  1.56 us
  transfers between devices with their start and end apart: 7, of which 5 were waited for; matrix products, arithmetic and copies ran while one was open for 0% of the time, Pallas kernels for 0%

profile of v4, /device:TPU:8, one launch (start us, length us, event | category | flops | bytes accessed | tf_op | source)
XLA Modules:
  0.0 53.5 jit_solution(12228602785237392876)
XLA Ops:
  0.0 0.0 copy-start
  0.0 4.7 %spectra.1 = bf16[8,256,128]{2,1,0:T(8,128)(2,1)S(1)} custom-call(bf16[2,256,4096]{2,1,0:T(8,128)(2,1)} %traces.1, bf16[1024,512]{1,0:T(8,128)(2,1)} %constant.25.clone.table), custom_call_target="tpu_custom_call" | custom-call | tf_op jit(solution)/shard_map/spectra/pallas_call | solution.py:101
  4.8 15.5 %all_to_all.5 = bf16[8,256,128]{2,1,0:T(8,128)(2,1)S(1)} all-to-all(bf16[8,256,128]{2,1,0:T(8,128)(2,1)S(1)} %spectra.1), channel_id=1, replica_groups=mesh['zh'=4,'y'=4,'core'=2,'zl'=2,'x'=4] {'zl','x'}, dimensions={0} | all-to-all | bytes 1048576 | tf_op jit(solution)/shard_map/all_to_all | solution.py:205
  20.3 0.0 collective-permute-start
  20.3 0.0 copy-done
  20.3 0.1 copy.5.pairs
  20.4 1.8 %collective-permute-done.sib = bf16[16,128,128]{2,1,0:T(8,128)(2,1)S(1)} collective-permute-done((bf16[16,128,128]{2,1,0:T(8,128)(2,1)S(1)}, bf16[16,128,128]{2,1,0:T(8,128)(2,1)S(1)}, u32[]{:S(2)}, u32[]{:S(2)}) %collective-permute-start) | collective-permute-done | bytes 524320 | tf_op jit(solution)/shard_map/ppermute | solution.py:193
  22.2 1.6 %products.1 = (f32[4,2,128,128]{3,2,1,0:T(8,128)S(1)}, bf16[4,2,128,128]{3,2,1,0:T(8,128)(2,1)S(1)}, bf16[4,2,128,128]{3,2,1,0:T(8,128)(2,1)S(1)}, bf16[4,2,128,128]{3,2,1,0:T(8,128)(2,1)S(1)}) custom-call(s32[32,2]{1,0:T(8,128)S(1)} %copy.5.pairs, bf16[16,128,128]{2,1,0:T(8,128)(2,1)S(1)} %bitcast.6, bf16[16,128,128]{2,1,0:T(8,128)(2,1)S(1)} %collective-permute-done.sib), custom_call_target="tpu_custom_call" | custom-call | tf_op jit(solution)/shard_map/products/pallas_call | solution.py:155
  23.8 2.4 %collective-permute-start.1 = (bf16[4,2,128,128]{3,2,1,0:T(8,128)(2,1)S(1)}, bf16[4,2,128,128]{3,2,1,0:T(8,128)(2,1)S(1)}, u32[]{:S(2)}, u32[]{:S(2)}) collective-permute-start(bf16[4,2,128,128]{3,2,1,0:T(8,128)(2,1)S(1)} %get-tuple-element.14), channel_id=1, source_target_pairs={{0,32},{16,48},{32,0},{48,16},{1,33},{17,49},{33,1},{49,17},{2,34}... | collective-permute-start | bytes 786440 | tf_op jit(solution)/shard_map/ppermute | solution.py:193
  26.1 0.0 collective-permute-start.2
  26.2 2.0 %collective-permute-start.3 = (bf16[4,2,128,128]{3,2,1,0:T(8,128)(2,1)S(1)}, bf16[4,2,128,128]{3,2,1,0:T(8,128)(2,1)S(1)}, u32[]{:S(2)}, u32[]{:S(2)}) collective-permute-start(bf16[4,2,128,128]{3,2,1,0:T(8,128)(2,1)S(1)} %get-tuple-element.16), channel_id=1, source_target_pairs={{0,48},{16,0},{32,16},{48,32},{1,49},{17,1},{33,17},{49,33},{2,50}... | collective-permute-start | bytes 786440 | tf_op jit(solution)/shard_map/ppermute | solution.py:193
  28.2 6.4 %collective-permute-done.1.refs_1_ = bf16[4,2,128,128]{3,2,1,0:T(8,128)(2,1)S(1)} collective-permute-done((bf16[4,2,128,128]{3,2,1,0:T(8,128)(2,1)S(1)}, bf16[4,2,128,128]{3,2,1,0:T(8,128)(2,1)S(1)}, u32[]{:S(2)}, u32[]{:S(2)}) %collective-permute-start.1) | collective-permute-done | bytes 262176 | tf_op jit(solution)/shard_map/ppermute | solution.py:193
  34.6 4.9 %collective-permute-done.2.refs_2_ = bf16[4,2,128,128]{3,2,1,0:T(8,128)(2,1)S(1)} collective-permute-done((bf16[4,2,128,128]{3,2,1,0:T(8,128)(2,1)S(1)}, bf16[4,2,128,128]{3,2,1,0:T(8,128)(2,1)S(1)}, u32[]{:S(2)}, u32[]{:S(2)}) %collective-permute-start.2) | collective-permute-done | bytes 262176 | tf_op jit(solution)/shard_map/ppermute | solution.py:193
  39.5 0.0 collective-permute-done.3.refs_3_
  39.5 0.1 stage.1
  39.6 6.4 %collective-permute-start.4 = (bf16[2,128,128]{2,1,0:T(8,128)(2,1)S(1)}, bf16[2,128,128]{2,1,0:T(8,128)(2,1)S(1)}, u32[]{:S(2)}, u32[]{:S(2)}) collective-permute-start(bf16[2,128,128]{2,1,0:T(8,128)(2,1)S(1)} %get-tuple-element.18), channel_id=1, source_target_pairs={{0,128},{64,192},{128,0},{192,64},{1,129},{65,193},{129,1},{193,65... | collective-permute-start | bytes 196616 | tf_op jit(solution)/shard_map/ppermute | solution.py:193
  46.0 1.5 %collective-permute-start.5 = (bf16[2,128,128]{2,1,0:T(8,128)(2,1)S(1)}, bf16[2,128,128]{2,1,0:T(8,128)(2,1)S(1)}, u32[]{:S(2)}, u32[]{:S(2)}) collective-permute-start(bf16[2,128,128]{2,1,0:T(8,128)(2,1)S(1)} %get-tuple-element.19), channel_id=1, source_target_pairs={{0,64},{64,128},{128,192},{192,0},{1,65},{65,129},{129,193},{193,1... | collective-permute-start | bytes 196616 | tf_op jit(solution)/shard_map/ppermute | solution.py:193
  47.5 2.6 %collective-permute-start.6 = (bf16[2,128,128]{2,1,0:T(8,128)(2,1)S(1)}, bf16[2,128,128]{2,1,0:T(8,128)(2,1)S(1)}, u32[]{:S(2)}, u32[]{:S(2)}) collective-permute-start(bf16[2,128,128]{2,1,0:T(8,128)(2,1)S(1)} %get-tuple-element.20), channel_id=1, source_target_pairs={{0,192},{64,0},{128,64},{192,128},{1,193},{65,1},{129,65},{193,129... | collective-permute-start | bytes 196616 | tf_op jit(solution)/shard_map/ppermute | solution.py:193
  50.8 0.0 collective-permute-done.4
  50.8 1.6 %collective-permute-done.5 = bf16[2,128,128]{2,1,0:T(8,128)(2,1)S(1)} collective-permute-done((bf16[2,128,128]{2,1,0:T(8,128)(2,1)S(1)}, bf16[2,128,128]{2,1,0:T(8,128)(2,1)S(1)}, u32[]{:S(2)}, u32[]{:S(2)}) %collective-permute-start.5) | collective-permute-done | bytes 65568 | tf_op jit(solution)/shard_map/ppermute | solution.py:193
  52.3 0.5 collective-permute-done.6
  52.8 0.7 %multiply_bitcast_fusion = f32[1,1,2,128,128]{4,3,2,1,0:T(8,128)} fusion(bf16[2,128,128]{2,1,0:T(8,128)(2,1)S(1)} %collective-permute-done.6, bf16[2,128,128]{2,1,0:T(8,128)(2,1)S(1)} %collective-permute-done.5, f32[2,128,128]{2,1,0:T(8,128)S(1)} %get-tuple-element.17, bf16[2,128,128]{2,1,0:T(8,128)(2,1)S(1)} %collective-permute-done.4, f32[]{:T(128)S(6)} %mul_shard_map.3), kind=kLoop, calls=%fused_computation | loop fusion | flops 229376 | bytes 458756 | tf_op jit(solution)/shard_map/broadcast_in_dim | solution.py:216
Async XLA Ops:
  0.0 20.3 %copy-start = (s32[32,2]{0,1:T(2,128)S(1)}, s32[32,2]{0,1:T(2,128)}, u32[]{:S(2)}) copy-start(s32[32,2]{0,1:T(2,128)} %param.5) | copy-start | bytes 772
  20.3 1.9 %collective-permute-start = (bf16[16,128,128]{2,1,0:T(8,128)(2,1)S(1)}, bf16[16,128,128]{2,1,0:T(8,128)(2,1)S(1)}, u32[]{:S(2)}, u32[]{:S(2)}) collective-permute-start(bf16[16,128,128]{2,1,0:T(8,128)(2,1)S(1)} %bitcast.5), channel_id=1, source_target_pairs={{0,8},{8,0},{1,9},{9,1},{2,10},{10,2},{3,11},{11,3},{4,12},{12,4},... | collective-permute-start | bytes 1572872 | tf_op jit(solution)/shard_map/ppermute | solution.py:193
  23.8 10.8 %collective-permute-start.1 = (bf16[4,2,128,128]{3,2,1,0:T(8,128)(2,1)S(1)}, bf16[4,2,128,128]{3,2,1,0:T(8,128)(2,1)S(1)}, u32[]{:S(2)}, u32[]{:S(2)}) collective-permute-start(bf16[4,2,128,128]{3,2,1,0:T(8,128)(2,1)S(1)} %get-tuple-element.14), channel_id=1, source_target_pairs={{0,32},{16,48},{32,0},{48,16},{1,33},{17,49},{33,1},{49,17},{2,34}... | collective-permute-start | bytes 786440 | tf_op jit(solution)/shard_map/ppermute | solution.py:193
  26.1 13.3 %collective-permute-start.2 = (bf16[4,2,128,128]{3,2,1,0:T(8,128)(2,1)S(1)}, bf16[4,2,128,128]{3,2,1,0:T(8,128)(2,1)S(1)}, u32[]{:S(2)}, u32[]{:S(2)}) collective-permute-start(bf16[4,2,128,128]{3,2,1,0:T(8,128)(2,1)S(1)} %get-tuple-element.15), channel_id=1, source_target_pairs={{0,16},{16,32},{32,48},{48,0},{1,17},{17,33},{33,49},{49,1},{2,18}... | collective-permute-start | bytes 786440 | tf_op jit(solution)/shard_map/ppermute | solution.py:193
  26.2 13.3 %collective-permute-start.3 = (bf16[4,2,128,128]{3,2,1,0:T(8,128)(2,1)S(1)}, bf16[4,2,128,128]{3,2,1,0:T(8,128)(2,1)S(1)}, u32[]{:S(2)}, u32[]{:S(2)}) collective-permute-start(bf16[4,2,128,128]{3,2,1,0:T(8,128)(2,1)S(1)} %get-tuple-element.16), channel_id=1, source_target_pairs={{0,48},{16,0},{32,16},{48,32},{1,49},{17,1},{33,17},{49,33},{2,50}... | collective-permute-start | bytes 786440 | tf_op jit(solution)/shard_map/ppermute | solution.py:193
  39.6 11.2 %collective-permute-start.4 = (bf16[2,128,128]{2,1,0:T(8,128)(2,1)S(1)}, bf16[2,128,128]{2,1,0:T(8,128)(2,1)S(1)}, u32[]{:S(2)}, u32[]{:S(2)}) collective-permute-start(bf16[2,128,128]{2,1,0:T(8,128)(2,1)S(1)} %get-tuple-element.18), channel_id=1, source_target_pairs={{0,128},{64,192},{128,0},{192,64},{1,129},{65,193},{129,1},{193,65... | collective-permute-start | bytes 196616 | tf_op jit(solution)/shard_map/ppermute | solution.py:193
  46.0 6.4 %collective-permute-start.5 = (bf16[2,128,128]{2,1,0:T(8,128)(2,1)S(1)}, bf16[2,128,128]{2,1,0:T(8,128)(2,1)S(1)}, u32[]{:S(2)}, u32[]{:S(2)}) collective-permute-start(bf16[2,128,128]{2,1,0:T(8,128)(2,1)S(1)} %get-tuple-element.19), channel_id=1, source_target_pairs={{0,64},{64,128},{128,192},{192,0},{1,65},{65,129},{129,193},{193,1... | collective-permute-start | bytes 196616 | tf_op jit(solution)/shard_map/ppermute | solution.py:193
  47.5 5.3 %collective-permute-start.6 = (bf16[2,128,128]{2,1,0:T(8,128)(2,1)S(1)}, bf16[2,128,128]{2,1,0:T(8,128)(2,1)S(1)}, u32[]{:S(2)}, u32[]{:S(2)}) collective-permute-start(bf16[2,128,128]{2,1,0:T(8,128)(2,1)S(1)} %get-tuple-element.20), channel_id=1, source_target_pairs={{0,192},{64,0},{128,64},{192,128},{1,193},{65,1},{129,65},{193,129... | collective-permute-start | bytes 196616 | tf_op jit(solution)/shard_map/ppermute | solution.py:193

commit v5 on v4

--- a/solution.py
+++ b/solution.py
@@ -121,10 +121,11 @@
     here_y = lax.axis_index("y")
     core = lax.axis_index("core")
     cores = lax.axis_size("core")
-    for d, out in enumerate(outs):
-        size_z = out.shape[0]
-        for e in range(size_z):
-            chip = (here_z + e) % size_z * len(outs) + (here_y + d) % len(outs)
+    size_z = lax.axis_size("zh")
+    size_y = lax.axis_size("y")
+    for e in range(size_z):
+        for d in range(size_y):
+            chip = (here_z + e) % size_z * size_y + (here_y + d) % size_y
             slot = chip * cores + core
             r = pairs[slot, 0]
             s = pairs[slot, 1]
@@ -140,8 +141,9 @@
             a = jnp.concatenate([jnp.concatenate(upper, 1), jnp.concatenate(rotated, 1)], 0)
             b = jnp.concatenate(lower, 1)
             both = lax.dot_general(a, b, dims, preferred_element_type=jnp.float32)
-            out[e, 0] = both[:BLOCK].astype(out.dtype)
-            out[e, 1] = both[BLOCK:].astype(out.dtype)
+            out = outs[size_y + d].at[e - 1] if e else outs[d]
+            out[0] = both[:BLOCK].astype(out.dtype)
+            out[1] = both[BLOCK:].astype(out.dtype)
 
 
 def vmem():
@@ -151,38 +153,38 @@
 def partial_sums(pairs, own, sib):
     size_z = lax.axis_size("zh")
     size_y = lax.axis_size("y")
-    shape = (size_z, 2, BLOCK, BLOCK)
-    return pl.pallas_call(
+    shape = (2, BLOCK, BLOCK)
+    types = [jnp.bfloat16 if d else jnp.float32 for d in range(size_y)]
+    outs = pl.pallas_call(
         products_kernel,
-        out_shape=[
-            jax.ShapeDtypeStruct(shape, jnp.bfloat16 if d else jnp.float32) for d in range(size_y)
-        ],
+        out_shape=[jax.ShapeDtypeStruct(shape, dtype) for dtype in types]
+        + [jax.ShapeDtypeStruct((size_z - 1,) + shape, dtype) for dtype in types],
         in_specs=[pl.BlockSpec(memory_space=pltpu.SMEM), vmem(), vmem()],
-        out_specs=[vmem()] * size_y,
+        out_specs=[vmem()] * (2 * size_y),
         compiler_params=pltpu.CompilerParams(vmem_limit_bytes=8 << 20),
         name="products",
     )(pairs, own, sib)
+    return outs[:size_y], outs[size_y:]
 
 
 def stage_kernel(*refs):
-    parts = len(refs) // 2
-    for e in range(parts):
+    came = refs[0].shape[0]
+    for e in range(came):
         total = refs[0][e]
-        for ref in refs[1:parts]:
+        for ref in refs[1:-came]:
             total = total + ref[e].astype(jnp.float32)
-        refs[parts + e][...] = total.astype(refs[parts + e].dtype)
+        out = refs[e - came]
+        out[...] = total.astype(out.dtype)
 
 
 def stage_sums(arrays):
-    size_z = arrays[0].shape[0]
+    parts = arrays[0].shape[0]
     shape = arrays[0].shape[1:]
     return pl.pallas_call(
         stage_kernel,
-        out_shape=[
-            jax.ShapeDtypeStruct(shape, jnp.bfloat16 if e else jnp.float32) for e in range(size_z)
-        ],
+        out_shape=[jax.ShapeDtypeStruct(shape, jnp.bfloat16)] * parts,
         in_specs=[vmem()] * len(arrays),
-        out_specs=[vmem()] * size_z,
+        out_specs=[vmem()] * parts,
         compiler_params=pltpu.CompilerParams(vmem_limit_bytes=8 << 20),
         name="stage",
     )(*arrays)
@@ -205,10 +207,12 @@
     banded = lax.all_to_all(grouped, ("zl", "x"), split_axis=0, concat_axis=0, tiled=True)
     own = banded.reshape(-1, BLOCK, banded.shape[2])
     sib = shifted(own, "core", 1)
-    along_y = spread(partial_sums(block_pairs, own, sib), "y")
-    along_z = spread(stage_sums(along_y), "zh")
-    total = along_z[0]
-    for values in along_z[1:]:
+    staying, going = partial_sums(block_pairs, own, sib)
+    going = spread(going, "y")
+    staying = spread(staying, "y")
+    along_z = spread([None, *stage_sums(going)], "zh")
+    total = staying[0]
+    for values in staying[1:] + along_z[1:]:
         total = total + values.astype(jnp.float32)
     stack_scale = 1.0 / math.sqrt(windows * GROUP)
     slot = lax.axis_index(("zh", "y", "core"))

time: 54 us -> 52.4 us (0.970)
  waiting for transfers between devices: 15.1 us -> 9.24 us
  starting transfers between devices: 14.9 us -> 19.4 us
    ppermute x7 -> x10, waiting for transfers between devices: 15.1 us -> 9.24 us  [shifted(): lax.ppermute(values, axis, [(i, (i + offset) % size) for i in range(size)])]
    ppermute x7 -> x10, starting transfers between devices: 14.9 us -> 19.4 us  [shifted(): lax.ppermute(values, axis, [(i, (i + offset) % size) for i in range(size)])]
  transfers between devices with their start and end apart: 7 -> 10, of which waited for: 5 -> 5; matrix products, arithmetic and copies ran while one was open for 0% -> 0% of each run, Pallas kernels for 0% -> 0%
where the time goes in v5:
time: 52.4 us; the launch traced here: 52 us
  starting transfers between devices  19.4 us (37%)
  blocking collectives  15.5 us (30%)
  waiting for transfers between devices  9.24 us (18%)
  Pallas kernels  6.39 us (12%)
  other arithmetic  0.72 us (1%)
  between operations  0.71 us (1%)
    ppermute x10, starting transfers between devices, shifted(): lax.ppermute(values, axis, [(i, (i + offset) % size) for i in range(size)])  19.4 us
    all_to_all x1, blocking collectives, on_device(): lax.all_to_all(grouped, ('zl', 'x'), split_axis=0, concat_axis=0, tiled=T...  15.5 us
    ppermute x10, waiting for transfers between devices, shifted(): lax.ppermute(values, axis, [(i, (i + offset) % size) for i in range(size)])  9.24 us
    pallas_call x1, Pallas kernels, whitened_groups(): pl.pallas_call(spectra_kernel, out_shape=jax.ShapeDtypeStruct((groups, ch...  4.74 us
    pallas_call x1, Pallas kernels, partial_sums(): pl.pallas_call(products_kernel, out_shape=[jax.ShapeDtypeStruct(shape, dt...  1.56 us
  transfers between devices with their start and end apart: 10, of which 5 were waited for; matrix products, arithmetic and copies ran while one was open for 0% of the time, Pallas kernels for 0%

profile of v5, /device:TPU:8, one launch (start us, length us, event | category | flops | bytes accessed | tf_op | source)
XLA Modules:
  0.0 52.0 jit_solution(834658278957912814)
XLA Ops:
  0.0 0.0 copy-start
  0.0 4.7 %spectra.1 = bf16[8,256,128]{2,1,0:T(8,128)(2,1)S(1)} custom-call(bf16[2,256,4096]{2,1,0:T(8,128)(2,1)} %traces.1, bf16[1024,512]{1,0:T(8,128)(2,1)} %constant.25.clone.table), custom_call_target="tpu_custom_call" | custom-call | tf_op jit(solution)/shard_map/spectra/pallas_call | solution.py:101
  4.8 15.5 %all_to_all.5 = bf16[8,256,128]{2,1,0:T(8,128)(2,1)S(1)} all-to-all(bf16[8,256,128]{2,1,0:T(8,128)(2,1)S(1)} %spectra.1), channel_id=1, replica_groups=mesh['zh'=4,'y'=4,'core'=2,'zl'=2,'x'=4] {'zl','x'}, dimensions={0} | all-to-all | bytes 1048576 | tf_op jit(solution)/shard_map/all_to_all | solution.py:207
  20.3 0.0 collective-permute-start
  20.3 0.0 copy-done
  20.3 0.1 copy.5.pairs
  20.4 1.8 %collective-permute-done.sib = bf16[16,128,128]{2,1,0:T(8,128)(2,1)S(1)} collective-permute-done((bf16[16,128,128]{2,1,0:T(8,128)(2,1)S(1)}, bf16[16,128,128]{2,1,0:T(8,128)(2,1)S(1)}, u32[]{:S(2)}, u32[]{:S(2)}) %collective-permute-start) | collective-permute-done | bytes 524320 | tf_op jit(solution)/shard_map/ppermute | solution.py:195
  22.2 1.6 %products.1 = (f32[2,128,128]{2,1,0:T(8,128)S(1)}, bf16[2,128,128]{2,1,0:T(8,128)(2,1)S(1)}, bf16[2,128,128]{2,1,0:T(8,128)(2,1)S(1)}, bf16[2,128,128]{2,1,0:T(8...) custom-call(s32[32,2]{1,0:T(8,128)S(1)} %copy.5.pairs, ...), custom_call_target="tpu_custom_call" | custom-call | tf_op jit(solution)/shard_map/products/pallas_call | solution.py:158
  23.8 2.4 %collective-permute-start.4 = (bf16[3,2,128,128]{3,2,1,0:T(8,128)(2,1)S(1)}, bf16[3,2,128,128]{3,2,1,0:T(8,128)(2,1)S(1)}, u32[]{:S(2)}, u32[]{:S(2)}) collective-permute-start(bf16[3,2,128,128]{3,2,1,0:T(8,128)(2,1)S(1)} %get-tuple-element.21), channel_id=1, source_target_pairs={{0,32},{16,48},{32,0},{48,16},{1,33},{17,49},{33,1},{49,17},{2,34}... | collective-permute-start | bytes 589832 | tf_op jit(solution)/shard_map/ppermute | solution.py:195
  26.1 0.0 collective-permute-start.5
  26.1 2.0 %collective-permute-start.6 = (bf16[3,2,128,128]{3,2,1,0:T(8,128)(2,1)S(1)}, bf16[3,2,128,128]{3,2,1,0:T(8,128)(2,1)S(1)}, u32[]{:S(2)}, u32[]{:S(2)}) collective-permute-start(bf16[3,2,128,128]{3,2,1,0:T(8,128)(2,1)S(1)} %get-tuple-element.23), channel_id=1, source_target_pairs={{0,48},{16,0},{32,16},{48,32},{1,49},{17,1},{33,17},{49,33},{2,50}... | collective-permute-start | bytes 589832 | tf_op jit(solution)/shard_map/ppermute | solution.py:195
  28.2 1.4 %collective-permute-start.1 = (bf16[2,128,128]{2,1,0:T(8,128)(2,1)S(1)}, bf16[2,128,128]{2,1,0:T(8,128)(2,1)S(1)}, u32[]{:S(2)}, u32[]{:S(2)}) collective-permute-start(bf16[2,128,128]{2,1,0:T(8,128)(2,1)S(1)} %get-tuple-element.17), channel_id=1, source_target_pairs={{0,32},{16,48},{32,0},{48,16},{1,33},{17,49},{33,1},{49,17},{2,34}... | collective-permute-start | bytes 196616 | tf_op jit(solution)/shard_map/ppermute | solution.py:195
  29.6 2.6 %collective-permute-start.2 = (bf16[2,128,128]{2,1,0:T(8,128)(2,1)S(1)}, bf16[2,128,128]{2,1,0:T(8,128)(2,1)S(1)}, u32[]{:S(2)}, u32[]{:S(2)}) collective-permute-start(bf16[2,128,128]{2,1,0:T(8,128)(2,1)S(1)} %get-tuple-element.18), channel_id=1, source_target_pairs={{0,16},{16,32},{32,48},{48,0},{1,17},{17,33},{33,49},{49,1},{2,18}... | collective-permute-start | bytes 196616 | tf_op jit(solution)/shard_map/ppermute | solution.py:195
  32.2 0.9 %collective-permute-done.4.refs_1_ = bf16[3,2,128,128]{3,2,1,0:T(8,128)(2,1)S(1)} collective-permute-done((bf16[3,2,128,128]{3,2,1,0:T(8,128)(2,1)S(1)}, bf16[3,2,128,128]{3,2,1,0:T(8,128)(2,1)S(1)}, u32[]{:S(2)}, u32[]{:S(2)}) %collective-permute-start.4) | collective-permute-done | bytes 196640 | tf_op jit(solution)/shard_map/ppermute | solution.py:195
  33.1 0.4 collective-permute-start.3
  33.6 3.9 %collective-permute-done.5.refs_2_ = bf16[3,2,128,128]{3,2,1,0:T(8,128)(2,1)S(1)} collective-permute-done((bf16[3,2,128,128]{3,2,1,0:T(8,128)(2,1)S(1)}, bf16[3,2,128,128]{3,2,1,0:T(8,128)(2,1)S(1)}, u32[]{:S(2)}, u32[]{:S(2)}) %collective-permute-start.5) | collective-permute-done | bytes 196640 | tf_op jit(solution)/shard_map/ppermute | solution.py:195
  37.5 0.0 collective-permute-done.6.refs_3_
  37.5 0.1 stage.1
  37.6 6.4 %collective-permute-start.7 = (bf16[2,128,128]{2,1,0:T(8,128)(2,1)S(1)}, bf16[2,128,128]{2,1,0:T(8,128)(2,1)S(1)}, u32[]{:S(2)}, u32[]{:S(2)}) collective-permute-start(bf16[2,128,128]{2,1,0:T(8,128)(2,1)S(1)} %get-tuple-element.24), channel_id=1, source_target_pairs={{0,128},{64,192},{128,0},{192,64},{1,129},{65,193},{129,1},{193,65... | collective-permute-start | bytes 196616 | tf_op jit(solution)/shard_map/ppermute | solution.py:195
  43.9 1.5 %collective-permute-start.8 = (bf16[2,128,128]{2,1,0:T(8,128)(2,1)S(1)}, bf16[2,128,128]{2,1,0:T(8,128)(2,1)S(1)}, u32[]{:S(2)}, u32[]{:S(2)}) collective-permute-start(bf16[2,128,128]{2,1,0:T(8,128)(2,1)S(1)} %get-tuple-element.25), channel_id=1, source_target_pairs={{0,64},{64,128},{128,192},{192,0},{1,65},{65,129},{129,193},{193,1... | collective-permute-start | bytes 196616 | tf_op jit(solution)/shard_map/ppermute | solution.py:195
  45.4 0.0 collective-permute-done.1
  45.4 2.7 %collective-permute-start.9 = (bf16[2,128,128]{2,1,0:T(8,128)(2,1)S(1)}, bf16[2,128,128]{2,1,0:T(8,128)(2,1)S(1)}, u32[]{:S(2)}, u32[]{:S(2)}) collective-permute-start(bf16[2,128,128]{2,1,0:T(8,128)(2,1)S(1)} %get-tuple-element.26), channel_id=1, source_target_pairs={{0,192},{64,0},{128,64},{192,128},{1,193},{65,1},{129,65},{193,129... | collective-permute-start | bytes 196616 | tf_op jit(solution)/shard_map/ppermute | solution.py:195
  48.7 0.0 collective-permute-done.2
  48.8 0.0 collective-permute-done.3
  48.8 0.0 collective-permute-done.7
  48.8 1.5 %collective-permute-done.8 = bf16[2,128,128]{2,1,0:T(8,128)(2,1)S(1)} collective-permute-done((bf16[2,128,128]{2,1,0:T(8,128)(2,1)S(1)}, bf16[2,128,128]{2,1,0:T(8,128)(2,1)S(1)}, u32[]{:S(2)}, u32[]{:S(2)}) %collective-permute-start.8) | collective-permute-done | bytes 65568 | tf_op jit(solution)/shard_map/ppermute | solution.py:195
  50.3 1.0 %collective-permute-done.9 = bf16[2,128,128]{2,1,0:T(8,128)(2,1)S(1)} collective-permute-done((bf16[2,128,128]{2,1,0:T(8,128)(2,1)S(1)}, bf16[2,128,128]{2,1,0:T(8,128)(2,1)S(1)}, u32[]{:S(2)}, u32[]{:S(2)}) %collective-permute-start.9) | collective-permute-done | bytes 65568 | tf_op jit(solution)/shard_map/ppermute | solution.py:195
  51.3 0.7 %multiply_bitcast_fusion = f32[1,1,2,128,128]{4,3,2,1,0:T(8,128)} fusion(bf16[2,128,128]{2,1,0:T(8,128)(2,1)S(1)} %collective-permute-done.9, bf16[2,128,128]{2,1,0:T(8,128)(2,1)S(1)} %collective-permute-done.8, bf16[2,128,128]{2,1,0:T(8,128)(2,1)S(1)} %collective-permute-done.7, bf16[2,128,128]{2,1,0:T(8,128)(2,1)S(1)} %collective-permute-done.3, ...), kind=kLoop, calls=%fused_computation | loop fusion | flops 425984 | bytes 655364 | tf_op jit(solution)/shard_map/broadcast_in_dim | solution.py:220
Async XLA Ops:
  0.0 20.3 %copy-start = (s32[32,2]{0,1:T(2,128)S(1)}, s32[32,2]{0,1:T(2,128)}, u32[]{:S(2)}) copy-start(s32[32,2]{0,1:T(2,128)} %param.5) | copy-start | bytes 772
  20.3 1.9 %collective-permute-start = (bf16[16,128,128]{2,1,0:T(8,128)(2,1)S(1)}, bf16[16,128,128]{2,1,0:T(8,128)(2,1)S(1)}, u32[]{:S(2)}, u32[]{:S(2)}) collective-permute-start(bf16[16,128,128]{2,1,0:T(8,128)(2,1)S(1)} %bitcast.5), channel_id=1, source_target_pairs={{0,8},{8,0},{1,9},{9,1},{2,10},{10,2},{3,11},{11,3},{4,12},{12,4},... | collective-permute-start | bytes 1572872 | tf_op jit(solution)/shard_map/ppermute | solution.py:195
  23.8 9.4 %collective-permute-start.4 = (bf16[3,2,128,128]{3,2,1,0:T(8,128)(2,1)S(1)}, bf16[3,2,128,128]{3,2,1,0:T(8,128)(2,1)S(1)}, u32[]{:S(2)}, u32[]{:S(2)}) collective-permute-start(bf16[3,2,128,128]{3,2,1,0:T(8,128)(2,1)S(1)} %get-tuple-element.21), channel_id=1, source_target_pairs={{0,32},{16,48},{32,0},{48,16},{1,33},{17,49},{33,1},{49,17},{2,34}... | collective-permute-start | bytes 589832 | tf_op jit(solution)/shard_map/ppermute | solution.py:195
  26.1 11.3 %collective-permute-start.5 = (bf16[3,2,128,128]{3,2,1,0:T(8,128)(2,1)S(1)}, bf16[3,2,128,128]{3,2,1,0:T(8,128)(2,1)S(1)}, u32[]{:S(2)}, u32[]{:S(2)}) collective-permute-start(bf16[3,2,128,128]{3,2,1,0:T(8,128)(2,1)S(1)} %get-tuple-element.22), channel_id=1, source_target_pairs={{0,16},{16,32},{32,48},{48,0},{1,17},{17,33},{33,49},{49,1},{2,18}... | collective-permute-start | bytes 589832 | tf_op jit(solution)/shard_map/ppermute | solution.py:195
  26.1 11.3 %collective-permute-start.6 = (bf16[3,2,128,128]{3,2,1,0:T(8,128)(2,1)S(1)}, bf16[3,2,128,128]{3,2,1,0:T(8,128)(2,1)S(1)}, u32[]{:S(2)}, u32[]{:S(2)}) collective-permute-start(bf16[3,2,128,128]{3,2,1,0:T(8,128)(2,1)S(1)} %get-tuple-element.23), channel_id=1, source_target_pairs={{0,48},{16,0},{32,16},{48,32},{1,49},{17,1},{33,17},{49,33},{2,50}... | collective-permute-start | bytes 589832 | tf_op jit(solution)/shard_map/ppermute | solution.py:195
  28.2 17.3 %collective-permute-start.1 = (bf16[2,128,128]{2,1,0:T(8,128)(2,1)S(1)}, bf16[2,128,128]{2,1,0:T(8,128)(2,1)S(1)}, u32[]{:S(2)}, u32[]{:S(2)}) collective-permute-start(bf16[2,128,128]{2,1,0:T(8,128)(2,1)S(1)} %get-tuple-element.17), channel_id=1, source_target_pairs={{0,32},{16,48},{32,0},{48,16},{1,33},{17,49},{33,1},{49,17},{2,34}... | collective-permute-start | bytes 196616 | tf_op jit(solution)/shard_map/ppermute | solution.py:195
  29.6 19.2 %collective-permute-start.2 = (bf16[2,128,128]{2,1,0:T(8,128)(2,1)S(1)}, bf16[2,128,128]{2,1,0:T(8,128)(2,1)S(1)}, u32[]{:S(2)}, u32[]{:S(2)}) collective-permute-start(bf16[2,128,128]{2,1,0:T(8,128)(2,1)S(1)} %get-tuple-element.18), channel_id=1, source_target_pairs={{0,16},{16,32},{32,48},{48,0},{1,17},{17,33},{33,49},{49,1},{2,18}... | collective-permute-start | bytes 196616 | tf_op jit(solution)/shard_map/ppermute | solution.py:195
  33.1 15.6 %collective-permute-start.3 = (bf16[2,128,128]{2,1,0:T(8,128)(2,1)S(1)}, bf16[2,128,128]{2,1,0:T(8,128)(2,1)S(1)}, u32[]{:S(2)}, u32[]{:S(2)}) collective-permute-start(bf16[2,128,128]{2,1,0:T(8,128)(2,1)S(1)} %get-tuple-element.19), channel_id=1, source_target_pairs={{0,48},{16,0},{32,16},{48,32},{1,49},{17,1},{33,17},{49,33},{2,50}... | collective-permute-start | bytes 196616 | tf_op jit(solution)/shard_map/ppermute | solution.py:195
  37.6 11.2 %collective-permute-start.7 = (bf16[2,128,128]{2,1,0:T(8,128)(2,1)S(1)}, bf16[2,128,128]{2,1,0:T(8,128)(2,1)S(1)}, u32[]{:S(2)}, u32[]{:S(2)}) collective-permute-start(bf16[2,128,128]{2,1,0:T(8,128)(2,1)S(1)} %get-tuple-element.24), channel_id=1, source_target_pairs={{0,128},{64,192},{128,0},{192,64},{1,129},{65,193},{129,1},{193,65... | collective-permute-start | bytes 196616 | tf_op jit(solution)/shard_map/ppermute | solution.py:195
  43.9 6.4 %collective-permute-start.8 = (bf16[2,128,128]{2,1,0:T(8,128)(2,1)S(1)}, bf16[2,128,128]{2,1,0:T(8,128)(2,1)S(1)}, u32[]{:S(2)}, u32[]{:S(2)}) collective-permute-start(bf16[2,128,128]{2,1,0:T(8,128)(2,1)S(1)} %get-tuple-element.25), channel_id=1, source_target_pairs={{0,64},{64,128},{128,192},{192,0},{1,65},{65,129},{129,193},{193,1... | collective-permute-start | bytes 196616 | tf_op jit(solution)/shard_map/ppermute | solution.py:195
  45.4 5.9 %collective-permute-start.9 = (bf16[2,128,128]{2,1,0:T(8,128)(2,1)S(1)}, bf16[2,128,128]{2,1,0:T(8,128)(2,1)S(1)}, u32[]{:S(2)}, u32[]{:S(2)}) collective-permute-start(bf16[2,128,128]{2,1,0:T(8,128)(2,1)S(1)} %get-tuple-element.26), channel_id=1, source_target_pairs={{0,192},{64,0},{128,64},{192,128},{1,193},{65,1},{129,65},{193,129... | collective-permute-start | bytes 196616 | tf_op jit(solution)/shard_map/ppermute | solution.py:195

commit v6 on v5

--- a/solution.py
+++ b/solution.py
@@ -1,3 +1,4 @@
+import functools
 import math
 
 import jax
@@ -15,6 +16,7 @@
 EPS = 1e-06
 QUARTERS = 4
 ROWS = 32
+Z_GROUPS = ((2, 1), (3, 0))
 
 
 def packed_table(length):
@@ -113,7 +115,7 @@
     )(in_hbm(traces), in_hbm(table))
 
 
-def products_kernel(pairs, own, sib, *outs):
+def products_kernel(groups, pairs, own, sib, *outs):
     lanes = lax.broadcasted_iota(jnp.int32, (BLOCK, 128), 1)
     is_re = lanes < 64
     dims = (((1,), (1,)), ((), ()))
@@ -123,9 +125,9 @@
     cores = lax.axis_size("core")
     size_z = lax.axis_size("zh")
     size_y = lax.axis_size("y")
-    for e in range(size_z):
-        for d in range(size_y):
-            chip = (here_z + e) % size_z * size_y + (here_y + d) % size_y
+    for n, out in enumerate(outs):
+        for i, e in enumerate(groups[n // size_y]):
+            chip = (here_z + e) % size_z * size_y + (here_y + n % size_y) % size_y
             slot = chip * cores + core
             r = pairs[slot, 0]
             s = pairs[slot, 1]
@@ -141,48 +143,49 @@
             a = jnp.concatenate([jnp.concatenate(upper, 1), jnp.concatenate(rotated, 1)], 0)
             b = jnp.concatenate(lower, 1)
             both = lax.dot_general(a, b, dims, preferred_element_type=jnp.float32)
-            out = outs[size_y + d].at[e - 1] if e else outs[d]
-            out[0] = both[:BLOCK].astype(out.dtype)
-            out[1] = both[BLOCK:].astype(out.dtype)
+            out[i, 0] = both[:BLOCK].astype(out.dtype)
+            out[i, 1] = both[BLOCK:].astype(out.dtype)
 
 
 def vmem():
     return pl.BlockSpec(memory_space=pltpu.VMEM)
 
 
-def partial_sums(pairs, own, sib):
-    size_z = lax.axis_size("zh")
+def partial_sums(groups, pairs, own, sib):
     size_y = lax.axis_size("y")
-    shape = (2, BLOCK, BLOCK)
-    types = [jnp.bfloat16 if d else jnp.float32 for d in range(size_y)]
     outs = pl.pallas_call(
-        products_kernel,
-        out_shape=[jax.ShapeDtypeStruct(shape, dtype) for dtype in types]
-        + [jax.ShapeDtypeStruct((size_z - 1,) + shape, dtype) for dtype in types],
+        functools.partial(products_kernel, groups),
+        out_shape=[
+            jax.ShapeDtypeStruct(
+                (len(group), 2, BLOCK, BLOCK), jnp.bfloat16 if d else jnp.float32
+            )
+            for group in groups
+            for d in range(size_y)
+        ],
         in_specs=[pl.BlockSpec(memory_space=pltpu.SMEM), vmem(), vmem()],
-        out_specs=[vmem()] * (2 * size_y),
+        out_specs=[vmem()] * (len(groups) * size_y),
         compiler_params=pltpu.CompilerParams(vmem_limit_bytes=8 << 20),
         name="products",
     )(pairs, own, sib)
-    return outs[:size_y], outs[size_y:]
+    return [outs[g * size_y : (g + 1) * size_y] for g in range(len(groups))]
 
 
 def stage_kernel(*refs):
     came = refs[0].shape[0]
-    for e in range(came):
-        total = refs[0][e]
+    for i in range(came):
+        total = refs[0][i]
         for ref in refs[1:-came]:
-            total = total + ref[e].astype(jnp.float32)
-        out = refs[e - came]
+            total = total + ref[i].astype(jnp.float32)
+        out = refs[i - came]
         out[...] = total.astype(out.dtype)
 
 
-def stage_sums(arrays):
-    parts = arrays[0].shape[0]
+def stage_sums(group, arrays):
+    parts = len(group)
     shape = arrays[0].shape[1:]
     return pl.pallas_call(
         stage_kernel,
-        out_shape=[jax.ShapeDtypeStruct(shape, jnp.bfloat16)] * parts,
+        out_shape=[jax.ShapeDtypeStruct(shape, jnp.bfloat16 if e else jnp.float32) for e in group],
         in_specs=[vmem()] * len(arrays),
         out_specs=[vmem()] * parts,
         compiler_params=pltpu.CompilerParams(vmem_limit_bytes=8 << 20),
@@ -195,9 +198,13 @@
     return lax.ppermute(values, axis, [(i, (i + offset) % size) for i in range(size)])
 
 
+def far_first(size):
+    ways = [min(d, size - d) for d in range(size)]
+    return [[d for d in range(size) if ways[d] == way] for way in sorted(set(ways), reverse=True)]
+
+
 def spread(arrays, axis):
-    size = len(arrays)
-    order = sorted(range(1, size), key=lambda d: -min(d, size - d))
+    order = [d for group in far_first(len(arrays)) for d in group if d]
     return [arrays[0]] + [shifted(arrays[d], axis, d) for d in order]
 
 
@@ -207,12 +214,13 @@
     banded = lax.all_to_all(grouped, ("zl", "x"), split_axis=0, concat_axis=0, tiled=True)
     own = banded.reshape(-1, BLOCK, banded.shape[2])
     sib = shifted(own, "core", 1)
-    staying, going = partial_sums(block_pairs, own, sib)
-    going = spread(going, "y")
-    staying = spread(staying, "y")
-    along_z = spread([None, *stage_sums(going)], "zh")
-    total = staying[0]
-    for values in staying[1:] + along_z[1:]:
+    parts = []
+    for group, arrays in zip(Z_GROUPS, partial_sums(Z_GROUPS, block_pairs, own, sib)):
+        along_y = spread(arrays, "y")
+        staged = stage_sums(group, along_y)
+        parts += [shifted(values, "zh", e) if e else values for e, values in zip(group, staged)]
+    total = parts[0].astype(jnp.float32)
+    for values in parts[1:]:
         total = total + values.astype(jnp.float32)
     stack_scale = 1.0 / math.sqrt(windows * GROUP)
     slot = lax.axis_index(("zh", "y", "core"))

time: 52.4 us -> 52 us (level)
  the two profiles are of different devices: /device:TPU:8 before, /device:TPU:24 now
where the time goes in v6:
time: 52 us; the launch traced here: 51.9 us
  starting transfers between devices  18.1 us (35%)
  blocking collectives  15.5 us (30%)
  waiting for transfers between devices  10.3 us (20%)
  Pallas kernels  6.43 us (12%)
  between operations  0.71 us (1%)
  other arithmetic  0.69 us (1%)
    ppermute x10, starting transfers between devices, shifted(): lax.ppermute(values, axis, [(i, (i + offset) % size) for i in range(size)])  18.1 us
    all_to_all x1, blocking collectives, on_device(): lax.all_to_all(grouped, ('zl', 'x'), split_axis=0, concat_axis=0, tiled=T...  15.5 us
    ppermute x10, waiting for transfers between devices, shifted(): lax.ppermute(values, axis, [(i, (i + offset) % size) for i in range(size)])  10.3 us
    pallas_call x1, Pallas kernels, whitened_groups(): pl.pallas_call(spectra_kernel, out_shape=jax.ShapeDtypeStruct((groups, ch...  4.75 us
    pallas_call x1, Pallas kernels, partial_sums(): pl.pallas_call(functools.partial(products_kernel, groups), out_shape=[jax...  1.56 us
  transfers between devices with their start and end apart: 10, of which 6 were waited for; matrix products, arithmetic and copies ran while one was open for 0% of the time, Pallas kernels for 0%

profile of v6, /device:TPU:24, one launch (start us, length us, event | category | flops | bytes accessed | tf_op | source)
XLA Modules:
  0.0 51.9 jit_solution(15827919289074311477)
XLA Ops:
  0.0 0.0 copy-start
  0.0 4.7 %spectra.1 = bf16[8,256,128]{2,1,0:T(8,128)(2,1)S(1)} custom-call(bf16[2,256,4096]{2,1,0:T(8,128)(2,1)} %traces.1, bf16[1024,512]{1,0:T(8,128)(2,1)} %constant.25.clone.table), custom_call_target="tpu_custom_call" | custom-call | tf_op jit(solution)/shard_map/spectra/pallas_call | solution.py:103
  4.8 15.5 %all_to_all.5 = bf16[8,256,128]{2,1,0:T(8,128)(2,1)S(1)} all-to-all(bf16[8,256,128]{2,1,0:T(8,128)(2,1)S(1)} %spectra.1), channel_id=1, replica_groups=mesh['zh'=4,'y'=4,'core'=2,'zl'=2,'x'=4] {'zl','x'}, dimensions={0} | all-to-all | bytes 1048576 | tf_op jit(solution)/shard_map/all_to_all | solution.py:214
  20.3 0.0 collective-permute-start
  20.3 0.0 copy-done
  20.3 0.1 copy.5.pairs
  20.4 1.8 %collective-permute-done.sib = bf16[16,128,128]{2,1,0:T(8,128)(2,1)S(1)} collective-permute-done((bf16[16,128,128]{2,1,0:T(8,128)(2,1)S(1)}, bf16[16,128,128]{2,1,0:T(8,128)(2,1)S(1)}, u32[]{:S(2)}, u32[]{:S(2)}) %collective-permute-start) | collective-permute-done | bytes 524320 | tf_op jit(solution)/shard_map/ppermute | solution.py:198
  22.2 1.6 %products.1 = (f32[2,2,128,128]{3,2,1,0:T(8,128)S(1)}, bf16[2,2,128,128]{3,2,1,0:T(8,128)(2,1)S(1)}, bf16[2,2,128,128]{3,2,1,0:T(8,128)(2,1)S(1)}, bf16[2,2,128,...) custom-call(s32[32,2]{1,0:T(8,128)S(1)} %copy.5.pairs, ...), custom_call_target="tpu_custom_call" | custom-call | tf_op jit(solution)/shard_map/products/pallas_call | solution.py:156
  23.8 1.3 %collective-permute-start.1 = (bf16[2,2,128,128]{3,2,1,0:T(8,128)(2,1)S(1)}, bf16[2,2,128,128]{3,2,1,0:T(8,128)(2,1)S(1)}, u32[]{:S(2)}, u32[]{:S(2)}) collective-permute-start(bf16[2,2,128,128]{3,2,1,0:T(8,128)(2,1)S(1)} %get-tuple-element.18), channel_id=1, source_target_pairs={{0,32},{16,48},{32,0},{48,16},{1,33},{17,49},{33,1},{49,17},{2,34}... | collective-permute-start | bytes 393224 | tf_op jit(solution)/shard_map/ppermute | solution.py:198
  25.1 2.2 %collective-permute-start.2 = (bf16[2,2,128,128]{3,2,1,0:T(8,128)(2,1)S(1)}, bf16[2,2,128,128]{3,2,1,0:T(8,128)(2,1)S(1)}, u32[]{:S(2)}, u32[]{:S(2)}) collective-permute-start(bf16[2,2,128,128]{3,2,1,0:T(8,128)(2,1)S(1)} %get-tuple-element.19), channel_id=1, source_target_pairs={{0,16},{16,32},{32,48},{48,0},{1,17},{17,33},{33,49},{49,1},{2,18}... | collective-permute-start | bytes 393224 | tf_op jit(solution)/shard_map/ppermute | solution.py:198
  27.3 0.0 collective-permute-start.3
  27.3 2.1 %collective-permute-start.6 = (bf16[2,2,128,128]{3,2,1,0:T(8,128)(2,1)S(1)}, bf16[2,2,128,128]{3,2,1,0:T(8,128)(2,1)S(1)}, u32[]{:S(2)}, u32[]{:S(2)}) collective-permute-start(bf16[2,2,128,128]{3,2,1,0:T(8,128)(2,1)S(1)} %get-tuple-element.24), channel_id=1, source_target_pairs={{0,32},{16,48},{32,0},{48,16},{1,33},{17,49},{33,1},{49,17},{2,34}... | collective-permute-start | bytes 393224 | tf_op jit(solution)/shard_map/ppermute | solution.py:198
  29.4 1.1 %collective-permute-start.7 = (bf16[2,2,128,128]{3,2,1,0:T(8,128)(2,1)S(1)}, bf16[2,2,128,128]{3,2,1,0:T(8,128)(2,1)S(1)}, u32[]{:S(2)}, u32[]{:S(2)}) collective-permute-start(bf16[2,2,128,128]{3,2,1,0:T(8,128)(2,1)S(1)} %get-tuple-element.25), channel_id=1, source_target_pairs={{0,16},{16,32},{32,48},{48,0},{1,17},{17,33},{33,49},{49,1},{2,18}... | collective-permute-start | bytes 393224 | tf_op jit(solution)/shard_map/ppermute | solution.py:198
  30.5 1.2 %collective-permute-done.1.refs_1_ = bf16[2,2,128,128]{3,2,1,0:T(8,128)(2,1)S(1)} collective-permute-done((bf16[2,2,128,128]{3,2,1,0:T(8,128)(2,1)S(1)}, bf16[2,2,128,128]{3,2,1,0:T(8,128)(2,1)S(1)}, u32[]{:S(2)}, u32[]{:S(2)}) %collective-permute-start.1) | collective-permute-done | bytes 131104 | tf_op jit(solution)/shard_map/ppermute | solution.py:198
  31.7 0.8 %collective-permute-start.8 = (bf16[2,2,128,128]{3,2,1,0:T(8,128)(2,1)S(1)}, bf16[2,2,128,128]{3,2,1,0:T(8,128)(2,1)S(1)}, u32[]{:S(2)}, u32[]{:S(2)}) collective-permute-start(bf16[2,2,128,128]{3,2,1,0:T(8,128)(2,1)S(1)} %get-tuple-element.26), channel_id=1, source_target_pairs={{0,48},{16,0},{32,16},{48,32},{1,49},{17,1},{33,17},{49,33},{2,50}... | collective-permute-start | bytes 393224 | tf_op jit(solution)/shard_map/ppermute | solution.py:198
  32.5 0.1 collective-permute-done.2.refs_2_
  32.6 4.6 %collective-permute-done.3.refs_3_ = bf16[2,2,128,128]{3,2,1,0:T(8,128)(2,1)S(1)} collective-permute-done((bf16[2,2,128,128]{3,2,1,0:T(8,128)(2,1)S(1)}, bf16[2,2,128,128]{3,2,1,0:T(8,128)(2,1)S(1)}, u32[]{:S(2)}, u32[]{:S(2)}) %collective-permute-start.3) | collective-permute-done | bytes 131104 | tf_op jit(solution)/shard_map/ppermute | solution.py:198
  37.2 0.1 stage.2
  37.2 6.4 %collective-permute-start.4 = (bf16[2,128,128]{2,1,0:T(8,128)(2,1)S(1)}, bf16[2,128,128]{2,1,0:T(8,128)(2,1)S(1)}, u32[]{:S(2)}, u32[]{:S(2)}) collective-permute-start(bf16[2,128,128]{2,1,0:T(8,128)(2,1)S(1)} %get-tuple-element.21), channel_id=1, source_target_pairs={{0,128},{64,192},{128,0},{192,64},{1,129},{65,193},{129,1},{193,65... | collective-permute-start | bytes 196616 | tf_op jit(solution)/shard_map/ppermute | solution.py:198
  43.6 1.4 %collective-permute-start.5 = (bf16[2,128,128]{2,1,0:T(8,128)(2,1)S(1)}, bf16[2,128,128]{2,1,0:T(8,128)(2,1)S(1)}, u32[]{:S(2)}, u32[]{:S(2)}) collective-permute-start(bf16[2,128,128]{2,1,0:T(8,128)(2,1)S(1)} %get-tuple-element.22), channel_id=1, source_target_pairs={{0,64},{64,128},{128,192},{192,0},{1,65},{65,129},{129,193},{193,1... | collective-permute-start | bytes 196616 | tf_op jit(solution)/shard_map/ppermute | solution.py:198
  45.0 0.0 collective-permute-done.6.refs_1_
  45.0 0.0 collective-permute-done.7.refs_2_
  45.1 0.0 collective-permute-done.8.refs_3_
  45.1 0.1 stage.3
  45.1 2.8 %collective-permute-start.9 = (bf16[2,128,128]{2,1,0:T(8,128)(2,1)S(1)}, bf16[2,128,128]{2,1,0:T(8,128)(2,1)S(1)}, u32[]{:S(2)}, u32[]{:S(2)}) collective-permute-start(bf16[2,128,128]{2,1,0:T(8,128)(2,1)S(1)} %get-tuple-element.27), channel_id=1, source_target_pairs={{0,192},{64,0},{128,64},{192,128},{1,193},{65,1},{129,65},{193,129... | collective-permute-start | bytes 196616 | tf_op jit(solution)/shard_map/ppermute | solution.py:198
  48.6 0.0 collective-permute-done.4
  48.6 1.4 %collective-permute-done.5 = bf16[2,128,128]{2,1,0:T(8,128)(2,1)S(1)} collective-permute-done((bf16[2,128,128]{2,1,0:T(8,128)(2,1)S(1)}, bf16[2,128,128]{2,1,0:T(8,128)(2,1)S(1)}, u32[]{:S(2)}, u32[]{:S(2)}) %collective-permute-start.5) | collective-permute-done | bytes 65568 | tf_op jit(solution)/shard_map/ppermute | solution.py:198
  50.0 1.2 %collective-permute-done.9 = bf16[2,128,128]{2,1,0:T(8,128)(2,1)S(1)} collective-permute-done((bf16[2,128,128]{2,1,0:T(8,128)(2,1)S(1)}, bf16[2,128,128]{2,1,0:T(8,128)(2,1)S(1)}, u32[]{:S(2)}, u32[]{:S(2)}) %collective-permute-start.9) | collective-permute-done | bytes 65568 | tf_op jit(solution)/shard_map/ppermute | solution.py:198
  51.2 0.7 %multiply_bitcast_fusion = f32[1,1,2,128,128]{4,3,2,1,0:T(8,128)} fusion(f32[2,128,128]{2,1,0:T(8,128)S(1)} %get-tuple-element.28, bf16[2,128,128]{2,1,0:T(8,128)(2,1)S(1)} %collective-permute-done.9, bf16[2,128,128]{2,1,0:T(8,128)(2,1)S(1)} %collective-permute-done.5, bf16[2,128,128]{2,1,0:T(8,128)(2,1)S(1)} %collective-permute-done.4, f32[]{:T(128)S(6)} %mul_shard_map.3), kind=kLoop, calls=%fused_computation | loop fusion | flops 229376 | bytes 458756 | tf_op jit(solution)/shard_map/broadcast_in_dim | solution.py:228
Async XLA Ops:
  0.0 20.3 %copy-start = (s32[32,2]{0,1:T(2,128)S(1)}, s32[32,2]{0,1:T(2,128)}, u32[]{:S(2)}) copy-start(s32[32,2]{0,1:T(2,128)} %param.5) | copy-start | bytes 772
  20.3 1.9 %collective-permute-start = (bf16[16,128,128]{2,1,0:T(8,128)(2,1)S(1)}, bf16[16,128,128]{2,1,0:T(8,128)(2,1)S(1)}, u32[]{:S(2)}, u32[]{:S(2)}) collective-permute-start(bf16[16,128,128]{2,1,0:T(8,128)(2,1)S(1)} %bitcast.5), channel_id=1, source_target_pairs={{0,8},{8,0},{1,9},{9,1},{2,10},{10,2},{3,11},{11,3},{4,12},{12,4},... | collective-permute-start | bytes 1572872 | tf_op jit(solution)/shard_map/ppermute | solution.py:198
  23.8 7.9 %collective-permute-start.1 = (bf16[2,2,128,128]{3,2,1,0:T(8,128)(2,1)S(1)}, bf16[2,2,128,128]{3,2,1,0:T(8,128)(2,1)S(1)}, u32[]{:S(2)}, u32[]{:S(2)}) collective-permute-start(bf16[2,2,128,128]{3,2,1,0:T(8,128)(2,1)S(1)} %get-tuple-element.18), channel_id=1, source_target_pairs={{0,32},{16,48},{32,0},{48,16},{1,33},{17,49},{33,1},{49,17},{2,34}... | collective-permute-start | bytes 393224 | tf_op jit(solution)/shard_map/ppermute | solution.py:198
  25.1 7.5 %collective-permute-start.2 = (bf16[2,2,128,128]{3,2,1,0:T(8,128)(2,1)S(1)}, bf16[2,2,128,128]{3,2,1,0:T(8,128)(2,1)S(1)}, u32[]{:S(2)}, u32[]{:S(2)}) collective-permute-start(bf16[2,2,128,128]{3,2,1,0:T(8,128)(2,1)S(1)} %get-tuple-element.19), channel_id=1, source_target_pairs={{0,16},{16,32},{32,48},{48,0},{1,17},{17,33},{33,49},{49,1},{2,18}... | collective-permute-start | bytes 393224 | tf_op jit(solution)/shard_map/ppermute | solution.py:198
  27.3 9.9 %collective-permute-start.3 = (bf16[2,2,128,128]{3,2,1,0:T(8,128)(2,1)S(1)}, bf16[2,2,128,128]{3,2,1,0:T(8,128)(2,1)S(1)}, u32[]{:S(2)}, u32[]{:S(2)}) collective-permute-start(bf16[2,2,128,128]{3,2,1,0:T(8,128)(2,1)S(1)} %get-tuple-element.20), channel_id=1, source_target_pairs={{0,48},{16,0},{32,16},{48,32},{1,49},{17,1},{33,17},{49,33},{2,50}... | collective-permute-start | bytes 393224 | tf_op jit(solution)/shard_map/ppermute | solution.py:198
  27.3 17.8 %collective-permute-start.6 = (bf16[2,2,128,128]{3,2,1,0:T(8,128)(2,1)S(1)}, bf16[2,2,128,128]{3,2,1,0:T(8,128)(2,1)S(1)}, u32[]{:S(2)}, u32[]{:S(2)}) collective-permute-start(bf16[2,2,128,128]{3,2,1,0:T(8,128)(2,1)S(1)} %get-tuple-element.24), channel_id=1, source_target_pairs={{0,32},{16,48},{32,0},{48,16},{1,33},{17,49},{33,1},{49,17},{2,34}... | collective-permute-start | bytes 393224 | tf_op jit(solution)/shard_map/ppermute | solution.py:198
  29.4 15.6 %collective-permute-start.7 = (bf16[2,2,128,128]{3,2,1,0:T(8,128)(2,1)S(1)}, bf16[2,2,128,128]{3,2,1,0:T(8,128)(2,1)S(1)}, u32[]{:S(2)}, u32[]{:S(2)}) collective-permute-start(bf16[2,2,128,128]{3,2,1,0:T(8,128)(2,1)S(1)} %get-tuple-element.25), channel_id=1, source_target_pairs={{0,16},{16,32},{32,48},{48,0},{1,17},{17,33},{33,49},{49,1},{2,18}... | collective-permute-start | bytes 393224 | tf_op jit(solution)/shard_map/ppermute | solution.py:198
  31.7 13.4 %collective-permute-start.8 = (bf16[2,2,128,128]{3,2,1,0:T(8,128)(2,1)S(1)}, bf16[2,2,128,128]{3,2,1,0:T(8,128)(2,1)S(1)}, u32[]{:S(2)}, u32[]{:S(2)}) collective-permute-start(bf16[2,2,128,128]{3,2,1,0:T(8,128)(2,1)S(1)} %get-tuple-element.26), channel_id=1, source_target_pairs={{0,48},{16,0},{32,16},{48,32},{1,49},{17,1},{33,17},{49,33},{2,50}... | collective-permute-start | bytes 393224 | tf_op jit(solution)/shard_map/ppermute | solution.py:198
  37.2 11.3 %collective-permute-start.4 = (bf16[2,128,128]{2,1,0:T(8,128)(2,1)S(1)}, bf16[2,128,128]{2,1,0:T(8,128)(2,1)S(1)}, u32[]{:S(2)}, u32[]{:S(2)}) collective-permute-start(bf16[2,128,128]{2,1,0:T(8,128)(2,1)S(1)} %get-tuple-element.21), channel_id=1, source_target_pairs={{0,128},{64,192},{128,0},{192,64},{1,129},{65,193},{129,1},{193,65... | collective-permute-start | bytes 196616 | tf_op jit(solution)/shard_map/ppermute | solution.py:198
  43.6 6.4 %collective-permute-start.5 = (bf16[2,128,128]{2,1,0:T(8,128)(2,1)S(1)}, bf16[2,128,128]{2,1,0:T(8,128)(2,1)S(1)}, u32[]{:S(2)}, u32[]{:S(2)}) collective-permute-start(bf16[2,128,128]{2,1,0:T(8,128)(2,1)S(1)} %get-tuple-element.22), channel_id=1, source_target_pairs={{0,64},{64,128},{128,192},{192,0},{1,65},{65,129},{129,193},{193,1... | collective-permute-start | bytes 196616 | tf_op jit(solution)/shard_map/ppermute | solution.py:198
  45.1 6.0 %collective-permute-start.9 = (bf16[2,128,128]{2,1,0:T(8,128)(2,1)S(1)}, bf16[2,128,128]{2,1,0:T(8,128)(2,1)S(1)}, u32[]{:S(2)}, u32[]{:S(2)}) collective-permute-start(bf16[2,128,128]{2,1,0:T(8,128)(2,1)S(1)} %get-tuple-element.27), channel_id=1, source_target_pairs={{0,192},{64,0},{128,64},{192,128},{1,193},{65,1},{129,65},{193,129... | collective-permute-start | bytes 196616 | tf_op jit(solution)/shard_map/ppermute | solution.py:198

commit v7 on v6

--- a/solution.py
+++ b/solution.py
@@ -215,8 +215,12 @@
     own = banded.reshape(-1, BLOCK, banded.shape[2])
     sib = shifted(own, "core", 1)
     parts = []
+    first = None
     for group, arrays in zip(Z_GROUPS, partial_sums(Z_GROUPS, block_pairs, own, sib)):
+        if first is not None:
+            arrays, first = lax.optimization_barrier((arrays, first))
         along_y = spread(arrays, "y")
+        first = along_y[1]
         staged = stage_sums(group, along_y)
         parts += [shifted(values, "zh", e) if e else values for e, values in zip(group, staged)]
     total = parts[0].astype(jnp.float32)

time: 52 us -> 51.3 us (0.987)
  the two profiles are of different devices: /device:TPU:24 before, /device:TPU:8 now
where the time goes in v7:
time: 51.3 us; the launch traced here: 50.8 us
  starting transfers between devices  19.3 us (38%)
  blocking collectives  15.5 us (30%)
  waiting for transfers between devices  8 us (16%)
  Pallas kernels  6.42 us (13%)
  between operations  0.71 us (1%)
  other arithmetic  0.69 us (1%)
    ppermute x10, starting transfers between devices, shifted(): lax.ppermute(values, axis, [(i, (i + offset) % size) for i in range(size)])  19.3 us
    all_to_all x1, blocking collectives, on_device(): lax.all_to_all(grouped, ('zl', 'x'), split_axis=0, concat_axis=0, tiled=T...  15.5 us
    ppermute x10, waiting for transfers between devices, shifted(): lax.ppermute(values, axis, [(i, (i + offset) % size) for i in range(size)])  8 us
    pallas_call x1, Pallas kernels, whitened_groups(): pl.pallas_call(spectra_kernel, out_shape=jax.ShapeDtypeStruct((groups, ch...  4.74 us
    pallas_call x1, Pallas kernels, partial_sums(): pl.pallas_call(functools.partial(products_kernel, groups), out_shape=[jax...  1.56 us
  transfers between devices with their start and end apart: 10, of which 4 were waited for; matrix products, arithmetic and copies ran while one was open for 0% of the time, Pallas kernels for 0%

profile of v7, /device:TPU:8, one launch (start us, length us, event | category | flops | bytes accessed | tf_op | source)
XLA Modules:
  0.0 50.8 jit_solution(3503903010438145275)
XLA Ops:
  0.0 0.0 copy-start
  0.0 4.7 %spectra.1 = bf16[8,256,128]{2,1,0:T(8,128)(2,1)S(1)} custom-call(bf16[2,256,4096]{2,1,0:T(8,128)(2,1)} %traces.1, bf16[1024,512]{1,0:T(8,128)(2,1)} %constant.25.clone.table), custom_call_target="tpu_custom_call" | custom-call | tf_op jit(solution)/shard_map/spectra/pallas_call | solution.py:103
  4.8 15.5 %all_to_all.5 = bf16[8,256,128]{2,1,0:T(8,128)(2,1)S(1)} all-to-all(bf16[8,256,128]{2,1,0:T(8,128)(2,1)S(1)} %spectra.1), channel_id=1, replica_groups=mesh['zh'=4,'y'=4,'core'=2,'zl'=2,'x'=4] {'zl','x'}, dimensions={0} | all-to-all | bytes 1048576 | tf_op jit(solution)/shard_map/all_to_all | solution.py:214
  20.3 0.0 collective-permute-start
  20.3 0.0 copy-done
  20.3 0.1 copy.5.pairs
  20.4 1.8 %collective-permute-done.sib = bf16[16,128,128]{2,1,0:T(8,128)(2,1)S(1)} collective-permute-done((bf16[16,128,128]{2,1,0:T(8,128)(2,1)S(1)}, bf16[16,128,128]{2,1,0:T(8,128)(2,1)S(1)}, u32[]{:S(2)}, u32[]{:S(2)}) %collective-permute-start) | collective-permute-done | bytes 524320 | tf_op jit(solution)/shard_map/ppermute | solution.py:198
  22.2 1.6 %products.1 = (f32[2,2,128,128]{3,2,1,0:T(8,128)S(1)}, bf16[2,2,128,128]{3,2,1,0:T(8,128)(2,1)S(1)}, bf16[2,2,128,128]{3,2,1,0:T(8,128)(2,1)S(1)}, bf16[2,2,128,...) custom-call(s32[32,2]{1,0:T(8,128)S(1)} %copy.5.pairs, ...), custom_call_target="tpu_custom_call" | custom-call | tf_op jit(solution)/shard_map/products/pallas_call | solution.py:156
  23.8 2.4 %collective-permute-start.1 = (bf16[2,2,128,128]{3,2,1,0:T(8,128)(2,1)S(1)}, bf16[2,2,128,128]{3,2,1,0:T(8,128)(2,1)S(1)}, u32[]{:S(2)}, u32[]{:S(2)}) collective-permute-start(bf16[2,2,128,128]{3,2,1,0:T(8,128)(2,1)S(1)} %get-tuple-element.22), channel_id=1, source_target_pairs={{0,32},{16,48},{32,0},{48,16},{1,33},{17,49},{33,1},{49,17},{2,34}... | collective-permute-start | bytes 393224 | tf_op jit(solution)/shard_map/ppermute | solution.py:198
  26.1 0.0 collective-permute-start.2
  26.1 2.0 %collective-permute-start.3 = (bf16[2,2,128,128]{3,2,1,0:T(8,128)(2,1)S(1)}, bf16[2,2,128,128]{3,2,1,0:T(8,128)(2,1)S(1)}, u32[]{:S(2)}, u32[]{:S(2)}) collective-permute-start(bf16[2,2,128,128]{3,2,1,0:T(8,128)(2,1)S(1)} %get-tuple-element.24), channel_id=1, source_target_pairs={{0,48},{16,0},{32,16},{48,32},{1,49},{17,1},{33,17},{49,33},{2,50}... | collective-permute-start | bytes 393224 | tf_op jit(solution)/shard_map/ppermute | solution.py:198
  28.2 3.5 %collective-permute-done.1.refs_1_ = bf16[2,2,128,128]{3,2,1,0:T(8,128)(2,1)S(1)} collective-permute-done((bf16[2,2,128,128]{3,2,1,0:T(8,128)(2,1)S(1)}, bf16[2,2,128,128]{3,2,1,0:T(8,128)(2,1)S(1)}, u32[]{:S(2)}, u32[]{:S(2)}) %collective-permute-start.1) | collective-permute-done | bytes 131104 | tf_op jit(solution)/shard_map/ppermute | solution.py:198
  31.7 2.3 %collective-permute-start.6 = (bf16[2,2,128,128]{3,2,1,0:T(8,128)(2,1)S(1)}, bf16[2,2,128,128]{3,2,1,0:T(8,128)(2,1)S(1)}, u32[]{:S(2)}, u32[]{:S(2)}) collective-permute-start(bf16[2,2,128,128]{3,2,1,0:T(8,128)(2,1)S(1)} %get-tuple-element.32), channel_id=1, source_target_pairs={{0,32},{16,48},{32,0},{48,16},{1,33},{17,49},{33,1},{49,17},{2,34}... | collective-permute-start | bytes 393224 | tf_op jit(solution)/shard_map/ppermute | solution.py:198
  34.0 0.0 collective-permute-start.7
  34.0 2.0 %collective-permute-start.8 = (bf16[2,2,128,128]{3,2,1,0:T(8,128)(2,1)S(1)}, bf16[2,2,128,128]{3,2,1,0:T(8,128)(2,1)S(1)}, u32[]{:S(2)}, u32[]{:S(2)}) collective-permute-start(bf16[2,2,128,128]{3,2,1,0:T(8,128)(2,1)S(1)} %get-tuple-element.34), channel_id=1, source_target_pairs={{0,48},{16,0},{32,16},{48,32},{1,49},{17,1},{33,17},{49,33},{2,50}... | collective-permute-start | bytes 393224 | tf_op jit(solution)/shard_map/ppermute | solution.py:198
  36.0 0.0 collective-permute-done.2.refs_2_
  36.0 0.0 collective-permute-done.3.refs_3_
  36.0 0.1 stage.2
  36.1 6.4 %collective-permute-start.4 = (bf16[2,128,128]{2,1,0:T(8,128)(2,1)S(1)}, bf16[2,128,128]{2,1,0:T(8,128)(2,1)S(1)}, u32[]{:S(2)}, u32[]{:S(2)}) collective-permute-start(bf16[2,128,128]{2,1,0:T(8,128)(2,1)S(1)} %get-tuple-element.25), channel_id=1, source_target_pairs={{0,128},{64,192},{128,0},{192,64},{1,129},{65,193},{129,1},{193,65... | collective-permute-start | bytes 196616 | tf_op jit(solution)/shard_map/ppermute | solution.py:198
  42.5 1.5 %collective-permute-start.5 = (bf16[2,128,128]{2,1,0:T(8,128)(2,1)S(1)}, bf16[2,128,128]{2,1,0:T(8,128)(2,1)S(1)}, u32[]{:S(2)}, u32[]{:S(2)}) collective-permute-start(bf16[2,128,128]{2,1,0:T(8,128)(2,1)S(1)} %get-tuple-element.26), channel_id=1, source_target_pairs={{0,64},{64,128},{128,192},{192,0},{1,65},{65,129},{129,193},{193,1... | collective-permute-start | bytes 196616 | tf_op jit(solution)/shard_map/ppermute | solution.py:198
  43.9 0.0 collective-permute-done.6.refs_1_
  44.0 0.0 collective-permute-done.7.refs_2_
  44.0 0.0 collective-permute-done.8.refs_3_
  44.0 0.1 stage.3
  44.0 2.7 %collective-permute-start.9 = (bf16[2,128,128]{2,1,0:T(8,128)(2,1)S(1)}, bf16[2,128,128]{2,1,0:T(8,128)(2,1)S(1)}, u32[]{:S(2)}, u32[]{:S(2)}) collective-permute-start(bf16[2,128,128]{2,1,0:T(8,128)(2,1)S(1)} %get-tuple-element.35), channel_id=1, source_target_pairs={{0,192},{64,0},{128,64},{192,128},{1,193},{65,1},{129,65},{193,129... | collective-permute-start | bytes 196616 | tf_op jit(solution)/shard_map/ppermute | solution.py:198
  47.4 0.0 collective-permute-done.4
  47.4 1.4 %collective-permute-done.5 = bf16[2,128,128]{2,1,0:T(8,128)(2,1)S(1)} collective-permute-done((bf16[2,128,128]{2,1,0:T(8,128)(2,1)S(1)}, bf16[2,128,128]{2,1,0:T(8,128)(2,1)S(1)}, u32[]{:S(2)}, u32[]{:S(2)}) %collective-permute-start.5) | collective-permute-done | bytes 65568 | tf_op jit(solution)/shard_map/ppermute | solution.py:198
  48.8 1.2 %collective-permute-done.9 = bf16[2,128,128]{2,1,0:T(8,128)(2,1)S(1)} collective-permute-done((bf16[2,128,128]{2,1,0:T(8,128)(2,1)S(1)}, bf16[2,128,128]{2,1,0:T(8,128)(2,1)S(1)}, u32[]{:S(2)}, u32[]{:S(2)}) %collective-permute-start.9) | collective-permute-done | bytes 65568 | tf_op jit(solution)/shard_map/ppermute | solution.py:198
  50.1 0.7 %multiply_bitcast_fusion = f32[1,1,2,128,128]{4,3,2,1,0:T(8,128)} fusion(f32[2,128,128]{2,1,0:T(8,128)S(1)} %get-tuple-element.36, bf16[2,128,128]{2,1,0:T(8,128)(2,1)S(1)} %collective-permute-done.9, bf16[2,128,128]{2,1,0:T(8,128)(2,1)S(1)} %collective-permute-done.5, bf16[2,128,128]{2,1,0:T(8,128)(2,1)S(1)} %collective-permute-done.4, f32[]{:T(128)S(6)} %mul_shard_map.3), kind=kLoop, calls=%fused_computation | loop fusion | flops 229376 | bytes 458756 | tf_op jit(solution)/shard_map/broadcast_in_dim | solution.py:232
Async XLA Ops:
  0.0 20.3 %copy-start = (s32[32,2]{0,1:T(2,128)S(1)}, s32[32,2]{0,1:T(2,128)}, u32[]{:S(2)}) copy-start(s32[32,2]{0,1:T(2,128)} %param.5) | copy-start | bytes 772
  20.3 1.9 %collective-permute-start = (bf16[16,128,128]{2,1,0:T(8,128)(2,1)S(1)}, bf16[16,128,128]{2,1,0:T(8,128)(2,1)S(1)}, u32[]{:S(2)}, u32[]{:S(2)}) collective-permute-start(bf16[16,128,128]{2,1,0:T(8,128)(2,1)S(1)} %bitcast.5), channel_id=1, source_target_pairs={{0,8},{8,0},{1,9},{9,1},{2,10},{10,2},{3,11},{11,3},{4,12},{12,4},... | collective-permute-start | bytes 1572872 | tf_op jit(solution)/shard_map/ppermute | solution.py:198
  23.8 7.9 %collective-permute-start.1 = (bf16[2,2,128,128]{3,2,1,0:T(8,128)(2,1)S(1)}, bf16[2,2,128,128]{3,2,1,0:T(8,128)(2,1)S(1)}, u32[]{:S(2)}, u32[]{:S(2)}) collective-permute-start(bf16[2,2,128,128]{3,2,1,0:T(8,128)(2,1)S(1)} %get-tuple-element.22), channel_id=1, source_target_pairs={{0,32},{16,48},{32,0},{48,16},{1,33},{17,49},{33,1},{49,17},{2,34}... | collective-permute-start | bytes 393224 | tf_op jit(solution)/shard_map/ppermute | solution.py:198
  26.1 9.9 %collective-permute-start.2 = (bf16[2,2,128,128]{3,2,1,0:T(8,128)(2,1)S(1)}, bf16[2,2,128,128]{3,2,1,0:T(8,128)(2,1)S(1)}, u32[]{:S(2)}, u32[]{:S(2)}) collective-permute-start(bf16[2,2,128,128]{3,2,1,0:T(8,128)(2,1)S(1)} %get-tuple-element.23), channel_id=1, source_target_pairs={{0,16},{16,32},{32,48},{48,0},{1,17},{17,33},{33,49},{49,1},{2,18}... | collective-permute-start | bytes 393224 | tf_op jit(solution)/shard_map/ppermute | solution.py:198
  26.1 9.9 %collective-permute-start.3 = (bf16[2,2,128,128]{3,2,1,0:T(8,128)(2,1)S(1)}, bf16[2,2,128,128]{3,2,1,0:T(8,128)(2,1)S(1)}, u32[]{:S(2)}, u32[]{:S(2)}) collective-permute-start(bf16[2,2,128,128]{3,2,1,0:T(8,128)(2,1)S(1)} %get-tuple-element.24), channel_id=1, source_target_pairs={{0,48},{16,0},{32,16},{48,32},{1,49},{17,1},{33,17},{49,33},{2,50}... | collective-permute-start | bytes 393224 | tf_op jit(solution)/shard_map/ppermute | solution.py:198
  31.7 12.3 %collective-permute-start.6 = (bf16[2,2,128,128]{3,2,1,0:T(8,128)(2,1)S(1)}, bf16[2,2,128,128]{3,2,1,0:T(8,128)(2,1)S(1)}, u32[]{:S(2)}, u32[]{:S(2)}) collective-permute-start(bf16[2,2,128,128]{3,2,1,0:T(8,128)(2,1)S(1)} %get-tuple-element.32), channel_id=1, source_target_pairs={{0,32},{16,48},{32,0},{48,16},{1,33},{17,49},{33,1},{49,17},{2,34}... | collective-permute-start | bytes 393224 | tf_op jit(solution)/shard_map/ppermute | solution.py:198
  34.0 10.0 %collective-permute-start.7 = (bf16[2,2,128,128]{3,2,1,0:T(8,128)(2,1)S(1)}, bf16[2,2,128,128]{3,2,1,0:T(8,128)(2,1)S(1)}, u32[]{:S(2)}, u32[]{:S(2)}) collective-permute-start(bf16[2,2,128,128]{3,2,1,0:T(8,128)(2,1)S(1)} %get-tuple-element.33), channel_id=1, source_target_pairs={{0,16},{16,32},{32,48},{48,0},{1,17},{17,33},{33,49},{49,1},{2,18}... | collective-permute-start | bytes 393224 | tf_op jit(solution)/shard_map/ppermute | solution.py:198
  34.0 10.0 %collective-permute-start.8 = (bf16[2,2,128,128]{3,2,1,0:T(8,128)(2,1)S(1)}, bf16[2,2,128,128]{3,2,1,0:T(8,128)(2,1)S(1)}, u32[]{:S(2)}, u32[]{:S(2)}) collective-permute-start(bf16[2,2,128,128]{3,2,1,0:T(8,128)(2,1)S(1)} %get-tuple-element.34), channel_id=1, source_target_pairs={{0,48},{16,0},{32,16},{48,32},{1,49},{17,1},{33,17},{49,33},{2,50}... | collective-permute-start | bytes 393224 | tf_op jit(solution)/shard_map/ppermute | solution.py:198
  36.1 11.3 %collective-permute-start.4 = (bf16[2,128,128]{2,1,0:T(8,128)(2,1)S(1)}, bf16[2,128,128]{2,1,0:T(8,128)(2,1)S(1)}, u32[]{:S(2)}, u32[]{:S(2)}) collective-permute-start(bf16[2,128,128]{2,1,0:T(8,128)(2,1)S(1)} %get-tuple-element.25), channel_id=1, source_target_pairs={{0,128},{64,192},{128,0},{192,64},{1,129},{65,193},{129,1},{193,65... | collective-permute-start | bytes 196616 | tf_op jit(solution)/shard_map/ppermute | solution.py:198
  42.5 6.4 %collective-permute-start.5 = (bf16[2,128,128]{2,1,0:T(8,128)(2,1)S(1)}, bf16[2,128,128]{2,1,0:T(8,128)(2,1)S(1)}, u32[]{:S(2)}, u32[]{:S(2)}) collective-permute-start(bf16[2,128,128]{2,1,0:T(8,128)(2,1)S(1)} %get-tuple-element.26), channel_id=1, source_target_pairs={{0,64},{64,128},{128,192},{192,0},{1,65},{65,129},{129,193},{193,1... | collective-permute-start | bytes 196616 | tf_op jit(solution)/shard_map/ppermute | solution.py:198
  44.0 6.0 %collective-permute-start.9 = (bf16[2,128,128]{2,1,0:T(8,128)(2,1)S(1)}, bf16[2,128,128]{2,1,0:T(8,128)(2,1)S(1)}, u32[]{:S(2)}, u32[]{:S(2)}) collective-permute-start(bf16[2,128,128]{2,1,0:T(8,128)(2,1)S(1)} %get-tuple-element.35), channel_id=1, source_target_pairs={{0,192},{64,0},{128,64},{192,128},{1,193},{65,1},{129,65},{193,129... | collective-permute-start | bytes 196616 | tf_op jit(solution)/shard_map/ppermute | solution.py:198

commit v8 on v7

--- a/solution.py
+++ b/solution.py
@@ -119,18 +119,12 @@
     lanes = lax.broadcasted_iota(jnp.int32, (BLOCK, 128), 1)
     is_re = lanes < 64
     dims = (((1,), (1,)), ((), ()))
-    here_z = lax.axis_index("zh")
-    here_y = lax.axis_index("y")
-    core = lax.axis_index("core")
-    cores = lax.axis_size("core")
-    size_z = lax.axis_size("zh")
-    size_y = lax.axis_size("y")
+    size_y = len(outs) // len(groups)
     for n, out in enumerate(outs):
         for i, e in enumerate(groups[n // size_y]):
-            chip = (here_z + e) % size_z * size_y + (here_y + n % size_y) % size_y
-            slot = chip * cores + core
-            r = pairs[slot, 0]
-            s = pairs[slot, 1]
+            slot = e * size_y + n % size_y
+            r = pairs[2 * slot]
+            s = pairs[2 * slot + 1]
             upper = []
             rotated = []
             lower = []
@@ -198,14 +192,22 @@
     return lax.ppermute(values, axis, [(i, (i + offset) % size) for i in range(size)])
 
 
-def far_first(size):
-    ways = [min(d, size - d) for d in range(size)]
-    return [[d for d in range(size) if ways[d] == way] for way in sorted(set(ways), reverse=True)]
+def near_first(size):
+    return sorted(range(1, size), key=lambda d: min(d, size - d))
 
 
 def spread(arrays, axis):
-    order = [d for group in far_first(len(arrays)) for d in group if d]
-    return [arrays[0]] + [shifted(arrays[d], axis, d) for d in order]
+    return [arrays[0]] + [shifted(arrays[d], axis, d) for d in near_first(len(arrays))]
+
+
+def pairs_by_distance(pairs):
+    size_z = lax.axis_size("zh")
+    size_y = lax.axis_size("y")
+    table = pairs.reshape(size_z, size_y, lax.axis_size("core"), 2)
+    table = jnp.concatenate([table, table], axis=0)
+    table = jnp.concatenate([table, table], axis=1)
+    start = (lax.axis_index("zh"), lax.axis_index("y"), lax.axis_index("core"), 0)
+    return lax.dynamic_slice(table, start, (size_z, size_y, 1, 2)).reshape(-1)
 
 
 def on_device(traces, block_pairs, valid_count):
@@ -216,7 +218,7 @@
     sib = shifted(own, "core", 1)
     parts = []
     first = None
-    for group, arrays in zip(Z_GROUPS, partial_sums(Z_GROUPS, block_pairs, own, sib)):
+    for group, arrays in zip(Z_GROUPS, partial_sums(Z_GROUPS, pairs_by_distance(block_pairs), own, sib)):
         if first is not None:
             arrays, first = lax.optimization_barrier((arrays, first))
         along_y = spread(arrays, "y")

time: 51.3 us -> 49.6 us (0.967)
  waiting for transfers between devices: 8 us -> 5.71 us
  starting transfers between devices: 19.3 us -> 20.1 us
    ppermute x10, waiting for transfers between devices: 8 us -> 5.71 us  [shifted(): lax.ppermute(values, axis, [(i, (i + offset) % size) for i in range(size)])]
    ppermute x10, starting transfers between devices: 19.3 us -> 20.1 us  [shifted(): lax.ppermute(values, axis, [(i, (i + offset) % size) for i in range(size)])]
  transfers between devices with their start and end apart: 10 -> 10, of which waited for: 4 -> 5; matrix products, arithmetic and copies ran while one was open for 0% -> 1% of each run, Pallas kernels for 0% -> 0%
where the time goes in v8:
time: 49.6 us; the launch traced here: 49.5 us
  starting transfers between devices  20.1 us (41%)
  blocking collectives  15.5 us (31%)
  Pallas kernels  6.15 us (12%)
  waiting for transfers between devices  5.71 us (12%)
  other arithmetic  0.78 us (2%)
  between operations  0.72 us (1%)
  local copies, waits for them, and re-layouts  0.51 us (1%)
    ppermute x10, starting transfers between devices, shifted(): lax.ppermute(values, axis, [(i, (i + offset) % size) for i in range(size)])  20.1 us
    all_to_all x1, blocking collectives, on_device(): lax.all_to_all(grouped, ('zl', 'x'), split_axis=0, concat_axis=0, tiled=T...  15.5 us
    ppermute x10, waiting for transfers between devices, shifted(): lax.ppermute(values, axis, [(i, (i + offset) % size) for i in range(size)])  5.71 us
    pallas_call x1, Pallas kernels, whitened_groups(): pl.pallas_call(spectra_kernel, out_shape=jax.ShapeDtypeStruct((groups, ch...  4.74 us
    pallas_call x1, Pallas kernels, partial_sums(): pl.pallas_call(functools.partial(products_kernel, groups), out_shape=[jax...  1.28 us
  transfers between devices with their start and end apart: 10, of which 5 were waited for; matrix products, arithmetic and copies ran while one was open for 1% of the time, Pallas kernels for 0%

profile of v8, /device:TPU:8, one launch (start us, length us, event | category | flops | bytes accessed | tf_op | source)
XLA Modules:
  0.0 49.5 jit_solution(14211677093668612910)
XLA Ops:
  0.0 4.7 %spectra.1 = bf16[8,256,128]{2,1,0:T(8,128)(2,1)S(1)} custom-call(bf16[2,256,4096]{2,1,0:T(8,128)(2,1)} %traces.1, bf16[1024,512]{1,0:T(8,128)(2,1)} %constant.27.clone.table), custom_call_target="tpu_custom_call" | custom-call | tf_op jit(solution)/shard_map/spectra/pallas_call | solution.py:103
  4.8 15.5 %all_to_all.5 = bf16[8,256,128]{2,1,0:T(8,128)(2,1)S(1)} all-to-all(bf16[8,256,128]{2,1,0:T(8,128)(2,1)S(1)} %spectra.1), channel_id=1, replica_groups=mesh['zh'=4,'y'=4,'core'=2,'zl'=2,'x'=4] {'zl','x'}, dimensions={0} | all-to-all | bytes 1048576 | tf_op jit(solution)/shard_map/all_to_all | solution.py:216
  20.3 0.0 collective-permute-start
  20.3 0.0 copy-done
  20.3 0.1 reshape.9
  20.4 0.2 copy.12
  20.6 0.1 fusion
  20.7 0.1 copy.14
  20.8 0.1 reshape.10.pairs
  20.9 1.3 %collective-permute-done.sib = bf16[16,128,128]{2,1,0:T(8,128)(2,1)S(1)} collective-permute-done((bf16[16,128,128]{2,1,0:T(8,128)(2,1)S(1)}, bf16[16,128,128]{2,1,0:T(8,128)(2,1)S(1)}, u32[]{:S(2)}, u32[]{:S(2)}) %collective-permute-start) | collective-permute-done | bytes 524320 | tf_op jit(solution)/shard_map/ppermute | solution.py:192
  22.2 1.3 %products.1 = (f32[2,2,128,128]{3,2,1,0:T(8,128)S(1)}, bf16[2,2,128,128]{3,2,1,0:T(8,128)(2,1)S(1)}, bf16[2,2,128,128]{3,2,1,0:T(8,128)(2,1)S(1)}, bf16[2,2,128,...) custom-call(s32[32]{0:T(128)S(1)} %reshape.10.pairs, ...), custom_call_target="tpu_custom_call" | custom-call | tf_op jit(solution)/shard_map/products/pallas_call | solution.py:150
  23.5 1.7 %collective-permute-start.1 = (bf16[2,2,128,128]{3,2,1,0:T(8,128)(2,1)S(1)}, bf16[2,2,128,128]{3,2,1,0:T(8,128)(2,1)S(1)}, u32[]{:S(2)}, u32[]{:S(2)}) collective-permute-start(bf16[2,2,128,128]{3,2,1,0:T(8,128)(2,1)S(1)} %get-tuple-element.22), channel_id=1, source_target_pairs={{0,16},{16,32},{32,48},{48,0},{1,17},{17,33},{33,49},{49,1},{2,18}... | collective-permute-start | bytes 393224 | tf_op jit(solution)/shard_map/ppermute | solution.py:192
  25.1 0.4 collective-permute-start.2
  25.6 2.3 %collective-permute-start.3 = (bf16[2,2,128,128]{3,2,1,0:T(8,128)(2,1)S(1)}, bf16[2,2,128,128]{3,2,1,0:T(8,128)(2,1)S(1)}, u32[]{:S(2)}, u32[]{:S(2)}) collective-permute-start(bf16[2,2,128,128]{3,2,1,0:T(8,128)(2,1)S(1)} %get-tuple-element.24), channel_id=1, source_target_pairs={{0,32},{16,48},{32,0},{48,16},{1,33},{17,49},{33,1},{49,17},{2,34}... | collective-permute-start | bytes 393224 | tf_op jit(solution)/shard_map/ppermute | solution.py:192
  27.9 1.2 %collective-permute-done.1.refs_1_ = bf16[2,2,128,128]{3,2,1,0:T(8,128)(2,1)S(1)} collective-permute-done((bf16[2,2,128,128]{3,2,1,0:T(8,128)(2,1)S(1)}, bf16[2,2,128,128]{3,2,1,0:T(8,128)(2,1)S(1)}, u32[]{:S(2)}, u32[]{:S(2)}) %collective-permute-start.1) | collective-permute-done | bytes 131104 | tf_op jit(solution)/shard_map/ppermute | solution.py:192
  29.1 1.6 %collective-permute-start.6 = (bf16[2,2,128,128]{3,2,1,0:T(8,128)(2,1)S(1)}, bf16[2,2,128,128]{3,2,1,0:T(8,128)(2,1)S(1)}, u32[]{:S(2)}, u32[]{:S(2)}) collective-permute-start(bf16[2,2,128,128]{3,2,1,0:T(8,128)(2,1)S(1)} %get-tuple-element.32), channel_id=1, source_target_pairs={{0,16},{16,32},{32,48},{48,0},{1,17},{17,33},{33,49},{49,1},{2,18}... | collective-permute-start | bytes 393224 | tf_op jit(solution)/shard_map/ppermute | solution.py:192
  30.7 0.4 collective-permute-start.7
  31.1 3.1 %collective-permute-start.8 = (bf16[2,2,128,128]{3,2,1,0:T(8,128)(2,1)S(1)}, bf16[2,2,128,128]{3,2,1,0:T(8,128)(2,1)S(1)}, u32[]{:S(2)}, u32[]{:S(2)}) collective-permute-start(bf16[2,2,128,128]{3,2,1,0:T(8,128)(2,1)S(1)} %get-tuple-element.34), channel_id=1, source_target_pairs={{0,32},{16,48},{32,0},{48,16},{1,33},{17,49},{33,1},{49,17},{2,34}... | collective-permute-start | bytes 393224 | tf_op jit(solution)/shard_map/ppermute | solution.py:192
  34.2 0.0 collective-permute-done.2.refs_2_
  34.2 0.5 %collective-permute-done.3.refs_3_ = bf16[2,2,128,128]{3,2,1,0:T(8,128)(2,1)S(1)} collective-permute-done((bf16[2,2,128,128]{3,2,1,0:T(8,128)(2,1)S(1)}, bf16[2,2,128,128]{3,2,1,0:T(8,128)(2,1)S(1)}, u32[]{:S(2)}, u32[]{:S(2)}) %collective-permute-start.3) | collective-permute-done | bytes 131104 | tf_op jit(solution)/shard_map/ppermute | solution.py:192
  34.8 0.1 stage.2
  34.8 6.4 %collective-permute-start.4 = (bf16[2,128,128]{2,1,0:T(8,128)(2,1)S(1)}, bf16[2,128,128]{2,1,0:T(8,128)(2,1)S(1)}, u32[]{:S(2)}, u32[]{:S(2)}) collective-permute-start(bf16[2,128,128]{2,1,0:T(8,128)(2,1)S(1)} %get-tuple-element.25), channel_id=1, source_target_pairs={{0,128},{64,192},{128,0},{192,64},{1,129},{65,193},{129,1},{193,65... | collective-permute-start | bytes 196616 | tf_op jit(solution)/shard_map/ppermute | solution.py:192
  41.2 1.5 %collective-permute-start.5 = (bf16[2,128,128]{2,1,0:T(8,128)(2,1)S(1)}, bf16[2,128,128]{2,1,0:T(8,128)(2,1)S(1)}, u32[]{:S(2)}, u32[]{:S(2)}) collective-permute-start(bf16[2,128,128]{2,1,0:T(8,128)(2,1)S(1)} %get-tuple-element.26), channel_id=1, source_target_pairs={{0,64},{64,128},{128,192},{192,0},{1,65},{65,129},{129,193},{193,1... | collective-permute-start | bytes 196616 | tf_op jit(solution)/shard_map/ppermute | solution.py:192
  42.7 0.0 collective-permute-done.6.refs_1_
  42.7 0.0 collective-permute-done.7.refs_2_
  42.7 0.0 collective-permute-done.8.refs_3_
  42.7 0.1 stage.3
  42.8 2.7 %collective-permute-start.9 = (bf16[2,128,128]{2,1,0:T(8,128)(2,1)S(1)}, bf16[2,128,128]{2,1,0:T(8,128)(2,1)S(1)}, u32[]{:S(2)}, u32[]{:S(2)}) collective-permute-start(bf16[2,128,128]{2,1,0:T(8,128)(2,1)S(1)} %get-tuple-element.35), channel_id=1, source_target_pairs={{0,192},{64,0},{128,64},{192,128},{1,193},{65,1},{129,65},{193,129... | collective-permute-start | bytes 196616 | tf_op jit(solution)/shard_map/ppermute | solution.py:192
  46.1 0.0 collective-permute-done.4
  46.2 1.4 %collective-permute-done.5 = bf16[2,128,128]{2,1,0:T(8,128)(2,1)S(1)} collective-permute-done((bf16[2,128,128]{2,1,0:T(8,128)(2,1)S(1)}, bf16[2,128,128]{2,1,0:T(8,128)(2,1)S(1)}, u32[]{:S(2)}, u32[]{:S(2)}) %collective-permute-start.5) | collective-permute-done | bytes 65568 | tf_op jit(solution)/shard_map/ppermute | solution.py:192
  47.6 1.2 %collective-permute-done.9 = bf16[2,128,128]{2,1,0:T(8,128)(2,1)S(1)} collective-permute-done((bf16[2,128,128]{2,1,0:T(8,128)(2,1)S(1)}, bf16[2,128,128]{2,1,0:T(8,128)(2,1)S(1)}, u32[]{:S(2)}, u32[]{:S(2)}) %collective-permute-start.9) | collective-permute-done | bytes 65568 | tf_op jit(solution)/shard_map/ppermute | solution.py:192
  48.8 0.7 %multiply_bitcast_fusion = f32[1,1,2,128,128]{4,3,2,1,0:T(8,128)} fusion(f32[2,128,128]{2,1,0:T(8,128)S(1)} %get-tuple-element.36, bf16[2,128,128]{2,1,0:T(8,128)(2,1)S(1)} %collective-permute-done.9, bf16[2,128,128]{2,1,0:T(8,128)(2,1)S(1)} %collective-permute-done.5, bf16[2,128,128]{2,1,0:T(8,128)(2,1)S(1)} %collective-permute-done.4, f32[]{:T(128)S(6)} %mul_shard_map.3), kind=kLoop, calls=%fused_computation | loop fusion | flops 229376 | bytes 458756 | tf_op jit(solution)/shard_map/broadcast_in_dim | solution.py:234
  (2 shorter events, 0.0 us)
Async XLA Ops:
  0.0 20.3 %copy-start = (s32[32,2]{0,1:T(2,128)S(1)}, s32[32,2]{0,1:T(2,128)}, u32[]{:S(2)}) copy-start(s32[32,2]{0,1:T(2,128)} %param.5) | copy-start | bytes 772
  20.3 1.9 %collective-permute-start = (bf16[16,128,128]{2,1,0:T(8,128)(2,1)S(1)}, bf16[16,128,128]{2,1,0:T(8,128)(2,1)S(1)}, u32[]{:S(2)}, u32[]{:S(2)}) collective-permute-start(bf16[16,128,128]{2,1,0:T(8,128)(2,1)S(1)} %bitcast.9), channel_id=1, source_target_pairs={{0,8},{8,0},{1,9},{9,1},{2,10},{10,2},{3,11},{11,3},{4,12},{12,4},... | collective-permute-start | bytes 1572872 | tf_op jit(solution)/shard_map/ppermute | solution.py:192
  23.5 5.6 %collective-permute-start.1 = (bf16[2,2,128,128]{3,2,1,0:T(8,128)(2,1)S(1)}, bf16[2,2,128,128]{3,2,1,0:T(8,128)(2,1)S(1)}, u32[]{:S(2)}, u32[]{:S(2)}) collective-permute-start(bf16[2,2,128,128]{3,2,1,0:T(8,128)(2,1)S(1)} %get-tuple-element.22), channel_id=1, source_target_pairs={{0,16},{16,32},{32,48},{48,0},{1,17},{17,33},{33,49},{49,1},{2,18}... | collective-permute-start | bytes 393224 | tf_op jit(solution)/shard_map/ppermute | solution.py:192
  25.1 9.1 %collective-permute-start.2 = (bf16[2,2,128,128]{3,2,1,0:T(8,128)(2,1)S(1)}, bf16[2,2,128,128]{3,2,1,0:T(8,128)(2,1)S(1)}, u32[]{:S(2)}, u32[]{:S(2)}) collective-permute-start(bf16[2,2,128,128]{3,2,1,0:T(8,128)(2,1)S(1)} %get-tuple-element.23), channel_id=1, source_target_pairs={{0,48},{16,0},{32,16},{48,32},{1,49},{17,1},{33,17},{49,33},{2,50}... | collective-permute-start | bytes 393224 | tf_op jit(solution)/shard_map/ppermute | solution.py:192
  25.6 9.2 %collective-permute-start.3 = (bf16[2,2,128,128]{3,2,1,0:T(8,128)(2,1)S(1)}, bf16[2,2,128,128]{3,2,1,0:T(8,128)(2,1)S(1)}, u32[]{:S(2)}, u32[]{:S(2)}) collective-permute-start(bf16[2,2,128,128]{3,2,1,0:T(8,128)(2,1)S(1)} %get-tuple-element.24), channel_id=1, source_target_pairs={{0,32},{16,48},{32,0},{48,16},{1,33},{17,49},{33,1},{49,17},{2,34}... | collective-permute-start | bytes 393224 | tf_op jit(solution)/shard_map/ppermute | solution.py:192
  29.1 13.6 %collective-permute-start.6 = (bf16[2,2,128,128]{3,2,1,0:T(8,128)(2,1)S(1)}, bf16[2,2,128,128]{3,2,1,0:T(8,128)(2,1)S(1)}, u32[]{:S(2)}, u32[]{:S(2)}) collective-permute-start(bf16[2,2,128,128]{3,2,1,0:T(8,128)(2,1)S(1)} %get-tuple-element.32), channel_id=1, source_target_pairs={{0,16},{16,32},{32,48},{48,0},{1,17},{17,33},{33,49},{49,1},{2,18}... | collective-permute-start | bytes 393224 | tf_op jit(solution)/shard_map/ppermute | solution.py:192
  30.7 12.0 %collective-permute-start.7 = (bf16[2,2,128,128]{3,2,1,0:T(8,128)(2,1)S(1)}, bf16[2,2,128,128]{3,2,1,0:T(8,128)(2,1)S(1)}, u32[]{:S(2)}, u32[]{:S(2)}) collective-permute-start(bf16[2,2,128,128]{3,2,1,0:T(8,128)(2,1)S(1)} %get-tuple-element.33), channel_id=1, source_target_pairs={{0,48},{16,0},{32,16},{48,32},{1,49},{17,1},{33,17},{49,33},{2,50}... | collective-permute-start | bytes 393224 | tf_op jit(solution)/shard_map/ppermute | solution.py:192
  31.1 11.6 %collective-permute-start.8 = (bf16[2,2,128,128]{3,2,1,0:T(8,128)(2,1)S(1)}, bf16[2,2,128,128]{3,2,1,0:T(8,128)(2,1)S(1)}, u32[]{:S(2)}, u32[]{:S(2)}) collective-permute-start(bf16[2,2,128,128]{3,2,1,0:T(8,128)(2,1)S(1)} %get-tuple-element.34), channel_id=1, source_target_pairs={{0,32},{16,48},{32,0},{48,16},{1,33},{17,49},{33,1},{49,17},{2,34}... | collective-permute-start | bytes 393224 | tf_op jit(solution)/shard_map/ppermute | solution.py:192
  34.8 11.3 %collective-permute-start.4 = (bf16[2,128,128]{2,1,0:T(8,128)(2,1)S(1)}, bf16[2,128,128]{2,1,0:T(8,128)(2,1)S(1)}, u32[]{:S(2)}, u32[]{:S(2)}) collective-permute-start(bf16[2,128,128]{2,1,0:T(8,128)(2,1)S(1)} %get-tuple-element.25), channel_id=1, source_target_pairs={{0,128},{64,192},{128,0},{192,64},{1,129},{65,193},{129,1},{193,65... | collective-permute-start | bytes 196616 | tf_op jit(solution)/shard_map/ppermute | solution.py:192
  41.2 6.4 %collective-permute-start.5 = (bf16[2,128,128]{2,1,0:T(8,128)(2,1)S(1)}, bf16[2,128,128]{2,1,0:T(8,128)(2,1)S(1)}, u32[]{:S(2)}, u32[]{:S(2)}) collective-permute-start(bf16[2,128,128]{2,1,0:T(8,128)(2,1)S(1)} %get-tuple-element.26), channel_id=1, source_target_pairs={{0,64},{64,128},{128,192},{192,0},{1,65},{65,129},{129,193},{193,1... | collective-permute-start | bytes 196616 | tf_op jit(solution)/shard_map/ppermute | solution.py:192
  42.8 6.0 %collective-permute-start.9 = (bf16[2,128,128]{2,1,0:T(8,128)(2,1)S(1)}, bf16[2,128,128]{2,1,0:T(8,128)(2,1)S(1)}, u32[]{:S(2)}, u32[]{:S(2)}) collective-permute-start(bf16[2,128,128]{2,1,0:T(8,128)(2,1)S(1)} %get-tuple-element.35), channel_id=1, source_target_pairs={{0,192},{64,0},{128,64},{192,128},{1,193},{65,1},{129,65},{193,129... | collective-permute-start | bytes 196616 | tf_op jit(solution)/shard_map/ppermute | solution.py:192

commit v9 on v8

--- a/solution.py
+++ b/solution.py
@@ -16,7 +16,7 @@
 EPS = 1e-06
 QUARTERS = 4
 ROWS = 32
-Z_GROUPS = ((2, 1), (3, 0))
+Z_GROUPS = ((1, 2), (3, 0))
 
 
 def packed_table(length):
@@ -217,12 +217,9 @@
     own = banded.reshape(-1, BLOCK, banded.shape[2])
     sib = shifted(own, "core", 1)
     parts = []
-    first = None
-    for group, arrays in zip(Z_GROUPS, partial_sums(Z_GROUPS, pairs_by_distance(block_pairs), own, sib)):
-        if first is not None:
-            arrays, first = lax.optimization_barrier((arrays, first))
+    sums = partial_sums(Z_GROUPS, pairs_by_distance(block_pairs), own, sib)
+    for group, arrays in zip(Z_GROUPS, sums):
         along_y = spread(arrays, "y")
-        first = along_y[1]
         staged = stage_sums(group, along_y)
         parts += [shifted(values, "zh", e) if e else values for e, values in zip(group, staged)]
     total = parts[0].astype(jnp.float32)

time: 49.6 us -> 49.5 us (level)
  starting transfers between devices: 20.1 us -> 19.3 us
  waiting for transfers between devices: 5.71 us -> 6.39 us
    ppermute x10, starting transfers between devices: 20.1 us -> 19.3 us  [shifted(): lax.ppermute(values, axis, [(i, (i + offset) % size) for i in range(size)])]
    ppermute x10, waiting for transfers between devices: 5.71 us -> 6.39 us  [shifted(): lax.ppermute(values, axis, [(i, (i + offset) % size) for i in range(size)])]
  transfers between devices with their start and end apart: 10 -> 10, of which waited for: 5 -> 4; matrix products, arithmetic and copies ran while one was open for 1% -> 1% of each run, Pallas kernels for 0% -> 0%
where the time goes in v9:
time: 49.5 us; the launch traced here: 49.4 us
  starting transfers between devices  19.3 us (39%)
  blocking collectives  15.5 us (31%)
  waiting for transfers between devices  6.39 us (13%)
  Pallas kernels  6.15 us (12%)
  other arithmetic  0.78 us (2%)
  between operations  0.72 us (1%)
  local copies, waits for them, and re-layouts  0.51 us (1%)
    ppermute x10, starting transfers between devices, shifted(): lax.ppermute(values, axis, [(i, (i + offset) % size) for i in range(size)])  19.3 us
    all_to_all x1, blocking collectives, on_device(): lax.all_to_all(grouped, ('zl', 'x'), split_axis=0, concat_axis=0, tiled=T...  15.5 us
    ppermute x10, waiting for transfers between devices, shifted(): lax.ppermute(values, axis, [(i, (i + offset) % size) for i in range(size)])  6.39 us
    pallas_call x1, Pallas kernels, whitened_groups(): pl.pallas_call(spectra_kernel, out_shape=jax.ShapeDtypeStruct((groups, ch...  4.74 us
    pallas_call x1, Pallas kernels, partial_sums(): pl.pallas_call(functools.partial(products_kernel, groups), out_shape=[jax...  1.28 us
  transfers between devices with their start and end apart: 10, of which 4 were waited for; matrix products, arithmetic and copies ran while one was open for 1% of the time, Pallas kernels for 0%

profile of v9, /device:TPU:8, one launch (start us, length us, event | category | flops | bytes accessed | tf_op | source)
XLA Modules:
  0.0 49.4 jit_solution(4945083294953022832)
XLA Ops:
  0.0 4.7 %spectra.1 = bf16[8,256,128]{2,1,0:T(8,128)(2,1)S(1)} custom-call(bf16[2,256,4096]{2,1,0:T(8,128)(2,1)} %traces.1, bf16[1024,512]{1,0:T(8,128)(2,1)} %constant.27.clone.table), custom_call_target="tpu_custom_call" | custom-call | tf_op jit(solution)/shard_map/spectra/pallas_call | solution.py:103
  4.8 15.5 %all_to_all.5 = bf16[8,256,128]{2,1,0:T(8,128)(2,1)S(1)} all-to-all(bf16[8,256,128]{2,1,0:T(8,128)(2,1)S(1)} %spectra.1), channel_id=1, replica_groups=mesh['zh'=4,'y'=4,'core'=2,'zl'=2,'x'=4] {'zl','x'}, dimensions={0} | all-to-all | bytes 1048576 | tf_op jit(solution)/shard_map/all_to_all | solution.py:216
  20.3 0.0 collective-permute-start
  20.3 0.0 copy-done
  20.3 0.1 reshape.9
  20.4 0.2 copy.12
  20.6 0.1 fusion
  20.7 0.1 copy.14
  20.8 0.1 reshape.10.pairs
  20.9 1.3 %collective-permute-done.sib = bf16[16,128,128]{2,1,0:T(8,128)(2,1)S(1)} collective-permute-done((bf16[16,128,128]{2,1,0:T(8,128)(2,1)S(1)}, bf16[16,128,128]{2,1,0:T(8,128)(2,1)S(1)}, u32[]{:S(2)}, u32[]{:S(2)}) %collective-permute-start) | collective-permute-done | bytes 524320 | tf_op jit(solution)/shard_map/ppermute | solution.py:192
  22.2 1.3 %products.1 = (f32[2,2,128,128]{3,2,1,0:T(8,128)S(1)}, bf16[2,2,128,128]{3,2,1,0:T(8,128)(2,1)S(1)}, bf16[2,2,128,128]{3,2,1,0:T(8,128)(2,1)S(1)}, bf16[2,2,128,...) custom-call(s32[32]{0:T(128)S(1)} %reshape.10.pairs, ...), custom_call_target="tpu_custom_call" | custom-call | tf_op jit(solution)/shard_map/products/pallas_call | solution.py:150
  23.5 1.7 %collective-permute-start.1 = (bf16[2,2,128,128]{3,2,1,0:T(8,128)(2,1)S(1)}, bf16[2,2,128,128]{3,2,1,0:T(8,128)(2,1)S(1)}, u32[]{:S(2)}, u32[]{:S(2)}) collective-permute-start(bf16[2,2,128,128]{3,2,1,0:T(8,128)(2,1)S(1)} %get-tuple-element.18), channel_id=1, source_target_pairs={{0,16},{16,32},{32,48},{48,0},{1,17},{17,33},{33,49},{49,1},{2,18}... | collective-permute-start | bytes 393224 | tf_op jit(solution)/shard_map/ppermute | solution.py:192
  25.1 0.4 collective-permute-start.2
  25.6 2.3 %collective-permute-start.3 = (bf16[2,2,128,128]{3,2,1,0:T(8,128)(2,1)S(1)}, bf16[2,2,128,128]{3,2,1,0:T(8,128)(2,1)S(1)}, u32[]{:S(2)}, u32[]{:S(2)}) collective-permute-start(bf16[2,2,128,128]{3,2,1,0:T(8,128)(2,1)S(1)} %get-tuple-element.20), channel_id=1, source_target_pairs={{0,32},{16,48},{32,0},{48,16},{1,33},{17,49},{33,1},{49,17},{2,34}... | collective-permute-start | bytes 393224 | tf_op jit(solution)/shard_map/ppermute | solution.py:192
  27.9 0.8 %collective-permute-start.6 = (bf16[2,2,128,128]{3,2,1,0:T(8,128)(2,1)S(1)}, bf16[2,2,128,128]{3,2,1,0:T(8,128)(2,1)S(1)}, u32[]{:S(2)}, u32[]{:S(2)}) collective-permute-start(bf16[2,2,128,128]{3,2,1,0:T(8,128)(2,1)S(1)} %get-tuple-element.24), channel_id=1, source_target_pairs={{0,16},{16,32},{32,48},{48,0},{1,17},{17,33},{33,49},{49,1},{2,18}... | collective-permute-start | bytes 393224 | tf_op jit(solution)/shard_map/ppermute | solution.py:192
  28.7 1.2 %collective-permute-start.7 = (bf16[2,2,128,128]{3,2,1,0:T(8,128)(2,1)S(1)}, bf16[2,2,128,128]{3,2,1,0:T(8,128)(2,1)S(1)}, u32[]{:S(2)}, u32[]{:S(2)}) collective-permute-start(bf16[2,2,128,128]{3,2,1,0:T(8,128)(2,1)S(1)} %get-tuple-element.25), channel_id=1, source_target_pairs={{0,48},{16,0},{32,16},{48,32},{1,49},{17,1},{33,17},{49,33},{2,50}... | collective-permute-start | bytes 393224 | tf_op jit(solution)/shard_map/ppermute | solution.py:192
  29.9 0.0 collective-permute-done.1.refs_1_
  29.9 2.3 %collective-permute-start.8 = (bf16[2,2,128,128]{3,2,1,0:T(8,128)(2,1)S(1)}, bf16[2,2,128,128]{3,2,1,0:T(8,128)(2,1)S(1)}, u32[]{:S(2)}, u32[]{:S(2)}) collective-permute-start(bf16[2,2,128,128]{3,2,1,0:T(8,128)(2,1)S(1)} %get-tuple-element.26), channel_id=1, source_target_pairs={{0,32},{16,48},{32,0},{48,16},{1,33},{17,49},{33,1},{49,17},{2,34}... | collective-permute-start | bytes 393224 | tf_op jit(solution)/shard_map/ppermute | solution.py:192
  32.2 0.0 collective-permute-done.2.refs_2_
  32.2 2.8 %collective-permute-done.3.refs_3_ = bf16[2,2,128,128]{3,2,1,0:T(8,128)(2,1)S(1)} collective-permute-done((bf16[2,2,128,128]{3,2,1,0:T(8,128)(2,1)S(1)}, bf16[2,2,128,128]{3,2,1,0:T(8,128)(2,1)S(1)}, u32[]{:S(2)}, u32[]{:S(2)}) %collective-permute-start.3) | collective-permute-done | bytes 131104 | tf_op jit(solution)/shard_map/ppermute | solution.py:192
  35.0 0.1 stage.2
  35.1 3.4 %collective-permute-start.4 = (bf16[2,128,128]{2,1,0:T(8,128)(2,1)S(1)}, bf16[2,128,128]{2,1,0:T(8,128)(2,1)S(1)}, u32[]{:S(2)}, u32[]{:S(2)}) collective-permute-start(bf16[2,128,128]{2,1,0:T(8,128)(2,1)S(1)} %get-tuple-element.21), channel_id=1, source_target_pairs={{0,64},{64,128},{128,192},{192,0},{1,65},{65,129},{129,193},{193,1... | collective-permute-start | bytes 196616 | tf_op jit(solution)/shard_map/ppermute | solution.py:192
  38.5 4.5 %collective-permute-start.5 = (bf16[2,128,128]{2,1,0:T(8,128)(2,1)S(1)}, bf16[2,128,128]{2,1,0:T(8,128)(2,1)S(1)}, u32[]{:S(2)}, u32[]{:S(2)}) collective-permute-start(bf16[2,128,128]{2,1,0:T(8,128)(2,1)S(1)} %get-tuple-element.22), channel_id=1, source_target_pairs={{0,128},{64,192},{128,0},{192,64},{1,129},{65,193},{129,1},{193,65... | collective-permute-start | bytes 196616 | tf_op jit(solution)/shard_map/ppermute | solution.py:192
  43.0 0.0 collective-permute-done.6.refs_1_
  43.0 0.0 collective-permute-done.7.refs_2_
  43.0 0.0 collective-permute-done.8.refs_3_
  43.0 0.1 stage.3
  43.0 2.7 %collective-permute-start.9 = (bf16[2,128,128]{2,1,0:T(8,128)(2,1)S(1)}, bf16[2,128,128]{2,1,0:T(8,128)(2,1)S(1)}, u32[]{:S(2)}, u32[]{:S(2)}) collective-permute-start(bf16[2,128,128]{2,1,0:T(8,128)(2,1)S(1)} %get-tuple-element.27), channel_id=1, source_target_pairs={{0,192},{64,0},{128,64},{192,128},{1,193},{65,1},{129,65},{193,129... | collective-permute-start | bytes 196616 | tf_op jit(solution)/shard_map/ppermute | solution.py:192
  46.4 0.0 collective-permute-done.4
  46.4 0.9 %collective-permute-done.5 = bf16[2,128,128]{2,1,0:T(8,128)(2,1)S(1)} collective-permute-done((bf16[2,128,128]{2,1,0:T(8,128)(2,1)S(1)}, bf16[2,128,128]{2,1,0:T(8,128)(2,1)S(1)}, u32[]{:S(2)}, u32[]{:S(2)}) %collective-permute-start.5) | collective-permute-done | bytes 65568 | tf_op jit(solution)/shard_map/ppermute | solution.py:192
  47.3 1.4 %collective-permute-done.9 = bf16[2,128,128]{2,1,0:T(8,128)(2,1)S(1)} collective-permute-done((bf16[2,128,128]{2,1,0:T(8,128)(2,1)S(1)}, bf16[2,128,128]{2,1,0:T(8,128)(2,1)S(1)}, u32[]{:S(2)}, u32[]{:S(2)}) %collective-permute-start.9) | collective-permute-done | bytes 65568 | tf_op jit(solution)/shard_map/ppermute | solution.py:192
  48.7 0.7 %multiply_bitcast_fusion = f32[1,1,2,128,128]{4,3,2,1,0:T(8,128)} fusion(f32[2,128,128]{2,1,0:T(8,128)S(1)} %get-tuple-element.28, bf16[2,128,128]{2,1,0:T(8,128)(2,1)S(1)} %collective-permute-done.9, bf16[2,128,128]{2,1,0:T(8,128)(2,1)S(1)} %collective-permute-done.5, bf16[2,128,128]{2,1,0:T(8,128)(2,1)S(1)} %collective-permute-done.4, f32[]{:T(128)S(6)} %mul_shard_map.3), kind=kLoop, calls=%fused_computation | loop fusion | flops 229376 | bytes 458756 | tf_op jit(solution)/shard_map/broadcast_in_dim | solution.py:231
  (2 shorter events, 0.0 us)
Async XLA Ops:
  0.0 20.3 %copy-start = (s32[32,2]{0,1:T(2,128)S(1)}, s32[32,2]{0,1:T(2,128)}, u32[]{:S(2)}) copy-start(s32[32,2]{0,1:T(2,128)} %param.5) | copy-start | bytes 772
  20.3 1.9 %collective-permute-start = (bf16[16,128,128]{2,1,0:T(8,128)(2,1)S(1)}, bf16[16,128,128]{2,1,0:T(8,128)(2,1)S(1)}, u32[]{:S(2)}, u32[]{:S(2)}) collective-permute-start(bf16[16,128,128]{2,1,0:T(8,128)(2,1)S(1)} %bitcast.9), channel_id=1, source_target_pairs={{0,8},{8,0},{1,9},{9,1},{2,10},{10,2},{3,11},{11,3},{4,12},{12,4},... | collective-permute-start | bytes 1572872 | tf_op jit(solution)/shard_map/ppermute | solution.py:192
  23.5 6.4 %collective-permute-start.1 = (bf16[2,2,128,128]{3,2,1,0:T(8,128)(2,1)S(1)}, bf16[2,2,128,128]{3,2,1,0:T(8,128)(2,1)S(1)}, u32[]{:S(2)}, u32[]{:S(2)}) collective-permute-start(bf16[2,2,128,128]{3,2,1,0:T(8,128)(2,1)S(1)} %get-tuple-element.18), channel_id=1, source_target_pairs={{0,16},{16,32},{32,48},{48,0},{1,17},{17,33},{33,49},{49,1},{2,18}... | collective-permute-start | bytes 393224 | tf_op jit(solution)/shard_map/ppermute | solution.py:192
  25.1 7.1 %collective-permute-start.2 = (bf16[2,2,128,128]{3,2,1,0:T(8,128)(2,1)S(1)}, bf16[2,2,128,128]{3,2,1,0:T(8,128)(2,1)S(1)}, u32[]{:S(2)}, u32[]{:S(2)}) collective-permute-start(bf16[2,2,128,128]{3,2,1,0:T(8,128)(2,1)S(1)} %get-tuple-element.19), channel_id=1, source_target_pairs={{0,48},{16,0},{32,16},{48,32},{1,49},{17,1},{33,17},{49,33},{2,50}... | collective-permute-start | bytes 393224 | tf_op jit(solution)/shard_map/ppermute | solution.py:192
  25.6 9.5 %collective-permute-start.3 = (bf16[2,2,128,128]{3,2,1,0:T(8,128)(2,1)S(1)}, bf16[2,2,128,128]{3,2,1,0:T(8,128)(2,1)S(1)}, u32[]{:S(2)}, u32[]{:S(2)}) collective-permute-start(bf16[2,2,128,128]{3,2,1,0:T(8,128)(2,1)S(1)} %get-tuple-element.20), channel_id=1, source_target_pairs={{0,32},{16,48},{32,0},{48,16},{1,33},{17,49},{33,1},{49,17},{2,34}... | collective-permute-start | bytes 393224 | tf_op jit(solution)/shard_map/ppermute | solution.py:192
  27.9 15.1 %collective-permute-start.6 = (bf16[2,2,128,128]{3,2,1,0:T(8,128)(2,1)S(1)}, bf16[2,2,128,128]{3,2,1,0:T(8,128)(2,1)S(1)}, u32[]{:S(2)}, u32[]{:S(2)}) collective-permute-start(bf16[2,2,128,128]{3,2,1,0:T(8,128)(2,1)S(1)} %get-tuple-element.24), channel_id=1, source_target_pairs={{0,16},{16,32},{32,48},{48,0},{1,17},{17,33},{33,49},{49,1},{2,18}... | collective-permute-start | bytes 393224 | tf_op jit(solution)/shard_map/ppermute | solution.py:192
  28.7 14.3 %collective-permute-start.7 = (bf16[2,2,128,128]{3,2,1,0:T(8,128)(2,1)S(1)}, bf16[2,2,128,128]{3,2,1,0:T(8,128)(2,1)S(1)}, u32[]{:S(2)}, u32[]{:S(2)}) collective-permute-start(bf16[2,2,128,128]{3,2,1,0:T(8,128)(2,1)S(1)} %get-tuple-element.25), channel_id=1, source_target_pairs={{0,48},{16,0},{32,16},{48,32},{1,49},{17,1},{33,17},{49,33},{2,50}... | collective-permute-start | bytes 393224 | tf_op jit(solution)/shard_map/ppermute | solution.py:192
  29.9 13.1 %collective-permute-start.8 = (bf16[2,2,128,128]{3,2,1,0:T(8,128)(2,1)S(1)}, bf16[2,2,128,128]{3,2,1,0:T(8,128)(2,1)S(1)}, u32[]{:S(2)}, u32[]{:S(2)}) collective-permute-start(bf16[2,2,128,128]{3,2,1,0:T(8,128)(2,1)S(1)} %get-tuple-element.26), channel_id=1, source_target_pairs={{0,32},{16,48},{32,0},{48,16},{1,33},{17,49},{33,1},{49,17},{2,34}... | collective-permute-start | bytes 393224 | tf_op jit(solution)/shard_map/ppermute | solution.py:192
  35.1 11.3 %collective-permute-start.4 = (bf16[2,128,128]{2,1,0:T(8,128)(2,1)S(1)}, bf16[2,128,128]{2,1,0:T(8,128)(2,1)S(1)}, u32[]{:S(2)}, u32[]{:S(2)}) collective-permute-start(bf16[2,128,128]{2,1,0:T(8,128)(2,1)S(1)} %get-tuple-element.21), channel_id=1, source_target_pairs={{0,64},{64,128},{128,192},{192,0},{1,65},{65,129},{129,193},{193,1... | collective-permute-start | bytes 196616 | tf_op jit(solution)/shard_map/ppermute | solution.py:192
  38.5 8.8 %collective-permute-start.5 = (bf16[2,128,128]{2,1,0:T(8,128)(2,1)S(1)}, bf16[2,128,128]{2,1,0:T(8,128)(2,1)S(1)}, u32[]{:S(2)}, u32[]{:S(2)}) collective-permute-start(bf16[2,128,128]{2,1,0:T(8,128)(2,1)S(1)} %get-tuple-element.22), channel_id=1, source_target_pairs={{0,128},{64,192},{128,0},{192,64},{1,129},{65,193},{129,1},{193,65... | collective-permute-start | bytes 196616 | tf_op jit(solution)/shard_map/ppermute | solution.py:192
  43.0 5.6 %collective-permute-start.9 = (bf16[2,128,128]{2,1,0:T(8,128)(2,1)S(1)}, bf16[2,128,128]{2,1,0:T(8,128)(2,1)S(1)}, u32[]{:S(2)}, u32[]{:S(2)}) collective-permute-start(bf16[2,128,128]{2,1,0:T(8,128)(2,1)S(1)} %get-tuple-element.27), channel_id=1, source_target_pairs={{0,192},{64,0},{128,64},{192,128},{1,193},{65,1},{129,65},{193,129... | collective-permute-start | bytes 196616 | tf_op jit(solution)/shard_map/ppermute | solution.py:192

commit v10 on v8

--- a/solution.py
+++ b/solution.py
@@ -16,6 +16,7 @@
 EPS = 1e-06
 QUARTERS = 4
 ROWS = 32
+CHUNKS = (0, 64, 160, 256)
 Z_GROUPS = ((2, 1), (3, 0))
 
 
@@ -30,15 +31,15 @@
 
 
 def spectra_kernel(traces, table, out, table_buf, buf, sems):
-    steps, windows, span, length = buf.shape
+    windows, _, length = buf.shape
     quarter = length // QUARTERS
+    steps = len(CHUNKS) - 1
     load_table = pltpu.make_async_copy(table, table_buf, sems.at[steps])
     load_table.start()
     loads = []
     for step in range(steps):
-        load = pltpu.make_async_copy(
-            traces.at[:, pl.ds(step * span, span), :], buf.at[step], sems.at[step]
-        )
+        chunk = pl.ds(CHUNKS[step], CHUNKS[step + 1] - CHUNKS[step])
+        load = pltpu.make_async_copy(traces.at[:, chunk], buf.at[:, chunk], sems.at[step])
         load.start()
         loads.append(load)
     lanes = lax.broadcasted_iota(jnp.int32, (1, 128), 1)
@@ -51,6 +52,7 @@
     tiles = 2 * NBINS // 128
 
     def finish(step, dots):
+        span = CHUNKS[step + 1] - CHUNKS[step]
         for start in range(0, span, ROWS):
             spans = []
             for w in range(windows):
@@ -69,7 +71,7 @@
                 energy = jnp.sum(squares, axis=1, keepdims=True)
                 scale = lax.rsqrt(energy / NBINS + EPS)
                 spans.append([part * scale for part in parts])
-            rows = pl.ds(step * span + start, ROWS)
+            rows = pl.ds(CHUNKS[step] + start, ROWS)
             for t in range(tiles):
                 first, second = spans[0][t], spans[1][t]
                 even = jnp.where(lane32 == 0, first, pltpu.roll(second, 32, 1))
@@ -81,7 +83,7 @@
     before = None
     for step in range(steps):
         loads[step].wait()
-        whole = buf[step].reshape(windows * span, length)
+        whole = buf[:, CHUNKS[step] : CHUNKS[step + 1]].reshape(-1, length)
         stacked = jnp.concatenate(
             [whole[:, q * quarter : (q + 1) * quarter] for q in range(QUARTERS)], axis=0
         )
@@ -96,7 +98,7 @@
     return pltpu.with_memory_space_constraint(values, pltpu.HBM)
 
 
-def whitened_groups(traces, steps=4):
+def whitened_groups(traces):
     windows, channels, length = traces.shape
     table = jnp.asarray(packed_table(length))
     groups = NBINS // GROUP
@@ -107,8 +109,8 @@
         out_specs=pl.BlockSpec(memory_space=pltpu.VMEM),
         scratch_shapes=[
             pltpu.VMEM(table.shape, table.dtype),
-            pltpu.VMEM((steps, windows, channels // steps, length), traces.dtype),
-            pltpu.SemaphoreType.DMA((steps + 1,)),
+            pltpu.VMEM(traces.shape, traces.dtype),
+            pltpu.SemaphoreType.DMA((len(CHUNKS),)),
         ],
         compiler_params=pltpu.CompilerParams(vmem_limit_bytes=16 << 20),
         name="spectra",

time: 49.6 us -> 49.4 us (level)
  no operation moved by 1% of the time
where the time goes in v10:
time: 49.4 us; the launch traced here: 49.3 us
  starting transfers between devices  20.1 us (41%)
  blocking collectives  15.5 us (31%)
  Pallas kernels  5.98 us (12%)
  waiting for transfers between devices  5.69 us (12%)
  other arithmetic  0.78 us (2%)
  between operations  0.72 us (1%)
  local copies, waits for them, and re-layouts  0.51 us (1%)
    ppermute x10, starting transfers between devices, shifted(): lax.ppermute(values, axis, [(i, (i + offset) % size) for i in range(size)])  20.1 us
    all_to_all x1, blocking collectives, on_device(): lax.all_to_all(grouped, ('zl', 'x'), split_axis=0, concat_axis=0, tiled=T...  15.5 us
    ppermute x10, waiting for transfers between devices, shifted(): lax.ppermute(values, axis, [(i, (i + offset) % size) for i in range(size)])  5.69 us
    pallas_call x1, Pallas kernels, whitened_groups(): pl.pallas_call(spectra_kernel, out_shape=jax.ShapeDtypeStruct((groups, ch...  4.57 us
    pallas_call x1, Pallas kernels, partial_sums(): pl.pallas_call(functools.partial(products_kernel, groups), out_shape=[jax...  1.27 us
  transfers between devices with their start and end apart: 10, of which 5 were waited for; matrix products, arithmetic and copies ran while one was open for 1% of the time, Pallas kernels for 0%

profile of v10, /device:TPU:8, one launch (start us, length us, event | category | flops | bytes accessed | tf_op | source)
XLA Modules:
  0.0 49.3 jit_solution(8476878170027653645)
XLA Ops:
  0.0 4.6 %spectra.1 = bf16[8,256,128]{2,1,0:T(8,128)(2,1)S(1)} custom-call(bf16[2,256,4096]{2,1,0:T(8,128)(2,1)} %traces.1, bf16[1024,512]{1,0:T(8,128)(2,1)} %constant.27.clone.table), custom_call_target="tpu_custom_call" | custom-call | tf_op jit(solution)/shard_map/spectra/pallas_call | solution.py:105
  4.6 15.5 %all_to_all.5 = bf16[8,256,128]{2,1,0:T(8,128)(2,1)S(1)} all-to-all(bf16[8,256,128]{2,1,0:T(8,128)(2,1)S(1)} %spectra.1), channel_id=1, replica_groups=mesh['zh'=4,'y'=4,'core'=2,'zl'=2,'x'=4] {'zl','x'}, dimensions={0} | all-to-all | bytes 1048576 | tf_op jit(solution)/shard_map/all_to_all | solution.py:218
  20.1 0.0 collective-permute-start
  20.1 0.0 copy-done
  20.1 0.1 reshape.9
  20.2 0.2 copy.12
  20.4 0.1 fusion
  20.5 0.1 copy.14
  20.6 0.1 reshape.10.pairs
  20.7 1.3 %collective-permute-done.sib = bf16[16,128,128]{2,1,0:T(8,128)(2,1)S(1)} collective-permute-done((bf16[16,128,128]{2,1,0:T(8,128)(2,1)S(1)}, bf16[16,128,128]{2,1,0:T(8,128)(2,1)S(1)}, u32[]{:S(2)}, u32[]{:S(2)}) %collective-permute-start) | collective-permute-done | bytes 524320 | tf_op jit(solution)/shard_map/ppermute | solution.py:194
  22.0 1.3 %products.1 = (f32[2,2,128,128]{3,2,1,0:T(8,128)S(1)}, bf16[2,2,128,128]{3,2,1,0:T(8,128)(2,1)S(1)}, bf16[2,2,128,128]{3,2,1,0:T(8,128)(2,1)S(1)}, bf16[2,2,128,...) custom-call(s32[32]{0:T(128)S(1)} %reshape.10.pairs, ...), custom_call_target="tpu_custom_call" | custom-call | tf_op jit(solution)/shard_map/products/pallas_call | solution.py:152
  23.3 1.7 %collective-permute-start.1 = (bf16[2,2,128,128]{3,2,1,0:T(8,128)(2,1)S(1)}, bf16[2,2,128,128]{3,2,1,0:T(8,128)(2,1)S(1)}, u32[]{:S(2)}, u32[]{:S(2)}) collective-permute-start(bf16[2,2,128,128]{3,2,1,0:T(8,128)(2,1)S(1)} %get-tuple-element.22), channel_id=1, source_target_pairs={{0,16},{16,32},{32,48},{48,0},{1,17},{17,33},{33,49},{49,1},{2,18}... | collective-permute-start | bytes 393224 | tf_op jit(solution)/shard_map/ppermute | solution.py:194
  24.9 0.4 collective-permute-start.2
  25.4 2.3 %collective-permute-start.3 = (bf16[2,2,128,128]{3,2,1,0:T(8,128)(2,1)S(1)}, bf16[2,2,128,128]{3,2,1,0:T(8,128)(2,1)S(1)}, u32[]{:S(2)}, u32[]{:S(2)}) collective-permute-start(bf16[2,2,128,128]{3,2,1,0:T(8,128)(2,1)S(1)} %get-tuple-element.24), channel_id=1, source_target_pairs={{0,32},{16,48},{32,0},{48,16},{1,33},{17,49},{33,1},{49,17},{2,34}... | collective-permute-start | bytes 393224 | tf_op jit(solution)/shard_map/ppermute | solution.py:194
  27.7 1.2 %collective-permute-done.1.refs_1_ = bf16[2,2,128,128]{3,2,1,0:T(8,128)(2,1)S(1)} collective-permute-done((bf16[2,2,128,128]{3,2,1,0:T(8,128)(2,1)S(1)}, bf16[2,2,128,128]{3,2,1,0:T(8,128)(2,1)S(1)}, u32[]{:S(2)}, u32[]{:S(2)}) %collective-permute-start.1) | collective-permute-done | bytes 131104 | tf_op jit(solution)/shard_map/ppermute | solution.py:194
  28.9 1.6 %collective-permute-start.6 = (bf16[2,2,128,128]{3,2,1,0:T(8,128)(2,1)S(1)}, bf16[2,2,128,128]{3,2,1,0:T(8,128)(2,1)S(1)}, u32[]{:S(2)}, u32[]{:S(2)}) collective-permute-start(bf16[2,2,128,128]{3,2,1,0:T(8,128)(2,1)S(1)} %get-tuple-element.32), channel_id=1, source_target_pairs={{0,16},{16,32},{32,48},{48,0},{1,17},{17,33},{33,49},{49,1},{2,18}... | collective-permute-start | bytes 393224 | tf_op jit(solution)/shard_map/ppermute | solution.py:194
  30.5 0.4 collective-permute-start.7
  30.9 3.1 %collective-permute-start.8 = (bf16[2,2,128,128]{3,2,1,0:T(8,128)(2,1)S(1)}, bf16[2,2,128,128]{3,2,1,0:T(8,128)(2,1)S(1)}, u32[]{:S(2)}, u32[]{:S(2)}) collective-permute-start(bf16[2,2,128,128]{3,2,1,0:T(8,128)(2,1)S(1)} %get-tuple-element.34), channel_id=1, source_target_pairs={{0,32},{16,48},{32,0},{48,16},{1,33},{17,49},{33,1},{49,17},{2,34}... | collective-permute-start | bytes 393224 | tf_op jit(solution)/shard_map/ppermute | solution.py:194
  34.0 0.0 collective-permute-done.2.refs_2_
  34.0 0.5 %collective-permute-done.3.refs_3_ = bf16[2,2,128,128]{3,2,1,0:T(8,128)(2,1)S(1)} collective-permute-done((bf16[2,2,128,128]{3,2,1,0:T(8,128)(2,1)S(1)}, bf16[2,2,128,128]{3,2,1,0:T(8,128)(2,1)S(1)}, u32[]{:S(2)}, u32[]{:S(2)}) %collective-permute-start.3) | collective-permute-done | bytes 131104 | tf_op jit(solution)/shard_map/ppermute | solution.py:194
  34.6 0.1 stage.2
  34.6 6.4 %collective-permute-start.4 = (bf16[2,128,128]{2,1,0:T(8,128)(2,1)S(1)}, bf16[2,128,128]{2,1,0:T(8,128)(2,1)S(1)}, u32[]{:S(2)}, u32[]{:S(2)}) collective-permute-start(bf16[2,128,128]{2,1,0:T(8,128)(2,1)S(1)} %get-tuple-element.25), channel_id=1, source_target_pairs={{0,128},{64,192},{128,0},{192,64},{1,129},{65,193},{129,1},{193,65... | collective-permute-start | bytes 196616 | tf_op jit(solution)/shard_map/ppermute | solution.py:194
  41.0 1.5 %collective-permute-start.5 = (bf16[2,128,128]{2,1,0:T(8,128)(2,1)S(1)}, bf16[2,128,128]{2,1,0:T(8,128)(2,1)S(1)}, u32[]{:S(2)}, u32[]{:S(2)}) collective-permute-start(bf16[2,128,128]{2,1,0:T(8,128)(2,1)S(1)} %get-tuple-element.26), channel_id=1, source_target_pairs={{0,64},{64,128},{128,192},{192,0},{1,65},{65,129},{129,193},{193,1... | collective-permute-start | bytes 196616 | tf_op jit(solution)/shard_map/ppermute | solution.py:194
  42.5 0.0 collective-permute-done.6.refs_1_
  42.5 0.0 collective-permute-done.7.refs_2_
  42.5 0.0 collective-permute-done.8.refs_3_
  42.5 0.1 stage.3
  42.6 2.7 %collective-permute-start.9 = (bf16[2,128,128]{2,1,0:T(8,128)(2,1)S(1)}, bf16[2,128,128]{2,1,0:T(8,128)(2,1)S(1)}, u32[]{:S(2)}, u32[]{:S(2)}) collective-permute-start(bf16[2,128,128]{2,1,0:T(8,128)(2,1)S(1)} %get-tuple-element.35), channel_id=1, source_target_pairs={{0,192},{64,0},{128,64},{192,128},{1,193},{65,1},{129,65},{193,129... | collective-permute-start | bytes 196616 | tf_op jit(solution)/shard_map/ppermute | solution.py:194
  46.0 0.0 collective-permute-done.4
  46.0 1.4 %collective-permute-done.5 = bf16[2,128,128]{2,1,0:T(8,128)(2,1)S(1)} collective-permute-done((bf16[2,128,128]{2,1,0:T(8,128)(2,1)S(1)}, bf16[2,128,128]{2,1,0:T(8,128)(2,1)S(1)}, u32[]{:S(2)}, u32[]{:S(2)}) %collective-permute-start.5) | collective-permute-done | bytes 65568 | tf_op jit(solution)/shard_map/ppermute | solution.py:194
  47.4 1.2 %collective-permute-done.9 = bf16[2,128,128]{2,1,0:T(8,128)(2,1)S(1)} collective-permute-done((bf16[2,128,128]{2,1,0:T(8,128)(2,1)S(1)}, bf16[2,128,128]{2,1,0:T(8,128)(2,1)S(1)}, u32[]{:S(2)}, u32[]{:S(2)}) %collective-permute-start.9) | collective-permute-done | bytes 65568 | tf_op jit(solution)/shard_map/ppermute | solution.py:194
  48.6 0.7 %multiply_bitcast_fusion = f32[1,1,2,128,128]{4,3,2,1,0:T(8,128)} fusion(f32[2,128,128]{2,1,0:T(8,128)S(1)} %get-tuple-element.36, bf16[2,128,128]{2,1,0:T(8,128)(2,1)S(1)} %collective-permute-done.9, bf16[2,128,128]{2,1,0:T(8,128)(2,1)S(1)} %collective-permute-done.5, bf16[2,128,128]{2,1,0:T(8,128)(2,1)S(1)} %collective-permute-done.4, f32[]{:T(128)S(6)} %mul_shard_map.3), kind=kLoop, calls=%fused_computation | loop fusion | flops 229376 | bytes 458756 | tf_op jit(solution)/shard_map/broadcast_in_dim | solution.py:236
  (2 shorter events, 0.0 us)
Async XLA Ops:
  0.0 20.1 %copy-start = (s32[32,2]{0,1:T(2,128)S(1)}, s32[32,2]{0,1:T(2,128)}, u32[]{:S(2)}) copy-start(s32[32,2]{0,1:T(2,128)} %param.5) | copy-start | bytes 772
  20.1 1.9 %collective-permute-start = (bf16[16,128,128]{2,1,0:T(8,128)(2,1)S(1)}, bf16[16,128,128]{2,1,0:T(8,128)(2,1)S(1)}, u32[]{:S(2)}, u32[]{:S(2)}) collective-permute-start(bf16[16,128,128]{2,1,0:T(8,128)(2,1)S(1)} %bitcast.9), channel_id=1, source_target_pairs={{0,8},{8,0},{1,9},{9,1},{2,10},{10,2},{3,11},{11,3},{4,12},{12,4},... | collective-permute-start | bytes 1572872 | tf_op jit(solution)/shard_map/ppermute | solution.py:194
  23.3 5.6 %collective-permute-start.1 = (bf16[2,2,128,128]{3,2,1,0:T(8,128)(2,1)S(1)}, bf16[2,2,128,128]{3,2,1,0:T(8,128)(2,1)S(1)}, u32[]{:S(2)}, u32[]{:S(2)}) collective-permute-start(bf16[2,2,128,128]{3,2,1,0:T(8,128)(2,1)S(1)} %get-tuple-element.22), channel_id=1, source_target_pairs={{0,16},{16,32},{32,48},{48,0},{1,17},{17,33},{33,49},{49,1},{2,18}... | collective-permute-start | bytes 393224 | tf_op jit(solution)/shard_map/ppermute | solution.py:194
  24.9 9.1 %collective-permute-start.2 = (bf16[2,2,128,128]{3,2,1,0:T(8,128)(2,1)S(1)}, bf16[2,2,128,128]{3,2,1,0:T(8,128)(2,1)S(1)}, u32[]{:S(2)}, u32[]{:S(2)}) collective-permute-start(bf16[2,2,128,128]{3,2,1,0:T(8,128)(2,1)S(1)} %get-tuple-element.23), channel_id=1, source_target_pairs={{0,48},{16,0},{32,16},{48,32},{1,49},{17,1},{33,17},{49,33},{2,50}... | collective-permute-start | bytes 393224 | tf_op jit(solution)/shard_map/ppermute | solution.py:194
  25.4 9.2 %collective-permute-start.3 = (bf16[2,2,128,128]{3,2,1,0:T(8,128)(2,1)S(1)}, bf16[2,2,128,128]{3,2,1,0:T(8,128)(2,1)S(1)}, u32[]{:S(2)}, u32[]{:S(2)}) collective-permute-start(bf16[2,2,128,128]{3,2,1,0:T(8,128)(2,1)S(1)} %get-tuple-element.24), channel_id=1, source_target_pairs={{0,32},{16,48},{32,0},{48,16},{1,33},{17,49},{33,1},{49,17},{2,34}... | collective-permute-start | bytes 393224 | tf_op jit(solution)/shard_map/ppermute | solution.py:194
  28.9 13.6 %collective-permute-start.6 = (bf16[2,2,128,128]{3,2,1,0:T(8,128)(2,1)S(1)}, bf16[2,2,128,128]{3,2,1,0:T(8,128)(2,1)S(1)}, u32[]{:S(2)}, u32[]{:S(2)}) collective-permute-start(bf16[2,2,128,128]{3,2,1,0:T(8,128)(2,1)S(1)} %get-tuple-element.32), channel_id=1, source_target_pairs={{0,16},{16,32},{32,48},{48,0},{1,17},{17,33},{33,49},{49,1},{2,18}... | collective-permute-start | bytes 393224 | tf_op jit(solution)/shard_map/ppermute | solution.py:194
  30.5 12.0 %collective-permute-start.7 = (bf16[2,2,128,128]{3,2,1,0:T(8,128)(2,1)S(1)}, bf16[2,2,128,128]{3,2,1,0:T(8,128)(2,1)S(1)}, u32[]{:S(2)}, u32[]{:S(2)}) collective-permute-start(bf16[2,2,128,128]{3,2,1,0:T(8,128)(2,1)S(1)} %get-tuple-element.33), channel_id=1, source_target_pairs={{0,48},{16,0},{32,16},{48,32},{1,49},{17,1},{33,17},{49,33},{2,50}... | collective-permute-start | bytes 393224 | tf_op jit(solution)/shard_map/ppermute | solution.py:194
  30.9 11.6 %collective-permute-start.8 = (bf16[2,2,128,128]{3,2,1,0:T(8,128)(2,1)S(1)}, bf16[2,2,128,128]{3,2,1,0:T(8,128)(2,1)S(1)}, u32[]{:S(2)}, u32[]{:S(2)}) collective-permute-start(bf16[2,2,128,128]{3,2,1,0:T(8,128)(2,1)S(1)} %get-tuple-element.34), channel_id=1, source_target_pairs={{0,32},{16,48},{32,0},{48,16},{1,33},{17,49},{33,1},{49,17},{2,34}... | collective-permute-start | bytes 393224 | tf_op jit(solution)/shard_map/ppermute | solution.py:194
  34.6 11.3 %collective-permute-start.4 = (bf16[2,128,128]{2,1,0:T(8,128)(2,1)S(1)}, bf16[2,128,128]{2,1,0:T(8,128)(2,1)S(1)}, u32[]{:S(2)}, u32[]{:S(2)}) collective-permute-start(bf16[2,128,128]{2,1,0:T(8,128)(2,1)S(1)} %get-tuple-element.25), channel_id=1, source_target_pairs={{0,128},{64,192},{128,0},{192,64},{1,129},{65,193},{129,1},{193,65... | collective-permute-start | bytes 196616 | tf_op jit(solution)/shard_map/ppermute | solution.py:194
  41.0 6.4 %collective-permute-start.5 = (bf16[2,128,128]{2,1,0:T(8,128)(2,1)S(1)}, bf16[2,128,128]{2,1,0:T(8,128)(2,1)S(1)}, u32[]{:S(2)}, u32[]{:S(2)}) collective-permute-start(bf16[2,128,128]{2,1,0:T(8,128)(2,1)S(1)} %get-tuple-element.26), channel_id=1, source_target_pairs={{0,64},{64,128},{128,192},{192,0},{1,65},{65,129},{129,193},{193,1... | collective-permute-start | bytes 196616 | tf_op jit(solution)/shard_map/ppermute | solution.py:194
  42.6 6.0 %collective-permute-start.9 = (bf16[2,128,128]{2,1,0:T(8,128)(2,1)S(1)}, bf16[2,128,128]{2,1,0:T(8,128)(2,1)S(1)}, u32[]{:S(2)}, u32[]{:S(2)}) collective-permute-start(bf16[2,128,128]{2,1,0:T(8,128)(2,1)S(1)} %get-tuple-element.35), channel_id=1, source_target_pairs={{0,192},{64,0},{128,64},{192,128},{1,193},{65,1},{129,65},{193,129... | collective-permute-start | bytes 196616 | tf_op jit(solution)/shard_map/ppermute | solution.py:194
